TPU v7x, 32 devices: a whole 2x2x4 slice. The times are simulated.
32 devices in a mesh: section: 2 (over y), tensor: 4 (over z), dp: 4 (over x, core).
Axes of the slice: x: 2, y: 2, z: 4, core: 2. Of those that a mesh axis runs over, the one named last changes fastest.
Arguments:
- tokens_in: bfloat16 [4, 256, 4, 2048], P(None, 'tensor', 'dp'), may hold values from -6 to 6
- cotangent: bfloat16 [4, 256, 4, 2048], P(None, 'tensor', 'dp'), may hold values from -6 to 6
- ln1_gain: bfloat16 [2, 2048], P('section'), may hold values from 0.5 to 1.5
- ln1_bias: bfloat16 [2, 2048], P('section'), may hold values from -1 to 1
- q_weight: bfloat16 [2, 2048, 2048], P('section', None, 'tensor'), may hold values from -0.125 to 0.125
- q_bias: bfloat16 [2, 2048], P('section', 'tensor'), may hold values from -1.5 to 1.5
- kv_weight: bfloat16 [2, 2048, 256], P('section'), may hold values from -0.125 to 0.125
- v_bias: bfloat16 [2, 128], P('section'), may hold values from -0.25 to 0.25
- o_weight: bfloat16 [2, 2048, 2048], P('section', 'tensor'), may hold values from -1.5 to 1.5
- o_bias: bfloat16 [2, 2048], P('section'), may hold values from -1.5 to 1.5
- ln2_gain: bfloat16 [2, 2048], P('section'), may hold values from 0.5 to 1.5
- ln2_bias: bfloat16 [2, 2048], P('section'), may hold values from -1 to 1
- up_weight: bfloat16 [2, 2048, 8192], P('section', None, 'tensor'), may hold values from -0.125 to 0.125
- up_bias: bfloat16 [2, 8192], P('section', 'tensor'), may hold values from -1.5 to 1.5
- down_weight: bfloat16 [2, 8192, 2048], P('section', 'tensor'), may hold values from -0.0625 to 0.0625
- down_bias: bfloat16 [2, 2048], P('section'), may hold values from -1.5 to 1.5
Outputs:
- layer_out: bfloat16 [2, 4, 256, 4, 2048], P('section', None, 'tensor', 'dp')
- input_grad: float32 [2, 4, 256, 4, 2048], P('section', None, 'tensor', 'dp')
- ln1_gain_grad: float32 [2, 2048], P('section')
- ln1_bias_grad: float32 [2, 2048], P('section')
- q_weight_grad: float32 [2, 2048, 2048], P('section', None, 'tensor')
- q_bias_grad: float32 [2, 2048], P('section', 'tensor')
- kv_weight_grad: float32 [2, 2048, 256], P('section')
- v_bias_grad: float32 [2, 128], P('section')
- o_weight_grad: float32 [2, 2048, 2048], P('section', 'tensor')
- o_bias_grad: float32 [2, 2048], P('section')
- ln2_gain_grad: float32 [2, 2048], P('section')
- ln2_bias_grad: float32 [2, 2048], P('section')
- up_weight_grad: float32 [2, 2048, 8192], P('section', None, 'tensor')
- up_bias_grad: float32 [2, 8192], P('section', 'tensor')
- down_weight_grad: float32 [2, 8192, 2048], P('section', 'tensor')
- down_bias_grad: float32 [2, 2048], P('section')
All inputs are finite; a program needn't handle non-finite values.
Results may differ from a plain program's by a relative error of at most 0.022.
Values may be sent and summed in bfloat16 or wider, within the bound.
A program may use at most 512 MiB of HBM per device.

v0:
```python
import math

import jax
import jax.numpy as jnp
from jax import lax
from jax.sharding import PartitionSpec as P

HD = 128


def from_behind(block, axis, distance):
    devices = range(lax.axis_size(axis))
    route = [(i - distance, i) for i in devices if i - distance in devices]
    return lax.ppermute(block, axis, route)


def for_sending(shard):
    return jax.tree.map(lambda a: a.astype(jnp.bfloat16) if a.dtype == jnp.float32 else a, shard)


def layer_norm(values, gain_vec, bias_vec):
    row_mean = jnp.mean(values, axis=-1, keepdims=True)
    centred = values - row_mean
    row_var = jnp.mean(centred * centred, axis=-1, keepdims=True)
    return centred * lax.rsqrt(row_var + 1e-05) * gain_vec + bias_vec


def gelu_tanh(values):
    return jax.nn.gelu(values, approximate=True)


def gather_rows(own_rows):
    return lax.all_gather(own_rows, "tensor", axis=0, tiled=True)


def sum_rows(term_fn, own_count):
    return lax.psum_scatter(
        term_fn(jnp.int32(0), own_count * lax.axis_size("tensor")).astype(jnp.bfloat16),
        "tensor",
        scatter_dimension=0,
        tiled=True,
    ).astype(jnp.float32)


def on_device(
    tokens_in,
    cotangent,
    ln1_gain,
    ln1_bias,
    q_weight,
    q_bias,
    kv_weight,
    v_bias,
    o_weight,
    o_bias,
    ln2_gain,
    ln2_bias,
    up_weight,
    up_bias,
    down_weight,
    down_bias,
):
    f32 = jnp.float32
    bf16 = jnp.bfloat16
    section = lax.axis_index("section")
    tensor_count = lax.axis_size("tensor")
    tensor_rank = lax.axis_index("tensor")
    gain_one = ln1_gain[0].astype(f32)
    bias_one = ln1_bias[0].astype(f32)
    w_query = q_weight[0]
    b_query = q_bias[0].astype(f32)
    w_pairs = kv_weight[0]
    pair_bias = jnp.concatenate([jnp.zeros((HD,), f32), v_bias[0].astype(f32)])
    w_out = o_weight[0]
    b_out = o_bias[0].astype(f32)
    gain_two = ln2_gain[0].astype(f32)
    bias_two = ln2_bias[0].astype(f32)
    w_up = up_weight[0]
    b_up = up_bias[0].astype(f32)
    w_down = down_weight[0]
    b_down = down_bias[0].astype(f32)
    blocks, own_count, seq_count, model_dim = tokens_in.shape
    block_len = own_count * tensor_count
    total_len = blocks * block_len
    heads_local = w_query.shape[1] // HD
    ff_local = w_up.shape[1]
    score_scale = 1.0 / math.sqrt(HD)
    positions = jnp.arange(total_len, dtype=jnp.int32)
    own_start = tensor_rank * own_count
    kept_normed = jnp.zeros((blocks, block_len, seq_count, model_dim), bf16)
    kept_query = jnp.zeros((blocks, block_len, seq_count, heads_local * HD), bf16)
    kept_attended = jnp.zeros((blocks, block_len, seq_count, heads_local * HD), bf16)
    kept_logsum = jnp.zeros((blocks, seq_count, block_len, heads_local), f32)
    kv_cache = jnp.zeros((total_len, seq_count, 2 * HD), bf16)
    kept_input = jnp.zeros((blocks, own_count, seq_count, model_dim), f32)
    kept_hidden = jnp.zeros((blocks, own_count, seq_count, model_dim), f32)
    kept_normed_two = jnp.zeros((blocks, block_len, seq_count, model_dim), bf16)
    kept_pre = jnp.zeros((blocks, block_len, seq_count, ff_local), f32)
    outputs = jnp.zeros((blocks, own_count, seq_count, model_dim), bf16)
    received = jnp.zeros((own_count, seq_count, model_dim), f32)
    for turn in range(blocks + 1):
        block_index = jnp.clip(turn - section, 0, blocks - 1)
        from_input = lax.dynamic_index_in_dim(tokens_in, block_index, 0, keepdims=False).astype(f32)
        layer_input = jnp.where(section == 0, from_input, received)
        normed = gather_rows(layer_norm(layer_input, gain_one, bias_one).astype(bf16))
        query = (
            jnp.einsum("rsd,de->rse", normed, w_query, preferred_element_type=f32) + b_query
        ).astype(bf16)
        pairs = jnp.einsum("rsd,dc->rsc", normed, w_pairs, preferred_element_type=f32) + pair_bias
        kv_cache = lax.dynamic_update_slice_in_dim(
            kv_cache, pairs.astype(bf16), block_index * block_len, 0
        )
        key_rows = kv_cache[..., :HD]
        value_rows = kv_cache[..., HD:]
        visible = positions < (block_index + 1) * block_len
        query_heads = query.reshape(block_len, seq_count, heads_local, HD)
        scores = (
            jnp.einsum("qshd,ksd->sqhk", query_heads, key_rows, preferred_element_type=f32)
            * score_scale
        )
        scores = jnp.where(visible, scores, -1e30)
        row_top = jnp.max(scores, axis=-1, keepdims=True)
        exponent = jnp.exp(scores - row_top)
        row_total = jnp.sum(exponent, axis=-1, keepdims=True)
        log_total = (row_top + jnp.log(row_total))[..., 0]
        weights_low = (exponent / row_total).astype(bf16)
        attended = jnp.einsum("sqhk,ksd->qshd", weights_low, value_rows, preferred_element_type=f32)
        attended = attended.reshape(block_len, seq_count, heads_local * HD).astype(bf16)

        def attention_term(start, count, attended=attended):
            return jnp.einsum("rse,ed->rsd", attended, w_out, preferred_element_type=f32)

        hidden = layer_input + sum_rows(attention_term, own_count) + b_out
        normed_two = gather_rows(layer_norm(hidden, gain_two, bias_two).astype(bf16))
        pre_active = jnp.einsum("rsd,df->rsf", normed_two, w_up, preferred_element_type=f32) + b_up
        active = gelu_tanh(pre_active).astype(bf16)

        def feed_term(start, count, active=active):
            return jnp.einsum("rsf,fd->rsd", active, w_down, preferred_element_type=f32)

        result_low = (hidden + sum_rows(feed_term, own_count) + b_down).astype(bf16)
        kept_normed = lax.dynamic_update_index_in_dim(kept_normed, normed, block_index, 0)
        kept_query = lax.dynamic_update_index_in_dim(kept_query, query, block_index, 0)
        kept_attended = lax.dynamic_update_index_in_dim(kept_attended, attended, block_index, 0)
        kept_logsum = lax.dynamic_update_index_in_dim(kept_logsum, log_total, block_index, 0)
        kept_input = lax.dynamic_update_index_in_dim(kept_input, layer_input, block_index, 0)
        kept_hidden = lax.dynamic_update_index_in_dim(kept_hidden, hidden, block_index, 0)
        kept_normed_two = lax.dynamic_update_index_in_dim(
            kept_normed_two, normed_two, block_index, 0
        )
        kept_pre = lax.dynamic_update_index_in_dim(kept_pre, pre_active, block_index, 0)
        outputs = lax.dynamic_update_index_in_dim(outputs, result_low, block_index, 0)
        received = from_behind(result_low, "section", 1).astype(f32)
    key_rows = kv_cache[..., :HD]
    value_rows = kv_cache[..., HD:]
    sharded_total = (
        jnp.zeros(w_query.shape, f32),
        jnp.zeros(b_query.shape, f32),
        jnp.zeros(w_out.shape, f32),
        jnp.zeros(w_up.shape, f32),
        jnp.zeros(b_up.shape, f32),
        jnp.zeros(w_down.shape, f32),
    )
    common_total = (
        jnp.zeros(gain_one.shape, f32),
        jnp.zeros(bias_one.shape, f32),
        jnp.zeros(b_out.shape, f32),
        jnp.zeros(gain_two.shape, f32),
        jnp.zeros(bias_two.shape, f32),
        jnp.zeros(b_down.shape, f32),
    )
    pair_total = (jnp.zeros(w_pairs.shape, f32), jnp.zeros((HD,), f32))
    sharded_total = sharded_total + pair_total
    pair_grad_acc = jnp.zeros((total_len, seq_count, 2 * HD), f32)
    input_grads = jnp.zeros((blocks, own_count, seq_count, model_dim), f32)
    received_back = jnp.zeros((own_count, seq_count, model_dim), f32)
    for turn in range(blocks + 1):
        step_count = turn - (1 - section)
        valid = (step_count >= 0) & (step_count < blocks)
        valid_scale = valid.astype(f32)
        block_index = blocks - 1 - jnp.clip(step_count, 0, blocks - 1)
        from_cot = lax.dynamic_index_in_dim(cotangent, block_index, 0, keepdims=False).astype(f32)
        grad_out = jnp.where(section == 1, from_cot, received_back) * valid_scale
        pre_active = lax.dynamic_index_in_dim(kept_pre, block_index, 0, keepdims=False)
        normed_two = lax.dynamic_index_in_dim(kept_normed_two, block_index, 0, keepdims=False)
        active = gelu_tanh(pre_active).astype(bf16)
        grad_mlp = gather_rows(grad_out.astype(bf16))
        grad_active = jnp.einsum("rsd,fd->rsf", grad_mlp, w_down, preferred_element_type=f32)
        gelu_back = jax.vjp(gelu_tanh, pre_active)[1]
        grad_pre = gelu_back(grad_active)[0].astype(bf16)
        down_w_term = jnp.einsum("rsf,rsd->fd", active, grad_mlp, preferred_element_type=f32)
        up_w_term = jnp.einsum("rsd,rsf->df", normed_two, grad_pre, preferred_element_type=f32)
        up_b_term = jnp.sum(grad_pre.astype(f32), axis=(0, 1))
        down_b_term = jnp.sum(grad_out, axis=(0, 1))

        def feed_back_term(start, count, grad_pre=grad_pre):
            return jnp.einsum("rsf,df->rsd", grad_pre, w_up, preferred_element_type=f32)

        grad_normed_two = sum_rows(feed_back_term, own_count)
        hidden_own = lax.dynamic_index_in_dim(kept_hidden, block_index, 0, keepdims=False)
        norm_back_two = jax.vjp(layer_norm, hidden_own, gain_two, bias_two)[1]
        grad_hidden_norm, gain_two_term, bias_two_term = norm_back_two(grad_normed_two)
        grad_hidden = grad_out + grad_hidden_norm
        out_b_term = jnp.sum(grad_hidden, axis=(0, 1))
        grad_branch = gather_rows(grad_hidden.astype(bf16))
        attended = lax.dynamic_index_in_dim(kept_attended, block_index, 0, keepdims=False)
        out_w_term = jnp.einsum("rse,rsd->ed", attended, grad_branch, preferred_element_type=f32)
        grad_attended = jnp.einsum(
            "rsd,ed->rse", grad_branch, w_out, preferred_element_type=f32
        ).astype(bf16)
        grad_attended = grad_attended.reshape(block_len, seq_count, heads_local, HD)
        query = lax.dynamic_index_in_dim(kept_query, block_index, 0, keepdims=False)
        query_heads = query.reshape(block_len, seq_count, heads_local, HD)
        log_total = lax.dynamic_index_in_dim(kept_logsum, block_index, 0, keepdims=False)
        visible = positions < (block_index + 1) * block_len
        scores = (
            jnp.einsum("qshd,ksd->sqhk", query_heads, key_rows, preferred_element_type=f32)
            * score_scale
        )
        scores = jnp.where(visible, scores, -1e30)
        probabilities = jnp.exp(scores - log_total[..., None])
        grad_probs = jnp.einsum(
            "qshd,ksd->sqhk", grad_attended, value_rows, preferred_element_type=f32
        )
        row_inner = jnp.sum(probabilities * grad_probs, axis=-1, keepdims=True)
        grad_scores = (probabilities * (grad_probs - row_inner)).astype(bf16)
        grad_query = (
            jnp.einsum("sqhk,ksd->qshd", grad_scores, key_rows, preferred_element_type=f32)
            * score_scale
        )
        grad_query = grad_query.astype(bf16).reshape(block_len, seq_count, heads_local * HD)
        grad_keys = (
            jnp.einsum("sqhk,qshd->ksd", grad_scores, query_heads, preferred_element_type=f32)
            * score_scale
        )
        grad_values = jnp.einsum(
            "sqhk,qshd->ksd", probabilities.astype(bf16), grad_attended, preferred_element_type=f32
        )
        pair_grad_acc = pair_grad_acc + jnp.concatenate([grad_keys, grad_values], axis=-1)
        block_pairs = lax.dynamic_slice_in_dim(pair_grad_acc, block_index * block_len, block_len, 0)
        grad_pairs = (
            lax.psum(block_pairs.astype(jnp.bfloat16), "tensor").astype(jnp.float32) * valid_scale
        ).astype(bf16)
        normed = lax.dynamic_index_in_dim(kept_normed, block_index, 0, keepdims=False)
        query_w_term = jnp.einsum("rsd,rse->de", normed, grad_query, preferred_element_type=f32)
        query_b_term = jnp.sum(grad_query.astype(f32), axis=(0, 1))
        own_pairs = lax.dynamic_slice_in_dim(grad_pairs, own_start, own_count, 0)
        pair_w_term = jnp.einsum("rsd,rsc->dc", normed, grad_pairs, preferred_element_type=f32)
        value_b_term = jnp.sum(grad_pairs[..., HD:].astype(f32), axis=(0, 1))

        def attention_back_term(start, count, grad_query=grad_query):
            return jnp.einsum("rse,de->rsd", grad_query, w_query, preferred_element_type=f32)

        grad_normed = sum_rows(attention_back_term, own_count)
        grad_normed = grad_normed + jnp.einsum(
            "rsc,dc->rsd", own_pairs, w_pairs, preferred_element_type=f32
        )
        layer_input = lax.dynamic_index_in_dim(kept_input, block_index, 0, keepdims=False)
        norm_back_one = jax.vjp(layer_norm, layer_input, gain_one, bias_one)[1]
        grad_input_norm, gain_one_term, bias_one_term = norm_back_one(grad_normed)
        grad_input = grad_hidden + grad_input_norm
        previous = lax.dynamic_index_in_dim(input_grads, block_index, 0, keepdims=False)
        input_grads = lax.dynamic_update_index_in_dim(
            input_grads, jnp.where(valid, grad_input, previous), block_index, 0
        )
        received_back = from_behind(grad_input.astype(jnp.bfloat16), "section", -1).astype(
            grad_input.dtype
        )
        sharded_terms = (query_w_term, query_b_term, out_w_term, up_w_term, up_b_term, down_w_term)
        common_terms = (
            gain_one_term,
            bias_one_term,
            out_b_term,
            gain_two_term,
            bias_two_term,
            down_b_term,
        )
        pair_terms = (pair_w_term, value_b_term)
        sharded_terms = sharded_terms + pair_terms
        sharded_total = jax.tree.map(jnp.add, sharded_total, sharded_terms)
        common_total = jax.tree.map(jnp.add, common_total, common_terms)
    sharded_total = jax.tree.map(
        lambda part: part.astype(jnp.float32), lax.psum(for_sending(sharded_total), "dp")
    )
    common_total = lax.psum(common_total, ("tensor", "dp"))
    pair_w_grad, value_b_grad = (sharded_total[6], sharded_total[7])
    return (
        outputs[None],
        input_grads[None],
        common_total[0][None],
        common_total[1][None],
        sharded_total[0][None],
        sharded_total[1][None],
        pair_w_grad[None],
        value_b_grad[None],
        sharded_total[2][None],
        common_total[2][None],
        common_total[3][None],
        common_total[4][None],
        sharded_total[3][None],
        sharded_total[4][None],
        sharded_total[5][None],
        common_total[5][None],
    )


def solution(mesh):
    placed = (
        P(None, "tensor", "dp", None),
        P(None, "tensor", "dp", None),
        P("section", None),
        P("section", None),
        P("section", None, "tensor"),
        P("section", "tensor"),
        P("section", None, None),
        P("section", None),
        P("section", "tensor", None),
        P("section", None),
        P("section", None),
        P("section", None),
        P("section", None, "tensor"),
        P("section", "tensor"),
        P("section", "tensor", None),
        P("section", None),
    )
    return jax.shard_map(
        on_device,
        mesh=mesh,
        in_specs=placed,
        out_specs=(
            P("section", None, "tensor", "dp", None),
            P("section", None, "tensor", "dp", None),
            P("section", None),
            P("section", None),
            P("section", None, "tensor"),
            P("section", "tensor"),
            P("section", None, None),
            P("section", None),
            P("section", "tensor", None),
            P("section", None),
            P("section", None),
            P("section", None),
            P("section", None, "tensor"),
            P("section", "tensor"),
            P("section", "tensor", None),
            P("section", None),
        ),
        check_vma=False,
    )
```

profile of v0, /device:TPU:1, one launch (start us, length us, event | category | flops | bytes accessed | tf_op | source)
XLA Modules:
  0.0 2236.0 jit_solution(8627879829273172787)
XLA Ops:
  15.2 28.6 %all-gather.21.cloned.1.call-done = bf16[256,1,2048]{2,0,1:T(8,128)(2,1)} async-done(((bf16[64,1,2048]{2,0,1:T(8,128)(2,1)}), bf16[256,1,2048]{2,0,1:T(8,128)(2,1)}) %all-gather.21.cloned.1.call-update) | async-done | bytes 1048592 | tf_op jit(solution)/shard_map/all_gather | solution.py:33
  52.4 26.6 %reduce-scatter.21.cloned.1.call-done = bf16[64,1,2048]{2,0,1:T(8,128)(2,1)} async-done(((bf16[256,1,2048]{2,0,1:T(8,128)(2,1)}), bf16[64,1,2048]{2,0,1:T(8,128)(2,1)}) %reduce-scatter.21.cloned.1.call-update) | async-done | bytes 262160 | tf_op jit(solution)/shard_map/reduce_scatter | solution.py:37
  84.4 26.7 %all-gather.23.cloned.1.call-done = bf16[256,1,2048]{2,0,1:T(8,128)(2,1)} async-done(((bf16[64,1,2048]{2,0,1:T(8,128)(2,1)}), bf16[256,1,2048]{2,0,1:T(8,128)(2,1)}) %all-gather.23.cloned.1.call-update) | async-done | bytes 1048592 | tf_op jit(solution)/shard_map/all_gather | solution.py:33
  126.4 26.7 %reduce-scatter.23.cloned.1.call-done = bf16[64,1,2048]{2,0,1:T(8,128)(2,1)} async-done(((bf16[256,1,2048]{2,0,1:T(8,128)(2,1)}), bf16[64,1,2048]{2,0,1:T(8,128)(2,1)}) %reduce-scatter.23.cloned.1.call-update) | async-done | bytes 262160 | tf_op jit(solution)/shard_map/reduce_scatter | solution.py:37
  168.4 28.6 %all-gather.25.cloned.1.call-done = bf16[256,1,2048]{2,0,1:T(8,128)(2,1)} async-done(((bf16[64,1,2048]{2,0,1:T(8,128)(2,1)}), bf16[256,1,2048]{2,0,1:T(8,128)(2,1)}) %all-gather.25.cloned.1.call-update) | async-done | bytes 1048592 | tf_op jit(solution)/shard_map/all_gather | solution.py:33
  205.4 26.7 %reduce-scatter.25.cloned.1.call-done = bf16[64,1,2048]{2,0,1:T(8,128)(2,1)} async-done(((bf16[256,1,2048]{2,0,1:T(8,128)(2,1)}), bf16[64,1,2048]{2,0,1:T(8,128)(2,1)}) %reduce-scatter.25.cloned.1.call-update) | async-done | bytes 262160 | tf_op jit(solution)/shard_map/reduce_scatter | solution.py:37
  234.6 26.7 %all-gather.27.cloned.1.call-done = bf16[256,1,2048]{2,0,1:T(8,128)(2,1)} async-done(((bf16[64,1,2048]{2,0,1:T(8,128)(2,1)}), bf16[256,1,2048]{2,0,1:T(8,128)(2,1)}) %all-gather.27.cloned.1.call-update) | async-done | bytes 1048592 | tf_op jit(solution)/shard_map/all_gather | solution.py:33
  275.6 26.7 %reduce-scatter.27.cloned.1.call-done = bf16[64,1,2048]{2,0,1:T(8,128)(2,1)} async-done(((bf16[256,1,2048]{2,0,1:T(8,128)(2,1)}), bf16[64,1,2048]{2,0,1:T(8,128)(2,1)}) %reduce-scatter.27.cloned.1.call-update) | async-done | bytes 262160 | tf_op jit(solution)/shard_map/reduce_scatter | solution.py:37
  317.8 28.3 %all-gather.29.cloned.1.call-done = bf16[256,1,2048]{2,0,1:T(8,128)(2,1)} async-done(((bf16[64,1,2048]{2,0,1:T(8,128)(2,1)}), bf16[256,1,2048]{2,0,1:T(8,128)(2,1)}) %all-gather.29.cloned.1.call-update) | async-done | bytes 1048592 | tf_op jit(solution)/shard_map/all_gather | solution.py:33
  355.2 26.7 %reduce-scatter.29.cloned.1.call-done = bf16[64,1,2048]{2,0,1:T(8,128)(2,1)} async-done(((bf16[256,1,2048]{2,0,1:T(8,128)(2,1)}), bf16[64,1,2048]{2,0,1:T(8,128)(2,1)}) %reduce-scatter.29.cloned.1.call-update) | async-done | bytes 262160 | tf_op jit(solution)/shard_map/reduce_scatter | solution.py:37
  384.9 26.7 %all-gather.31.cloned.1.call-done = bf16[256,1,2048]{2,0,1:T(8,128)(2,1)} async-done(((bf16[64,1,2048]{2,0,1:T(8,128)(2,1)}), bf16[256,1,2048]{2,0,1:T(8,128)(2,1)}) %all-gather.31.cloned.1.call-update) | async-done | bytes 1048592 | tf_op jit(solution)/shard_map/all_gather | solution.py:33
  426.0 26.7 %reduce-scatter.31.cloned.1.call-done = bf16[64,1,2048]{2,0,1:T(8,128)(2,1)} async-done(((bf16[256,1,2048]{2,0,1:T(8,128)(2,1)}), bf16[64,1,2048]{2,0,1:T(8,128)(2,1)}) %reduce-scatter.31.cloned.1.call-update) | async-done | bytes 262160 | tf_op jit(solution)/shard_map/reduce_scatter | solution.py:37
  468.0 28.5 %all-gather.33.cloned.1.call-done = bf16[256,1,2048]{2,0,1:T(8,128)(2,1)} async-done(((bf16[64,1,2048]{2,0,1:T(8,128)(2,1)}), bf16[256,1,2048]{2,0,1:T(8,128)(2,1)}) %all-gather.33.cloned.1.call-update) | async-done | bytes 1048592 | tf_op jit(solution)/shard_map/all_gather | solution.py:33
  505.6 26.7 %reduce-scatter.33.cloned.1.call-done = bf16[64,1,2048]{2,0,1:T(8,128)(2,1)} async-done(((bf16[256,1,2048]{2,0,1:T(8,128)(2,1)}), bf16[64,1,2048]{2,0,1:T(8,128)(2,1)}) %reduce-scatter.33.cloned.1.call-update) | async-done | bytes 262160 | tf_op jit(solution)/shard_map/reduce_scatter | solution.py:37
  535.3 26.7 %all-gather.35.cloned.1.call-done = bf16[256,1,2048]{2,0,1:T(8,128)(2,1)} async-done(((bf16[64,1,2048]{2,0,1:T(8,128)(2,1)}), bf16[256,1,2048]{2,0,1:T(8,128)(2,1)}) %all-gather.35.cloned.1.call-update) | async-done | bytes 1048592 | tf_op jit(solution)/shard_map/all_gather | solution.py:33
  576.4 26.8 %reduce-scatter.35.cloned.1.call-done = bf16[64,1,2048]{2,0,1:T(8,128)(2,1)} async-done(((bf16[256,1,2048]{2,0,1:T(8,128)(2,1)}), bf16[64,1,2048]{2,0,1:T(8,128)(2,1)}) %reduce-scatter.35.cloned.1.call-update) | async-done | bytes 262160 | tf_op jit(solution)/shard_map/reduce_scatter | solution.py:37
  618.3 28.7 %all-gather.37.cloned.1.call-done = bf16[256,1,2048]{2,0,1:T(8,128)(2,1)} async-done(((bf16[64,1,2048]{2,0,1:T(8,128)(2,1)}), bf16[256,1,2048]{2,0,1:T(8,128)(2,1)}) %all-gather.37.cloned.1.call-update) | async-done | bytes 1048592 | tf_op jit(solution)/shard_map/all_gather | solution.py:33
  656.2 26.7 %reduce-scatter.37.cloned.1.call-done = bf16[64,1,2048]{2,0,1:T(8,128)(2,1)} async-done(((bf16[256,1,2048]{2,0,1:T(8,128)(2,1)}), bf16[64,1,2048]{2,0,1:T(8,128)(2,1)}) %reduce-scatter.37.cloned.1.call-update) | async-done | bytes 262160 | tf_op jit(solution)/shard_map/reduce_scatter | solution.py:37
  865.7 30.7 %reduce-scatter.43.cloned.1.call-done = bf16[64,1,2048]{2,0,1:T(8,128)(2,1)} async-done(((bf16[256,1,2048]{2,0,1:T(8,128)(2,1)}), bf16[64,1,2048]{2,0,1:T(8,128)(2,1)}) %reduce-scatter.43.cloned.1.call-update) | async-done | bytes 262160 | tf_op jit(solution)/shard_map/reduce_scatter | solution.py:37
  911.7 26.9 %all-gather.45.cloned.1.call-done = bf16[256,1,2048]{2,0,1:T(8,128)(2,1)} async-done(((bf16[64,1,2048]{2,0,1:T(8,128)(2,1)}), bf16[256,1,2048]{2,0,1:T(8,128)(2,1)}) %all-gather.45.cloned.1.call-update) | async-done | bytes 1048592 | tf_op jit(solution)/shard_map/all_gather | solution.py:33
  955.9 25.5 %reduce-scatter.45.cloned.1.call-done = bf16[64,1,2048]{2,0,1:T(8,128)(2,1)} async-done(((bf16[256,1,2048]{2,0,1:T(8,128)(2,1)}), bf16[64,1,2048]{2,0,1:T(8,128)(2,1)}) %reduce-scatter.45.cloned.1.call-update) | async-done | bytes 262160 | tf_op jit(solution)/shard_map/reduce_scatter | solution.py:37
  1065.2 30.1 %reduce-scatter.47.cloned.1.call-done = bf16[64,1,2048]{2,0,1:T(8,128)(2,1)} async-done(((bf16[256,1,2048]{2,0,1:T(8,128)(2,1)}), bf16[64,1,2048]{2,0,1:T(8,128)(2,1)}) %reduce-scatter.47.cloned.1.call-update) | async-done | bytes 262160 | tf_op jit(solution)/shard_map/reduce_scatter | solution.py:37
  1110.9 26.7 %all-gather.49.cloned.1.call-done = bf16[256,1,2048]{2,0,1:T(8,128)(2,1)} async-done(((bf16[64,1,2048]{2,0,1:T(8,128)(2,1)}), bf16[256,1,2048]{2,0,1:T(8,128)(2,1)}) %all-gather.49.cloned.1.call-update) | async-done | bytes 1048592 | tf_op jit(solution)/shard_map/all_gather | solution.py:33
  1154.8 25.6 %reduce-scatter.49.cloned.1.call-done = bf16[64,1,2048]{2,0,1:T(8,128)(2,1)} async-done(((bf16[256,1,2048]{2,0,1:T(8,128)(2,1)}), bf16[64,1,2048]{2,0,1:T(8,128)(2,1)}) %reduce-scatter.49.cloned.1.call-update) | async-done | bytes 262160 | tf_op jit(solution)/shard_map/reduce_scatter | solution.py:37
  1264.2 30.2 %reduce-scatter.51.cloned.1.call-done = bf16[64,1,2048]{2,0,1:T(8,128)(2,1)} async-done(((bf16[256,1,2048]{2,0,1:T(8,128)(2,1)}), bf16[64,1,2048]{2,0,1:T(8,128)(2,1)}) %reduce-scatter.51.cloned.1.call-update) | async-done | bytes 262160 | tf_op jit(solution)/shard_map/reduce_scatter | solution.py:37
  1310.1 26.6 %all-gather.53.cloned.1.call-done = bf16[256,1,2048]{2,0,1:T(8,128)(2,1)} async-done(((bf16[64,1,2048]{2,0,1:T(8,128)(2,1)}), bf16[256,1,2048]{2,0,1:T(8,128)(2,1)}) %all-gather.53.cloned.1.call-update) | async-done | bytes 1048592 | tf_op jit(solution)/shard_map/all_gather | solution.py:33
  1354.0 25.5 %reduce-scatter.53.cloned.1.call-done = bf16[64,1,2048]{2,0,1:T(8,128)(2,1)} async-done(((bf16[256,1,2048]{2,0,1:T(8,128)(2,1)}), bf16[64,1,2048]{2,0,1:T(8,128)(2,1)}) %reduce-scatter.53.cloned.1.call-update) | async-done | bytes 262160 | tf_op jit(solution)/shard_map/reduce_scatter | solution.py:37
  1463.3 29.9 %reduce-scatter.55.cloned.1.call-done = bf16[64,1,2048]{2,0,1:T(8,128)(2,1)} async-done(((bf16[256,1,2048]{2,0,1:T(8,128)(2,1)}), bf16[64,1,2048]{2,0,1:T(8,128)(2,1)}) %reduce-scatter.55.cloned.1.call-update) | async-done | bytes 262160 | tf_op jit(solution)/shard_map/reduce_scatter | solution.py:37
  1744.9 26.9 %fusion.41 = bf16[1,2048,2048]{2,1,0:T(8,128)(2,1)} fusion(f32[2048,2048]{1,0:T(8,128)} %fusion.438, f32[2048,2048]{1,0:T(8,128)} %fusion.440, f32[2048,2048]{1,0:T(8,128)} %fusion.444, f32[2048,2048]{1,0:T(8,128)} %fusion.442, bf16[256,1,2048]{2,0,1:T(8,128)(2,1)S(1)} %copy-done.77, f32[4,256,1,2048]{3,1,2,0:T(8,128)} %get-tuple-element.207, s32[]{:T(128)S(6)} %select_n.364), kind=kOutput, calls=%fused_computation.43 | convolution fusion | flops 2173173760 | bytes 78643200 | tf_op jit(solution)/shard_map/rsf,rsd->fd/dot_general | solution.py:191
  1775.3 27.2 %fusion.40 = bf16[1,2048,2048]{2,1,0:T(8,128)(2,1)} fusion(bf16[256,2048]{1,0:T(8,128)(2,1)} %copy-done.78, f32[2048,2048]{1,0:T(8,128)} %fusion.447, f32[2048,2048]{1,0:T(8,128)} %fusion.449, f32[2048,2048]{1,0:T(8,128)} %fusion.453, f32[2048,2048]{1,0:T(8,128)} %fusion.451, bf16[4,256,1,2048]{3,1,2,0:T(8,128)(2,1)} %bitcast_dynamic-update-slice_fusion.5, ...), kind=kOutput, calls=%fused_computation.42 | convolution fusion | flops 2168455168 | bytes 77594624 | tf_op jit(solution)/shard_map/rsd,rsf->df/dot_general | solution.py:192
  1848.7 58.0 %all-reduce.1 = (f32[1,2048]{1,0:T(1,128)}, f32[1,2048]{1,0:T(1,128)}, f32[1,2048]{1,0:T(1,128)}, f32[1,2048]{1,0:T(1,128)}, f32[1,2048]{1,0:T(1,128)}, /*index=5*/f32[1,2048]{1,0:T(1,128)}) all-reduce(f32[1,2048]{1,0:T(1,128)S(1)} %bitcast.1391, ...), channel_id=1, replica_groups=mesh['section'=2,'tensor'=4,'dp'=4] {'tensor','dp'}, use_global_device_ids=true, to_apply=%region_105.106 | all-reduce | flops 12288 | bytes 98304 | tf_op jit(solution)/shard_map/psum | solution.py:285
  1911.0 285.5 %all-reduce.21.cloned.1.call-done = (bf16[1,2048,512]{2,1,0:T(8,128)(2,1)}, bf16[1,2048,256]{2,1,0:T(8,128)(2,1)}, bf16[1,512,2048]{2,1,0:T(8,128)(2,1)}, bf16[1...) async-done(((bf16[1,2048,512]{2,1,0:T(8,128)(2,1)}, bf16[1,2048,256]{2,1,0:T(8,128)(2,1)}, bf16[1,512,2048]{2,1,0:T(8,128)(2,1)}, bf16[1,2048,2048]{2,1,0:T(8,128)(2,1)}, ...) | async-done | bytes 22020112 | tf_op jit(solution)/shard_map/psum | solution.py:283
  (929 shorter events, 1053.1 us)
Async XLA Ops:
  13.8 65.3 %reduce-scatter.21.cloned.1.call-start = ((), (), s32[]{:S(2)}) async-start(), calls=%async_computation.21 | async-start | bytes 1310720 | tf_op jit(solution)/shard_map/reduce_scatter | solution.py:37
  84.4 68.7 %reduce-scatter.23.cloned.1.call-start = ((), (), s32[]{:S(2)}) async-start(), calls=%async_computation.23 | async-start | bytes 1310720 | tf_op jit(solution)/shard_map/reduce_scatter | solution.py:37
  126.3 70.7 %all-gather.25.cloned.1.call-start = ((), (), s32[]{:S(2)}) async-start(), calls=%async_computation.24 | async-start | bytes 1310720 | tf_op jit(solution)/shard_map/all_gather | solution.py:33
  168.1 64.0 %reduce-scatter.25.cloned.1.call-start = ((), (), s32[]{:S(2)}) async-start(), calls=%async_computation.25 | async-start | bytes 1310720 | tf_op jit(solution)/shard_map/reduce_scatter | solution.py:37
  234.6 67.8 %reduce-scatter.27.cloned.1.call-start = ((), (), s32[]{:S(2)}) async-start(), calls=%async_computation.27 | async-start | bytes 1310720 | tf_op jit(solution)/shard_map/reduce_scatter | solution.py:37
  275.6 70.5 %all-gather.29.cloned.1.call-start = ((), (), s32[]{:S(2)}) async-start(), calls=%async_computation.28 | async-start | bytes 1310720 | tf_op jit(solution)/shard_map/all_gather | solution.py:33
  317.3 64.6 %reduce-scatter.29.cloned.1.call-start = ((), (), s32[]{:S(2)}) async-start(), calls=%async_computation.29 | async-start | bytes 1310720 | tf_op jit(solution)/shard_map/reduce_scatter | solution.py:37
  384.9 67.8 %reduce-scatter.31.cloned.1.call-start = ((), (), s32[]{:S(2)}) async-start(), calls=%async_computation.31 | async-start | bytes 1310720 | tf_op jit(solution)/shard_map/reduce_scatter | solution.py:37
  425.9 70.5 %all-gather.33.cloned.1.call-start = ((), (), s32[]{:S(2)}) async-start(), calls=%async_computation.32 | async-start | bytes 1310720 | tf_op jit(solution)/shard_map/all_gather | solution.py:33
  467.7 64.6 %reduce-scatter.33.cloned.1.call-start = ((), (), s32[]{:S(2)}) async-start(), calls=%async_computation.33 | async-start | bytes 1310720 | tf_op jit(solution)/shard_map/reduce_scatter | solution.py:37
  535.3 67.9 %reduce-scatter.35.cloned.1.call-start = ((), (), s32[]{:S(2)}) async-start(), calls=%async_computation.35 | async-start | bytes 1310720 | tf_op jit(solution)/shard_map/reduce_scatter | solution.py:37
  576.3 70.7 %all-gather.37.cloned.1.call-start = ((), (), s32[]{:S(2)}) async-start(), calls=%async_computation.36 | async-start | bytes 1310720 | tf_op jit(solution)/shard_map/all_gather | solution.py:33
  618.3 64.6 %reduce-scatter.37.cloned.1.call-start = ((), (), s32[]{:S(2)}) async-start(), calls=%async_computation.37 | async-start | bytes 1310720 | tf_op jit(solution)/shard_map/reduce_scatter | solution.py:37
  688.2 96.1 %reduce-scatter.41.cloned.1.call-start = ((), (), s32[]{:S(2)}) async-start(), calls=%async_computation.41 | async-start | bytes 1310720 | tf_op jit(solution)/shard_map/reduce_scatter | solution.py:37
  792.4 72.4 %all-reduce.11.cloned.1.call-start = ((), (), s32[]{:S(2)}) async-start(), calls=%async_computation.44 | async-start | bytes 262144 | tf_op jit(solution)/shard_map/psum | solution.py:242
  836.0 102.5 %all-gather.45.cloned.1.call-start = ((), (), s32[]{:S(2)}) async-start(), calls=%async_computation.45 | async-start | bytes 1310720 | tf_op jit(solution)/shard_map/all_gather | solution.py:33
  911.6 69.8 %reduce-scatter.45.cloned.1.call-start = ((), (), s32[]{:S(2)}) async-start(), calls=%async_computation.46 | async-start | bytes 1310720 | tf_op jit(solution)/shard_map/reduce_scatter | solution.py:37
  989.5 74.1 %all-reduce.13.cloned.1.call-start = ((), (), s32[]{:S(2)}) async-start(), calls=%async_computation.49 | async-start | bytes 262144 | tf_op jit(solution)/shard_map/psum | solution.py:242
  1031.5 63.8 %reduce-scatter.47.cloned.1.call-start = ((), (), s32[]{:S(2)}) async-start(), calls=%async_computation.48 | async-start | bytes 1310720 | tf_op jit(solution)/shard_map/reduce_scatter | solution.py:37
  1035.0 102.6 %all-gather.49.cloned.1.call-start = ((), (), s32[]{:S(2)}) async-start(), calls=%async_computation.50 | async-start | bytes 1310720 | tf_op jit(solution)/shard_map/all_gather | solution.py:33
  1110.7 69.8 %reduce-scatter.49.cloned.1.call-start = ((), (), s32[]{:S(2)}) async-start(), calls=%async_computation.51 | async-start | bytes 1310720 | tf_op jit(solution)/shard_map/reduce_scatter | solution.py:37
  1188.5 74.1 %all-reduce.15.cloned.1.call-start = ((), (), s32[]{:S(2)}) async-start(), calls=%async_computation.54 | async-start | bytes 262144 | tf_op jit(solution)/shard_map/psum | solution.py:242
  1230.5 63.9 %reduce-scatter.51.cloned.1.call-start = ((), (), s32[]{:S(2)}) async-start(), calls=%async_computation.53 | async-start | bytes 1310720 | tf_op jit(solution)/shard_map/reduce_scatter | solution.py:37
  1234.0 102.7 %all-gather.53.cloned.1.call-start = ((), (), s32[]{:S(2)}) async-start(), calls=%async_computation.55 | async-start | bytes 1310720 | tf_op jit(solution)/shard_map/all_gather | solution.py:33
  1309.8 69.8 %reduce-scatter.53.cloned.1.call-start = ((), (), s32[]{:S(2)}) async-start(), calls=%async_computation.56 | async-start | bytes 1310720 | tf_op jit(solution)/shard_map/reduce_scatter | solution.py:37
  1387.6 74.1 %all-reduce.17.cloned.1.call-start = ((), (), s32[]{:S(2)}) async-start(), calls=%async_computation.59 | async-start | bytes 262144 | tf_op jit(solution)/shard_map/psum | solution.py:242
  1433.1 103.3 %all-gather.57.cloned.1.call-start = ((), (), s32[]{:S(2)}) async-start(), calls=%async_computation.60 | async-start | bytes 1310720 | tf_op jit(solution)/shard_map/all_gather | solution.py:33
  1509.4 69.8 %reduce-scatter.57.cloned.1.call-start = ((), (), s32[]{:S(2)}) async-start(), calls=%async_computation.61 | async-start | bytes 1310720 | tf_op jit(solution)/shard_map/reduce_scatter | solution.py:37
  1586.8 228.9 %all-reduce.19.cloned.1.call-start = ((), (), s32[]{:S(2)}) async-start(), calls=%async_computation.64 | async-start | bytes 262144 | tf_op jit(solution)/shard_map/psum | solution.py:242
  1625.5 198.8 %reduce-scatter.39.cloned.1.call-start = ((), (), s32[]{:S(2)}) async-start(), calls=%async_computation.39 | async-start | bytes 1310720 | tf_op jit(solution)/shard_map/reduce_scatter | solution.py:37
  1635.2 210.7 %reduce-scatter.59.cloned.1.call-start = ((), (), s32[]{:S(2)}) async-start(), calls=%async_computation.63 | async-start | bytes 1310720 | tf_op jit(solution)/shard_map/reduce_scatter | solution.py:37
  1775.2 421.3 %all-reduce.21.cloned.1.call-start = ((), (), s32[]{:S(2)}) async-start(), calls=%async_computation.65 | async-start | bytes 44040192 | tf_op jit(solution)/shard_map/psum | solution.py:283
  (237 other events, 4304.5 us)
Sparse Core Ops, SparseCore 0:
  13.9 29.8 all-gather.20
  52.4 26.6 reduce-scatter.20
  168.2 28.6 all-gather.24
  205.5 26.6 reduce-scatter.24
  275.7 26.6 reduce-scatter.26
  317.4 28.5 all-gather.28
  467.8 28.6 all-gather.32
  505.7 26.6 reduce-scatter.32
  535.4 26.6 all-gather.34
  576.5 26.6 reduce-scatter.34
  618.4 28.5 all-gather.36
  656.2 26.6 reduce-scatter.36
  714.1 27.4 all-gather.40
  792.5 26.6 all-gather.42
  832.8 31.9 all-reduce.10
  867.6 28.7 reduce-scatter.42
  911.7 26.7 all-gather.44
  1031.6 31.9 all-reduce.12
  1066.5 28.7 reduce-scatter.46
  1110.8 26.7 all-gather.48
  1188.6 26.6 all-gather.50
  1230.6 31.9 all-reduce.14
  1265.6 28.7 reduce-scatter.50
  1309.9 26.7 all-gather.52
  1387.7 26.6 all-gather.54
  1429.7 31.9 all-reduce.16
  1464.4 28.7 reduce-scatter.54
  1509.5 26.7 all-gather.56
  1586.9 26.6 all-gather.58
  1625.6 31.9 all-reduce.18
  1660.0 28.7 reduce-scatter.38
  1820.8 375.6 all-reduce.20
  (14 shorter events, 371.6 us)
where the time goes:
time: 2250 us; the launch traced here: 2240 us
  waiting for transfers between devices  1350 us (60%)
  matrix products  463 us (21%)
  other arithmetic  188 us (8%)
  local copies, waits for them, and re-layouts  126 us (6%)
  blocking collectives  68.7 us (3%)
  starting transfers between devices  23.4 us (1%)
    all_gather x20, waiting for transfers between devices, gather_rows(): return lax.all_gather(own_rows, 'tensor', axis=0, tiled=True)  474 us
    reduce_scatter x20, waiting for transfers between devices, sum_rows(): lax.psum_scatter(term_fn(jnp.int32(0), own_count * lax.axis_size('tensor'...  469 us
    psum x1, waiting for transfers between devices, on_device(): lax.psum(for_sending(sharded_total), 'dp')  286 us
    psum x5, waiting for transfers between devices, on_device(): lax.psum(block_pairs.astype(jnp.bfloat16), 'tensor').astype(jnp.float32)  72.2 us
    dot_general x5, matrix products, on_device(): jnp.einsum('rsf,rsd->fd', active, grad_mlp, preferred_element_type=f32)  67.2 us
    dot_general x5, matrix products, on_device(): jnp.einsum('rsd,rsf->df', normed_two, grad_pre, preferred_element_type=f32)  66.3 us
    psum x1, blocking collectives, on_device(): common_total = lax.psum(common_total, ('tensor', 'dp'))  58 us
    ppermute x8, waiting for transfers between devices, from_behind(): return lax.ppermute(block, axis, route)  46.9 us
  transfers between devices with their start and end apart: 54, of which 51 were waited for; matrix products, arithmetic and copies ran while one was open for 16% of the time, Pallas kernels for 0%

commit v1 on v0

v1 whole, which is shorter than its diff:
```python
import math

import jax
import jax.numpy as jnp
from jax import lax
from jax.sharding import PartitionSpec as P

HD = 128
F32 = jnp.float32
BF16 = jnp.bfloat16


def from_behind(block, axis, distance):
    devices = range(lax.axis_size(axis))
    route = [(i - distance, i) for i in devices if i - distance in devices]
    return lax.ppermute(block, axis, route)


def layer_norm(values, gain_vec, bias_vec):
    row_mean = jnp.mean(values, axis=-1, keepdims=True)
    centred = values - row_mean
    row_var = jnp.mean(centred * centred, axis=-1, keepdims=True)
    return centred * lax.rsqrt(row_var + 1e-05) * gain_vec + bias_vec


def gelu_tanh(values):
    return jax.nn.gelu(values, approximate=True)


def dot(a, b):
    return jnp.dot(a, b, preferred_element_type=F32)


def dot_t(a, b):
    return lax.dot_general(a, b, (((1,), (1,)), ((), ())), preferred_element_type=F32)


def t_dot(a, b):
    return lax.dot_general(a, b, (((0,), (0,)), ((), ())), preferred_element_type=F32)


def gather_rows(own_rows):
    return lax.all_gather(own_rows, "tensor", axis=0, tiled=True)


def sum_rows(partial):
    return lax.psum_scatter(
        partial.astype(BF16), "tensor", scatter_dimension=0, tiled=True
    ).astype(F32)


def swap(value, distance):
    size = lax.axis_size("dp")
    return lax.ppermute(value, "dp", [(i, i ^ distance) for i in range(size)])


def fold(value, distance, axis):
    bit = (lax.axis_index("dp") // distance) % 2
    half = value.shape[axis] // 2
    away = lax.dynamic_slice_in_dim(value, (1 - bit) * half, half, axis)
    kept = lax.dynamic_slice_in_dim(value, bit * half, half, axis)
    return kept + swap(away.astype(BF16), distance).astype(F32)


def unfold(value, distance, axis):
    bit = (lax.axis_index("dp") // distance) % 2
    other = swap(value, distance)
    low = jnp.where(bit == 0, value, other)
    high = jnp.where(bit == 0, other, value)
    return jnp.concatenate([low, high], axis=axis)


def sum_dp(value, axis, scatter=None):
    size = lax.axis_size("dp")
    distance = 1
    while distance < size:
        value = fold(value, distance, axis)
        if distance == 1 and scatter is not None:
            value = lax.psum_scatter(
                value.astype(BF16), "tensor", scatter_dimension=scatter, tiled=True
            ).astype(F32)
        distance *= 2
    value = value.astype(BF16)
    while distance > 1:
        distance //= 2
        value = unfold(value, distance, axis)
    return value.astype(F32)


def whole_weight(shard, split, join):
    size = lax.axis_size("dp")
    part = shard.shape[split] // size
    own = lax.dynamic_slice_in_dim(shard, lax.axis_index("dp") * part, part, split)
    own = lax.all_gather(own, "tensor", axis=join, tiled=True)
    return lax.all_gather(own, "dp", axis=split, tiled=True)


def on_device(
    tokens_in,
    cotangent,
    ln1_gain,
    ln1_bias,
    q_weight,
    q_bias,
    kv_weight,
    v_bias,
    o_weight,
    o_bias,
    ln2_gain,
    ln2_bias,
    up_weight,
    up_bias,
    down_weight,
    down_bias,
):
    section = lax.axis_index("section")
    tensor_count = lax.axis_size("tensor")
    tensor_rank = lax.axis_index("tensor")
    gain_one = ln1_gain[0].astype(F32)
    bias_one = ln1_bias[0].astype(F32)
    w_pairs = kv_weight[0]
    pair_bias = jnp.concatenate([jnp.zeros((HD,), F32), v_bias[0].astype(F32)])
    b_out = o_bias[0].astype(F32)
    gain_two = ln2_gain[0].astype(F32)
    bias_two = ln2_bias[0].astype(F32)
    w_up = up_weight[0]
    b_up = up_bias[0].astype(F32)
    w_down = down_weight[0]
    b_down = down_bias[0].astype(F32)
    blocks, own_count, seq_count, model_dim = tokens_in.shape
    assert seq_count == 1
    tokens_in = tokens_in[:, :, 0]
    cotangent = cotangent[:, :, 0]
    block_len = own_count * tensor_count
    total_len = blocks * block_len
    w_query = whole_weight(q_weight[0], 0, 1)
    w_out = whole_weight(o_weight[0], 1, 0)
    b_query = lax.all_gather(q_bias[0], "tensor", axis=0, tiled=True).astype(F32)
    heads = w_query.shape[1] // HD
    width = heads * HD
    ff_local = w_up.shape[1]
    score_scale = 1.0 / math.sqrt(HD)
    positions = jnp.arange(total_len, dtype=jnp.int32)

    def zeros(shape, dtype):
        return jnp.zeros(shape, dtype)

    kept_normed = zeros((blocks, own_count, model_dim), BF16)
    kept_query = zeros((blocks, own_count, width), BF16)
    kept_attended = zeros((blocks, own_count, width), BF16)
    kept_logsum = zeros((blocks, own_count * heads), F32)
    kv_cache = zeros((total_len, 2 * HD), BF16)
    kept_input = zeros((blocks, own_count, model_dim), F32)
    kept_hidden = zeros((blocks, own_count, model_dim), F32)
    kept_normed_two = zeros((blocks, block_len, model_dim), BF16)
    kept_pre = zeros((blocks, block_len, ff_local), F32)
    kept_active = zeros((blocks, block_len, ff_local), BF16)
    outputs = zeros((blocks, own_count, model_dim), BF16)
    received = zeros((own_count, model_dim), F32)

    def put(kept, value, index):
        return lax.dynamic_update_index_in_dim(kept, value, index, 0)

    def take(kept, index):
        return lax.dynamic_index_in_dim(kept, index, 0, keepdims=False)

    for turn in range(blocks + 1):
        block_index = jnp.clip(turn - section, 0, blocks - 1)
        layer_input = jnp.where(section == 0, take(tokens_in, block_index).astype(F32), received)
        normed = layer_norm(layer_input, gain_one, bias_one).astype(BF16)
        pairs = gather_rows((dot(normed, w_pairs) + pair_bias).astype(BF16))
        kv_cache = lax.dynamic_update_slice_in_dim(kv_cache, pairs, block_index * block_len, 0)
        query = (dot(normed, w_query) + b_query).astype(BF16)
        visible = positions < (block_index + 1) * block_len
        query_rows = query.reshape(own_count * heads, HD)
        scores = dot_t(query_rows, kv_cache[:, :HD]) * score_scale
        scores = jnp.where(visible, scores, -1e30)
        row_top = jnp.max(scores, axis=-1, keepdims=True)
        exponent = jnp.exp(scores - row_top)
        row_total = jnp.sum(exponent, axis=-1, keepdims=True)
        log_total = (row_top + jnp.log(row_total))[:, 0]
        weights_low = (exponent / row_total).astype(BF16)
        attended = dot(weights_low, kv_cache[:, HD:]).astype(BF16).reshape(own_count, width)
        hidden = layer_input + dot(attended, w_out) + b_out
        normed_two = gather_rows(layer_norm(hidden, gain_two, bias_two).astype(BF16))
        pre_active = dot(normed_two, w_up) + b_up
        active = gelu_tanh(pre_active).astype(BF16)
        result_low = (hidden + sum_rows(dot(active, w_down)) + b_down).astype(BF16)
        kept_normed = put(kept_normed, normed, block_index)
        kept_query = put(kept_query, query, block_index)
        kept_attended = put(kept_attended, attended, block_index)
        kept_logsum = put(kept_logsum, log_total, block_index)
        kept_input = put(kept_input, layer_input, block_index)
        kept_hidden = put(kept_hidden, hidden, block_index)
        kept_normed_two = put(kept_normed_two, normed_two, block_index)
        kept_pre = put(kept_pre, pre_active, block_index)
        kept_active = put(kept_active, active, block_index)
        outputs = put(outputs, result_low, block_index)
        if turn < blocks:
            received = from_behind(result_low, "section", 1).astype(F32)

    key_rows = kv_cache[:, :HD]
    value_rows = kv_cache[:, HD:]
    kept_grad_mlp = zeros((blocks + 1, block_len, model_dim), BF16)
    kept_grad_pre = zeros((blocks + 1, block_len, ff_local), BF16)
    kept_branch = zeros((blocks + 1, own_count, model_dim), BF16)
    kept_grad_query = zeros((blocks + 1, own_count, width), BF16)
    kept_grad_pairs = zeros((blocks + 1, own_count, 2 * HD), BF16)
    input_grads = zeros((blocks + 1, own_count, model_dim), F32)
    pair_grad_acc = zeros((total_len, 2 * HD), F32)
    received_back = zeros((own_count, model_dim), F32)
    common = [zeros((model_dim,), F32) for _ in range(6)]
    for turn in range(blocks + 1):
        step_count = turn - (1 - section)
        valid = (step_count >= 0) & (step_count < blocks)
        block_index = blocks - 1 - jnp.clip(step_count, 0, blocks - 1)
        slot = jnp.where(valid, block_index, blocks)
        grad_out = jnp.where(section == 1, take(cotangent, block_index).astype(F32), received_back)
        grad_out = grad_out * valid.astype(F32)
        pre_active = take(kept_pre, block_index)
        grad_mlp = gather_rows(grad_out.astype(BF16))
        grad_active = dot_t(grad_mlp, w_down)
        grad_pre = jax.vjp(gelu_tanh, pre_active)[1](grad_active)[0].astype(BF16)
        grad_normed_two = sum_rows(dot_t(grad_pre, w_up))
        norm_back_two = jax.vjp(layer_norm, take(kept_hidden, block_index), gain_two, bias_two)[1]
        grad_hidden_norm, gain_two_term, bias_two_term = norm_back_two(grad_normed_two)
        grad_hidden = grad_out + grad_hidden_norm
        branch = grad_hidden.astype(BF16)
        grad_attended = dot_t(branch, w_out).astype(BF16).reshape(own_count * heads, HD)
        query_rows = take(kept_query, block_index).reshape(own_count * heads, HD)
        log_total = take(kept_logsum, block_index)
        visible = positions < (block_index + 1) * block_len
        scores = dot_t(query_rows, key_rows) * score_scale
        scores = jnp.where(visible, scores, -1e30)
        probabilities = jnp.exp(scores - log_total[:, None])
        grad_probs = dot_t(grad_attended, value_rows)
        row_inner = jnp.sum(probabilities * grad_probs, axis=-1, keepdims=True)
        grad_scores = (probabilities * (grad_probs - row_inner)).astype(BF16)
        grad_query = (dot(grad_scores, key_rows) * score_scale).astype(BF16)
        grad_query = grad_query.reshape(own_count, width)
        grad_keys = t_dot(grad_scores, query_rows) * score_scale
        grad_values = t_dot(probabilities.astype(BF16), grad_attended)
        pair_grad_acc = pair_grad_acc + jnp.concatenate([grad_keys, grad_values], axis=-1)
        block_pairs = lax.dynamic_slice_in_dim(pair_grad_acc, block_index * block_len, block_len, 0)
        grad_pairs = sum_rows(block_pairs).astype(BF16)
        grad_normed = dot_t(grad_query, w_query) + dot_t(grad_pairs, w_pairs)
        norm_back_one = jax.vjp(layer_norm, take(kept_input, block_index), gain_one, bias_one)[1]
        grad_input_norm, gain_one_term, bias_one_term = norm_back_one(grad_normed)
        grad_input = grad_hidden + grad_input_norm
        if turn < blocks:
            received_back = from_behind(grad_input.astype(BF16), "section", -1).astype(F32)
        scale = valid.astype(F32)
        terms = (
            gain_one_term * scale,
            bias_one_term * scale,
            jnp.sum(grad_hidden, axis=0),
            gain_two_term,
            bias_two_term,
            jnp.sum(grad_out, axis=0),
        )
        common = [total + term for total, term in zip(common, terms)]
        input_grads = put(input_grads, grad_input, slot)
        kept_grad_mlp = put(kept_grad_mlp, grad_mlp, slot)
        kept_grad_pre = put(kept_grad_pre, grad_pre, slot)
        kept_branch = put(kept_branch, branch, slot)
        kept_grad_query = put(kept_grad_query, grad_query, slot)
        kept_grad_pairs = put(kept_grad_pairs, grad_pairs, slot)

    def flat(kept):
        return kept[:blocks].reshape(-1, kept.shape[-1])

    down_w = t_dot(flat(kept_active), flat(kept_grad_mlp))
    up_w = t_dot(flat(kept_normed_two), flat(kept_grad_pre))
    up_b = jnp.sum(flat(kept_grad_pre).astype(F32), axis=0)
    out_w = t_dot(flat(kept_attended), flat(kept_branch))
    query_w = t_dot(flat(kept_normed), flat(kept_grad_query))
    query_b = jnp.sum(flat(kept_grad_query).astype(F32), axis=0)
    pair_w = t_dot(flat(kept_normed), flat(kept_grad_pairs))
    value_b = jnp.sum(flat(kept_grad_pairs)[:, HD:].astype(F32), axis=0)
    down_w = sum_dp(down_w, 0)
    up_w = sum_dp(up_w, 0)
    out_w = sum_dp(out_w, 1, 0)
    query_w = sum_dp(query_w, 0, 1)
    pair_w = lax.psum(pair_w.astype(BF16), ("tensor", "dp")).astype(F32)
    wide = jnp.zeros((tensor_count, ff_local), F32)
    wide = lax.dynamic_update_index_in_dim(wide, up_b, tensor_rank, 0)
    packed = jnp.concatenate([*common, query_b, value_b, wide.reshape(-1)])
    packed = lax.psum(packed, ("tensor", "dp"))
    vecs = packed[: 6 * model_dim].reshape(6, model_dim)
    own_query = lax.dynamic_slice_in_dim(
        packed, 6 * model_dim + tensor_rank * (width // tensor_count), width // tensor_count, 0
    )
    value_b = lax.slice_in_dim(packed, 6 * model_dim + width, 6 * model_dim + width + HD)
    own_up = lax.dynamic_slice_in_dim(
        packed, 6 * model_dim + width + HD + tensor_rank * ff_local, ff_local, 0
    )
    return (
        outputs[None, :, :, None],
        input_grads[None, :blocks, :, None],
        vecs[0][None],
        vecs[1][None],
        query_w[None],
        own_query[None],
        pair_w[None],
        value_b[None],
        out_w[None],
        vecs[2][None],
        vecs[3][None],
        vecs[4][None],
        up_w[None],
        own_up[None],
        down_w[None],
        vecs[5][None],
    )


def solution(mesh):
    placed = (
        P(None, "tensor", "dp", None),
        P(None, "tensor", "dp", None),
        P("section", None),
        P("section", None),
        P("section", None, "tensor"),
        P("section", "tensor"),
        P("section", None, None),
        P("section", None),
        P("section", "tensor", None),
        P("section", None),
        P("section", None),
        P("section", None),
        P("section", None, "tensor"),
        P("section", "tensor"),
        P("section", "tensor", None),
        P("section", None),
    )
    return jax.shard_map(
        on_device,
        mesh=mesh,
        in_specs=placed,
        out_specs=(
            P("section", None, "tensor", "dp", None),
            P("section", None, "tensor", "dp", None),
            P("section", None),
            P("section", None),
            P("section", None, "tensor"),
            P("section", "tensor"),
            P("section", None, None),
            P("section", None),
            P("section", "tensor", None),
            P("section", None),
            P("section", None),
            P("section", None),
            P("section", None, "tensor"),
            P("section", "tensor"),
            P("section", "tensor", None),
            P("section", None),
        ),
        check_vma=False,
    )
```

time: 2250 us -> 1820 us (0.81)
  waiting for transfers between devices: 1350 us -> 880 us
  matrix products: 463 us -> 387 us
  local copies, waits for them, and re-layouts: 126 us -> 197 us
  other arithmetic: 188 us -> 224 us
    psum x6 -> x2, waiting for transfers between devices: 358 us -> 0.01 us  [the longest x1 0.01 us: on_device(): packed = lax.psum(packed, ('tensor', 'dp'))]
    all_gather x20 -> x10, waiting for transfers between devices: 474 us -> 222 us  [gather_rows(): return lax.all_gather(own_rows, 'tensor', axis=0, tiled=True)]
    reduce_scatter x20 -> x17, waiting for transfers between devices: 469 us -> 273 us  [the longest x15 205 us: sum_rows(): lax.psum_scatter(partial.astype(BF16), 'tensor', scatter_dimension=0, til...]
    all_gather x0 -> x4, waiting for transfers between devices: none -> 180 us  [the longest x2 93.4 us: whole_weight(): own = lax.all_gather(own, 'tensor', axis=join, tiled=True)]
    ppermute x0 -> x16, waiting for transfers between devices: none -> 162 us  [swap(): return lax.ppermute(value, 'dp', [(i, i ^ distance) for i in range(size)])]
    dot_general x110 -> x90, matrix products: 463 us -> 387 us  [the longest x40 185 us: dot_t(): lax.dot_general(a, b, (((1,), (1,)), ((), ())), preferred_element_type=F32)]
    psum x2 -> x0, blocking collectives: 68.7 us -> none  [the longest x1 58 us: on_device(): common_total = lax.psum(common_total, ('tensor', 'dp'))]
    all_gather x0 -> x6, blocking collectives: none -> 64.5 us  [the longest x5 55.3 us: gather_rows(): return lax.all_gather(own_rows, 'tensor', axis=0, tiled=True)]
  transfers between devices with their start and end apart: 54 -> 57, of which waited for: 51 -> 42; matrix products, arithmetic and copies ran while one was open for 16% -> 22% of each run, Pallas kernels for 0% -> 0%
where the time goes in v1:
time: 1820 us; the launch traced here: 1810 us
  waiting for transfers between devices  880 us (48%)
  matrix products  387 us (21%)
  other arithmetic  224 us (12%)
  local copies, waits for them, and re-layouts  197 us (11%)
  blocking collectives  64.5 us (4%)
  starting transfers between devices  38.8 us (2%)
    all_gather x10, waiting for transfers between devices, gather_rows(): return lax.all_gather(own_rows, 'tensor', axis=0, tiled=True)  222 us
    reduce_scatter x15, waiting for transfers between devices, sum_rows(): lax.psum_scatter(partial.astype(BF16), 'tensor', scatter_dimension=0, til...  205 us
    dot_general x40, matrix products, dot_t(): lax.dot_general(a, b, (((1,), (1,)), ((), ())), preferred_element_type=F32)  185 us
    ppermute x16, waiting for transfers between devices, swap(): return lax.ppermute(value, 'dp', [(i, i ^ distance) for i in range(size)])  162 us
    dot_general x35, matrix products, dot(): return jnp.dot(a, b, preferred_element_type=F32)  141 us
    all_gather x2, waiting for transfers between devices, whole_weight(): own = lax.all_gather(own, 'tensor', axis=join, tiled=True)  93.4 us
    all_gather x2, waiting for transfers between devices, whole_weight(): return lax.all_gather(own, 'dp', axis=split, tiled=True)  86.6 us
    reduce_scatter x2, waiting for transfers between devices, sum_dp(): lax.psum_scatter(value.astype(BF16), 'tensor', scatter_dimension=scatter,...  68 us
  transfers between devices with their start and end apart: 57, of which 42 were waited for; matrix products, arithmetic and copies ran while one was open for 22% of the time, Pallas kernels for 0%

profile of v1, /device:TPU:1, one launch (start us, length us, event | category | flops | bytes accessed | tf_op | source)
XLA Modules:
  0.0 1809.0 jit_solution(15878004784130863771)
XLA Ops:
  11.7 46.6 %all-gather.40.cloned.1.call-done = bf16[1,512,2048]{2,1,0:T(8,128)(2,1)} async-done(((bf16[1,512,512]{2,1,0:T(8,128)(2,1)}), bf16[1,512,2048]{2,1,0:T(8,128)(2,1)}) %all-gather.40.cloned.1.call-update) | async-done | bytes 2097168 | tf_op jit(solution)/shard_map/all_gather | solution.py:94
  58.3 46.8 %all-gather.44.cloned.1.call-done = bf16[1,2048,512]{2,1,0:T(8,128)(2,1)} async-done(((bf16[1,512,512]{2,1,0:T(8,128)(2,1)}), bf16[1,2048,512]{2,1,0:T(8,128)(2,1)}) %all-gather.44.cloned.1.call-update) | async-done | bytes 2097168 | tf_op jit(solution)/shard_map/all_gather | solution.py:94
  115.5 11.1 all_gather.63
  126.7 37.5 %all-gather.42.cloned.1.call-done = bf16[1,2048,2048]{2,1,0:T(8,128)(2,1)} async-done(((bf16[1,512,2048]{2,1,0:T(8,128)(2,1)}), bf16[1,2048,2048]{2,1,0:T(8,128)(2,1)}) %all-gather.42.cloned.1.call-update) | async-done | bytes 8388624 | tf_op jit(solution)/shard_map/all_gather | solution.py:95
  174.8 49.1 %all-gather.46.cloned.1.call-done = bf16[1,2048,2048]{2,1,0:T(8,128)(2,1)} async-done(((bf16[1,2048,512]{2,1,0:T(8,128)(2,1)}), bf16[1,2048,2048]{2,1,0:T(8,128)(2,1)}) %all-gather.46.cloned.1.call-update) | async-done | bytes 8388624 | tf_op jit(solution)/shard_map/all_gather | solution.py:95
  230.4 27.2 %all-gather.20.cloned.1.call-done = bf16[256,2048]{1,0:T(8,128)(2,1)} async-done(((bf16[64,2048]{1,0:T(8,128)(2,1)}), bf16[256,2048]{1,0:T(8,128)(2,1)}) %all-gather.20.cloned.1.call-update) | async-done | bytes 1048592 | tf_op jit(solution)/shard_map/all_gather | solution.py:43
  274.3 26.7 %reduce-scatter.18.cloned.1.call-done = bf16[64,2048]{1,0:T(8,128)(2,1)} async-done(((bf16[256,2048]{1,0:T(8,128)(2,1)}), bf16[64,2048]{1,0:T(8,128)(2,1)}) %reduce-scatter.18.cloned.1.call-update) | async-done | bytes 262160 | tf_op jit(solution)/shard_map/reduce_scatter | solution.py:47
  312.8 11.2 all_gather.67
  342.7 30.8 %all-gather.22.cloned.1.call-done = bf16[256,2048]{1,0:T(8,128)(2,1)} async-done(((bf16[64,2048]{1,0:T(8,128)(2,1)}), bf16[256,2048]{1,0:T(8,128)(2,1)}) %all-gather.22.cloned.1.call-update) | async-done | bytes 1048592 | tf_op jit(solution)/shard_map/all_gather | solution.py:43
  389.1 26.7 %reduce-scatter.20.cloned.1.call-done = bf16[64,2048]{1,0:T(8,128)(2,1)} async-done(((bf16[256,2048]{1,0:T(8,128)(2,1)}), bf16[64,2048]{1,0:T(8,128)(2,1)}) %reduce-scatter.20.cloned.1.call-update) | async-done | bytes 262160 | tf_op jit(solution)/shard_map/reduce_scatter | solution.py:47
  426.6 11.2 all_gather.69
  456.2 31.1 %all-gather.24.cloned.1.call-done = bf16[256,2048]{1,0:T(8,128)(2,1)} async-done(((bf16[64,2048]{1,0:T(8,128)(2,1)}), bf16[256,2048]{1,0:T(8,128)(2,1)}) %all-gather.24.cloned.1.call-update) | async-done | bytes 1048592 | tf_op jit(solution)/shard_map/all_gather | solution.py:43
  502.9 26.7 %reduce-scatter.22.cloned.1.call-done = bf16[64,2048]{1,0:T(8,128)(2,1)} async-done(((bf16[256,2048]{1,0:T(8,128)(2,1)}), bf16[64,2048]{1,0:T(8,128)(2,1)}) %reduce-scatter.22.cloned.1.call-update) | async-done | bytes 262160 | tf_op jit(solution)/shard_map/reduce_scatter | solution.py:47
  540.4 11.2 all_gather.71
  570.0 31.0 %all-gather.26.cloned.1.call-done = bf16[256,2048]{1,0:T(8,128)(2,1)} async-done(((bf16[64,2048]{1,0:T(8,128)(2,1)}), bf16[256,2048]{1,0:T(8,128)(2,1)}) %all-gather.26.cloned.1.call-update) | async-done | bytes 1048592 | tf_op jit(solution)/shard_map/all_gather | solution.py:43
  616.7 26.7 %reduce-scatter.24.cloned.1.call-done = bf16[64,2048]{1,0:T(8,128)(2,1)} async-done(((bf16[256,2048]{1,0:T(8,128)(2,1)}), bf16[64,2048]{1,0:T(8,128)(2,1)}) %reduce-scatter.24.cloned.1.call-update) | async-done | bytes 262160 | tf_op jit(solution)/shard_map/reduce_scatter | solution.py:47
  654.3 10.5 all_gather.73
  719.9 20.8 %all-gather.30.cloned.1.call-done = bf16[256,2048]{1,0:T(8,128)(2,1)} async-done(((bf16[64,2048]{1,0:T(8,128)(2,1)}), bf16[256,2048]{1,0:T(8,128)(2,1)}) %all-gather.30.cloned.1.call-update) | async-done | bytes 1048592 | tf_op jit(solution)/shard_map/all_gather | solution.py:43
  762.3 20.4 %reduce-scatter.28.cloned.1.call-done = bf16[64,2048]{1,0:T(8,128)(2,1)} async-done(((bf16[256,2048]{1,0:T(8,128)(2,1)}), bf16[64,2048]{1,0:T(8,128)(2,1)}) %reduce-scatter.28.cloned.1.call-update) | async-done | bytes 262160 | tf_op jit(solution)/shard_map/reduce_scatter | solution.py:47
  840.3 28.2 %all-gather.32.cloned.1.call-done = bf16[256,2048]{1,0:T(8,128)(2,1)} async-done(((bf16[64,2048]{1,0:T(8,128)(2,1)}), bf16[256,2048]{1,0:T(8,128)(2,1)}) %all-gather.32.cloned.1.call-update) | async-done | bytes 1048592 | tf_op jit(solution)/shard_map/all_gather | solution.py:43
  889.5 21.2 %reduce-scatter.32.cloned.1.call-done = bf16[64,2048]{1,0:T(8,128)(2,1)} async-done(((bf16[256,2048]{1,0:T(8,128)(2,1)}), bf16[64,2048]{1,0:T(8,128)(2,1)}) %reduce-scatter.32.cloned.1.call-update) | async-done | bytes 262160 | tf_op jit(solution)/shard_map/reduce_scatter | solution.py:47
  967.2 28.4 %all-gather.34.cloned.1.call-done = bf16[256,2048]{1,0:T(8,128)(2,1)} async-done(((bf16[64,2048]{1,0:T(8,128)(2,1)}), bf16[256,2048]{1,0:T(8,128)(2,1)}) %all-gather.34.cloned.1.call-update) | async-done | bytes 1048592 | tf_op jit(solution)/shard_map/all_gather | solution.py:43
  1016.6 21.2 %reduce-scatter.36.cloned.1.call-done = bf16[64,2048]{1,0:T(8,128)(2,1)} async-done(((bf16[256,2048]{1,0:T(8,128)(2,1)}), bf16[64,2048]{1,0:T(8,128)(2,1)}) %reduce-scatter.36.cloned.1.call-update) | async-done | bytes 262160 | tf_op jit(solution)/shard_map/reduce_scatter | solution.py:47
  1347.3 18.3 %convolution_bitcast_fusion = f32[2048,2048]{1,0:T(8,128)} fusion(bf16[4,256,2048]{1,2,0:T(8,128)(2,1)} %get-tuple-element.221, bf16[5,256,2048]{2,1,0:T(8,128)(2,1)} %bitcast_dynamic-update-slice_fusion.5), kind=kOutput, calls=%fused_computation | convolution fusion | flops 8589934592 | bytes 25165824 | tf_op jit(solution)/shard_map/dot_general | solution.py:39
  1406.9 12.6 convolution_bitcast_fusion.1
  1464.0 41.4 %collective-permute-done.21 = bf16[512,2048]{1,0:T(8,128)(2,1)} collective-permute-done((bf16[512,2048]{1,0:T(8,128)(2,1)}, bf16[512,2048]{1,0:T(8,128)(2,1)}, u32[]{:S(2)}, u32[]{:S(2)}) %collective-permute-start.21) | collective-permute-done | bytes 2097184 | tf_op jit(solution)/shard_map/ppermute | solution.py:54
  1522.4 29.8 %collective-permute-done.17 = bf16[512,2048]{1,0:T(8,128)(2,1)} collective-permute-done((bf16[512,2048]{1,0:T(8,128)(2,1)}, bf16[512,2048]{1,0:T(8,128)(2,1)}, u32[]{:S(2)}, u32[]{:S(2)}) %collective-permute-start.17) | collective-permute-done | bytes 2097184 | tf_op jit(solution)/shard_map/ppermute | solution.py:54
  1557.1 43.0 %collective-permute-done.22 = bf16[512,2048]{1,0:T(8,128)(2,1)} collective-permute-done((bf16[512,2048]{1,0:T(8,128)(2,1)}, bf16[512,2048]{1,0:T(8,128)(2,1)}, u32[]{:S(2)}, u32[]{:S(2)}) %collective-permute-start.22) | collective-permute-done | bytes 2097184 | tf_op jit(solution)/shard_map/ppermute | solution.py:54
  1608.0 37.0 %collective-permute-done.18 = bf16[512,2048]{1,0:T(8,128)(2,1)S(1)} collective-permute-done((bf16[512,2048]{1,0:T(8,128)(2,1)S(1)}, bf16[512,2048]{1,0:T(8,128)(2,1)S(1)}, u32[]{:S(2)}, u32[]{:S(2)}) %collective-permute-start.18) | collective-permute-done | bytes 2097184 | tf_op jit(solution)/shard_map/ppermute | solution.py:54
  1669.2 68.0 %reduce-scatter.50.cloned.1.call-done = bf16[512,1024]{1,0:T(8,128)(2,1)} async-done(((bf16[2048,1024]{1,0:T(8,128)(2,1)}), bf16[512,1024]{1,0:T(8,128)(2,1)}) %reduce-scatter.50.cloned.1.call-update) | async-done | bytes 1048592 | tf_op jit(solution)/shard_map/reduce_scatter | solution.py:79
  1740.8 11.8 maximum_convert_fusion.1
  1781.1 11.8 maximum_convert_fusion
  (898 shorter events, 915.1 us)
Async XLA Ops:
  9.6 95.5 %all-gather.44.cloned.1.call-start = ((), (), s32[]{:S(2)}) async-start(), calls=%async_computation.48 | async-start | bytes 2621440 | tf_op jit(solution)/shard_map/all_gather | solution.py:94
  11.7 152.5 %all-gather.42.cloned.1.call-start = ((), (), s32[]{:S(2)}) async-start(), calls=%async_computation.47 | async-start | bytes 10485760 | tf_op jit(solution)/shard_map/all_gather | solution.py:95
  58.3 165.6 %all-gather.46.cloned.1.call-start = ((), (), s32[]{:S(2)}) async-start(), calls=%async_computation.49 | async-start | bytes 10485760 | tf_op jit(solution)/shard_map/all_gather | solution.py:95
  105.2 152.5 %all-gather.20.cloned.1.call-start = ((), (), s32[]{:S(2)}) async-start(), calls=%async_computation.17 | async-start | bytes 1310720 | tf_op jit(solution)/shard_map/all_gather | solution.py:43
  230.1 70.8 %reduce-scatter.18.cloned.1.call-start = ((), (), s32[]{:S(2)}) async-start(), calls=%async_computation.18 | async-start | bytes 1310720 | tf_op jit(solution)/shard_map/reduce_scatter | solution.py:47
  274.2 99.2 %all-gather.22.cloned.1.call-start = ((), (), s32[]{:S(2)}) async-start(), calls=%async_computation.19 | async-start | bytes 1310720 | tf_op jit(solution)/shard_map/all_gather | solution.py:43
  342.2 73.6 %reduce-scatter.20.cloned.1.call-start = ((), (), s32[]{:S(2)}) async-start(), calls=%async_computation.20 | async-start | bytes 1310720 | tf_op jit(solution)/shard_map/reduce_scatter | solution.py:47
  389.0 98.2 %all-gather.24.cloned.1.call-start = ((), (), s32[]{:S(2)}) async-start(), calls=%async_computation.21 | async-start | bytes 1310720 | tf_op jit(solution)/shard_map/all_gather | solution.py:43
  456.0 73.7 %reduce-scatter.22.cloned.1.call-start = ((), (), s32[]{:S(2)}) async-start(), calls=%async_computation.22 | async-start | bytes 1310720 | tf_op jit(solution)/shard_map/reduce_scatter | solution.py:47
  502.9 98.2 %all-gather.26.cloned.1.call-start = ((), (), s32[]{:S(2)}) async-start(), calls=%async_computation.23 | async-start | bytes 1310720 | tf_op jit(solution)/shard_map/all_gather | solution.py:43
  569.8 73.7 %reduce-scatter.24.cloned.1.call-start = ((), (), s32[]{:S(2)}) async-start(), calls=%async_computation.24 | async-start | bytes 1310720 | tf_op jit(solution)/shard_map/reduce_scatter | solution.py:47
  616.7 95.2 %all-gather.28.cloned.1.call-start = ((), (), s32[]{:S(2)}) async-start(), calls=%async_computation.25 | async-start | bytes 1310720 | tf_op jit(solution)/shard_map/all_gather | solution.py:43
  683.0 99.7 %reduce-scatter.28.cloned.1.call-start = ((), (), s32[]{:S(2)}) async-start(), calls=%async_computation.28 | async-start | bytes 1310720 | tf_op jit(solution)/shard_map/reduce_scatter | solution.py:47
  839.8 70.8 %reduce-scatter.32.cloned.1.call-start = ((), (), s32[]{:S(2)}) async-start(), calls=%async_computation.31 | async-start | bytes 1310720 | tf_op jit(solution)/shard_map/reduce_scatter | solution.py:47
  883.9 68.3 %reduce-scatter.34.cloned.1.call-start = ((), (), s32[]{:S(2)}) async-start(), calls=%async_computation.32 | async-start | bytes 163840 | tf_op jit(solution)/shard_map/reduce_scatter | solution.py:47
  967.0 70.8 %reduce-scatter.36.cloned.1.call-start = ((), (), s32[]{:S(2)}) async-start(), calls=%async_computation.34 | async-start | bytes 1310720 | tf_op jit(solution)/shard_map/reduce_scatter | solution.py:47
  1011.0 68.3 %reduce-scatter.38.cloned.1.call-start = ((), (), s32[]{:S(2)}) async-start(), calls=%async_computation.35 | async-start | bytes 163840 | tf_op jit(solution)/shard_map/reduce_scatter | solution.py:47
  1094.1 70.8 %reduce-scatter.40.cloned.1.call-start = ((), (), s32[]{:S(2)}) async-start(), calls=%async_computation.37 | async-start | bytes 1310720 | tf_op jit(solution)/shard_map/reduce_scatter | solution.py:47
  1138.1 68.3 %reduce-scatter.42.cloned.1.call-start = ((), (), s32[]{:S(2)}) async-start(), calls=%async_computation.38 | async-start | bytes 163840 | tf_op jit(solution)/shard_map/reduce_scatter | solution.py:47
  1221.3 70.8 %reduce-scatter.44.cloned.1.call-start = ((), (), s32[]{:S(2)}) async-start(), calls=%async_computation.40 | async-start | bytes 1310720 | tf_op jit(solution)/shard_map/reduce_scatter | solution.py:47
  1265.4 118.9 %reduce-scatter.46.cloned.1.call-start = ((), (), s32[]{:S(2)}) async-start(), calls=%async_computation.41 | async-start | bytes 163840 | tf_op jit(solution)/shard_map/reduce_scatter | solution.py:47
  1314.2 205.5 %reduce-scatter.26.cloned.1.call-start = ((), (), s32[]{:S(2)}) async-start(), calls=%async_computation.26 | async-start | bytes 1310720 | tf_op jit(solution)/shard_map/reduce_scatter | solution.py:47
  1321.3 331.7 %all-reduce.4.cloned.1.call-start = ((), (), s32[]{:S(2)}) async-start(), calls=%async_computation.42 | async-start | bytes 188416 | tf_op jit(solution)/shard_map/psum | solution.py:288
  1374.7 69.2 %collective-permute-start.20 = (bf16[1024,2048]{1,0:T(8,128)(2,1)}, bf16[1024,2048]{1,0:T(8,128)(2,1)}, u32[]{:S(2)}, u32[]{:S(2)}) collective-permute-start(bf16[1024,2048]{1,0:T(8,128)(2,1)} %dynamic-slice_convert_fusion), channel_id=1, source_target_pairs={{0,1},{1,0},{2,3},{3,2},{4,5},{5,4},{6,7},{7,6},{8,9},{9,8},{10,11... | collective-permute-start | bytes 12582920 | tf_op jit(solution)/shard_map/ppermute | solution.py:54
  1395.6 261.4 %all-reduce.6.cloned.1.call-start = ((), (), s32[]{:S(2)}) async-start(), calls=%async_computation.44 | async-start | bytes 2097152 | tf_op jit(solution)/shard_map/psum | solution.py:284
  1398.3 267.7 %reduce-scatter.48.cloned.1.call-start = ((), (), s32[]{:S(2)}) async-start(), calls=%async_computation.43 | async-start | bytes 5242880 | tf_op jit(solution)/shard_map/reduce_scatter | solution.py:79
  1406.8 330.3 %reduce-scatter.50.cloned.1.call-start = ((), (), s32[]{:S(2)}) async-start(), calls=%async_computation.45 | async-start | bytes 5242880 | tf_op jit(solution)/shard_map/reduce_scatter | solution.py:79
  1463.7 88.6 %collective-permute-start.17 = (bf16[512,2048]{1,0:T(8,128)(2,1)}, bf16[512,2048]{1,0:T(8,128)(2,1)}, u32[]{:S(2)}, u32[]{:S(2)}) collective-permute-start(bf16[512,2048]{1,0:T(8,128)(2,1)} %dynamic-slice_convert_fusion.5), channel_id=1, source_target_pairs={{0,2},{1,3},{2,0},{3,1},{4,6},{5,7},{6,4},{7,5},{8,10},{9,11},{10,... | collective-permute-start | bytes 6291464 | tf_op jit(solution)/shard_map/ppermute | solution.py:54
  1510.3 89.7 %collective-permute-start.22 = (bf16[512,2048]{1,0:T(8,128)(2,1)}, bf16[512,2048]{1,0:T(8,128)(2,1)}, u32[]{:S(2)}, u32[]{:S(2)}) collective-permute-start(bf16[512,2048]{1,0:T(8,128)(2,1)} %add_convert_fusion.2), channel_id=1, source_target_pairs={{0,2},{1,3},{2,0},{3,1},{4,6},{5,7},{6,4},{7,5},{8,10},{9,11},{10,... | collective-permute-start | bytes 6291464 | tf_op jit(solution)/shard_map/ppermute | solution.py:54
  1555.9 89.1 %collective-permute-start.18 = (bf16[512,2048]{1,0:T(8,128)(2,1)S(1)}, bf16[512,2048]{1,0:T(8,128)(2,1)S(1)}, u32[]{:S(2)}, u32[]{:S(2)}) collective-permute-start(bf16[512,2048]{1,0:T(8,128)(2,1)S(1)} %add_convert_fusion.3), channel_id=1, source_target_pairs={{0,2},{1,3},{2,0},{3,1},{4,6},{5,7},{6,4},{7,5},{8,10},{9,11},{10,... | collective-permute-start | bytes 6291464 | tf_op jit(solution)/shard_map/ppermute | solution.py:54
  1648.8 108.6 %collective-permute-start.19 = (bf16[1024,2048]{1,0:T(8,128)(2,1)}, bf16[1024,2048]{1,0:T(8,128)(2,1)}, u32[]{:S(2)}, u32[]{:S(2)}) collective-permute-start(bf16[1024,2048]{1,0:T(8,128)(2,1)} %pad_maximum_fusion), channel_id=1, source_target_pairs={{0,1},{1,0},{2,3},{3,2},{4,5},{5,4},{6,7},{7,6},{8,9},{9,8},{10,11... | collective-permute-start | bytes 12582920 | tf_op jit(solution)/shard_map/ppermute | solution.py:54
  1667.9 84.7 %collective-permute-start.9 = (bf16[512,512]{1,0:T(8,128)(2,1)S(1)}, bf16[512,512]{1,0:T(8,128)(2,1)S(1)}, u32[]{:S(2)}, u32[]{:S(2)}) collective-permute-start(bf16[512,512]{1,0:T(8,128)(2,1)S(1)} %dynamic-slice_convert_fusion.7), channel_id=1, source_target_pairs={{0,2},{1,3},{2,0},{3,1},{4,6},{5,7},{6,4},{7,5},{8,10},{9,11},{10,... | collective-permute-start | bytes 1572872 | tf_op jit(solution)/shard_map/ppermute | solution.py:54
  (198 other events, 3786.8 us)
Sparse Core Ops, SparseCore 0:
  10.3 47.9 all-gather.39
  60.4 44.6 all-gather.43
  106.7 57.4 all-gather.41
  165.6 58.2 all-gather.45
  230.3 27.3 all-gather.19
  274.3 26.6 reduce-scatter.17
  342.3 31.0 all-gather.21
  389.1 26.5 reduce-scatter.19
  456.1 31.1 all-gather.23
  503.0 26.6 reduce-scatter.21
  569.9 31.1 all-gather.25
  616.8 26.5 reduce-scatter.23
  680.7 31.0 all-gather.27
  713.3 27.4 all-gather.29
  756.1 26.6 reduce-scatter.27
  808.5 15.7 reduce-scatter.29
  840.0 28.5 all-gather.31
  884.0 26.6 reduce-scatter.31
  936.5 15.6 reduce-scatter.33
  967.1 28.4 all-gather.33
  1011.1 26.6 reduce-scatter.35
  1063.5 15.7 reduce-scatter.37
  1094.2 28.5 all-gather.35
  1138.2 26.6 reduce-scatter.39
  1190.7 15.6 reduce-scatter.41
  1221.4 28.5 all-gather.37
  1265.5 26.6 reduce-scatter.43
  1332.3 27.4 reduce-scatter.25
  1395.7 84.6 all-reduce.3
  1483.8 93.2 all-reduce.5
  1580.0 76.9 reduce-scatter.47
  1659.8 77.2 reduce-scatter.49
  (1 shorter events, 15.6 us)

commit v2 on v1

--- a/solution.py
+++ b/solution.py
@@ -1,13 +1,520 @@
+import functools
 import math
 
 import jax
 import jax.numpy as jnp
 from jax import lax
+from jax.experimental import pallas as pl
+from jax.experimental.pallas import tpu as pltpu
 from jax.sharding import PartitionSpec as P
 
 HD = 128
 F32 = jnp.float32
 BF16 = jnp.bfloat16
+MESH = pl.DeviceIdType.MESH
+GELU_A = math.sqrt(2.0 / math.pi)
+GELU_B = 0.044715
+
+
+def dot(a, b):
+    return jnp.dot(a, b, preferred_element_type=F32)
+
+
+def dot_t(a, b):
+    return lax.dot_general(a, b, (((1,), (1,)), ((), ())), preferred_element_type=F32)
+
+
+def aligned(start, size):
+    return pl.ds(pl.multiple_of(start, size), size)
+
+
+def greet(n):
+    me = lax.axis_index("tensor")
+    barrier = pltpu.get_barrier_semaphore()
+    for k in range(1, n):
+        pl.semaphore_signal(
+            barrier, inc=1, device_id={"tensor": lax.rem(me + k, n)}, device_id_type=MESH
+        )
+    pl.semaphore_signal(
+        barrier, inc=1, device_id={"section": 1 - lax.axis_index("section")}, device_id_type=MESH
+    )
+    pl.semaphore_wait(barrier, n)
+
+
+def normalize(v):
+    mean = jnp.mean(v, axis=-1, keepdims=True)
+    centred = v - mean
+    var = jnp.mean(centred * centred, axis=-1, keepdims=True)
+    rstd = lax.rsqrt(var + 1e-05)
+    return centred * rstd, rstd
+
+
+def line_rounds(n, chunks, rows, bufs, compute, finish):
+    (g, terms, sum_r, sum_l, in_l, in_r) = bufs["refs"]
+    (gs_r, gs_l, g_recv, rs_r, rs_l, rr_l, rr_r) = bufs["sems"]
+    me = lax.axis_index("tensor")
+
+    def part(j):
+        return pl.ds(pl.multiple_of(j * rows, rows), rows)
+
+    def gather_copy(c, j, step, to_right):
+        return pltpu.make_async_remote_copy(
+            src_ref=g.at[c, part(j)],
+            dst_ref=g.at[c, part(j)],
+            send_sem=(gs_r if to_right else gs_l).at[c, step],
+            recv_sem=g_recv.at[c, j],
+            device_id={"tensor": jnp.minimum(me + 1, n - 1) if to_right else jnp.maximum(me - 1, 0)},
+            device_id_type=MESH,
+        )
+
+    def sum_copy(c, j, to_right):
+        return pltpu.make_async_remote_copy(
+            src_ref=(sum_r if to_right else sum_l).at[c, part(j)],
+            dst_ref=(in_l if to_right else in_r).at[c, part(j)],
+            send_sem=(rs_r if to_right else rs_l).at[c, j],
+            recv_sem=(rr_l if to_right else rr_r).at[c, j],
+            device_id={"tensor": jnp.minimum(me + 1, n - 1) if to_right else jnp.maximum(me - 1, 0)},
+            device_id_type=MESH,
+        )
+
+    def slot(s, carry):
+        for h in range(n):
+            c = s - h
+
+            @pl.when((c >= 0) & (c < chunks))
+            def _(h=h, c=c):
+                from_l = me - h >= 0
+                from_r = me + h <= n - 1
+                if h > 0:
+
+                    @pl.when(from_l)
+                    def _():
+                        gather_copy(c, jnp.maximum(me - h, 0), 0, True).wait_recv()
+
+                    @pl.when(from_r)
+                    def _():
+                        gather_copy(c, jnp.minimum(me + h, n - 1), 0, False).wait_recv()
+
+                if h < n - 1:
+
+                    @pl.when(from_l & (me < n - 1))
+                    def _():
+                        gather_copy(c, jnp.maximum(me - h, 0), h, True).start()
+
+                    @pl.when(from_r & (me > 0))
+                    def _():
+                        gather_copy(c, jnp.minimum(me + h, n - 1), h, False).start()
+
+        for h in range(n - 1):
+            c = s - n - h
+
+            @pl.when((c >= 0) & (c < chunks))
+            def _(h=h, c=c):
+                if h == 0:
+                    finish(c, "kept")
+
+                @pl.when((h >= me) & (me < n - 1))
+                def _():
+                    j = jnp.minimum(n - 1 - (h - me), n - 1)
+
+                    @pl.when(me > 0)
+                    def _():
+                        sum_copy(c, j, True).wait_recv()
+                        sum_r[c, part(j)] = (terms[c, part(j)] + in_l[c, part(j)].astype(F32)).astype(BF16)
+
+                    @pl.when(me == 0)
+                    def _():
+                        sum_r[c, part(j)] = terms[c, part(j)].astype(BF16)
+
+                    sum_copy(c, j, True).start()
+
+                @pl.when((h >= n - 1 - me) & (me > 0))
+                def _():
+                    j = jnp.maximum(h - (n - 1 - me), 0)
+
+                    @pl.when(me < n - 1)
+                    def _():
+                        sum_copy(c, j, False).wait_recv()
+                        sum_l[c, part(j)] = (terms[c, part(j)] + in_r[c, part(j)].astype(F32)).astype(BF16)
+
+                    @pl.when(me == n - 1)
+                    def _():
+                        sum_l[c, part(j)] = terms[c, part(j)].astype(BF16)
+
+                    sum_copy(c, j, False).start()
+
+        c_done = s - (2 * n - 1)
+
+        @pl.when((c_done >= 0) & (c_done < chunks))
+        def _():
+            @pl.when(me > 0)
+            def _():
+                sum_copy(c_done, me, True).wait_recv()
+                terms[c_done, part(me)] += in_l[c_done, part(me)].astype(F32)
+
+            @pl.when(me < n - 1)
+            def _():
+                sum_copy(c_done, me, False).wait_recv()
+                terms[c_done, part(me)] += in_r[c_done, part(me)].astype(F32)
+
+        c_now = s - (n - 1)
+
+        @pl.when((c_now >= 0) & (c_now < chunks))
+        def _():
+            compute(c_now)
+
+        return carry
+
+    lax.fori_loop(0, chunks + 2 * n - 1, slot, 0)
+
+    def drain(c, carry):
+        for h in range(n - 1):
+
+            @pl.when((me - h >= 0) & (me < n - 1))
+            def _(h=h):
+                gather_copy(c, jnp.maximum(me - h, 0), h, True).wait_send()
+
+            @pl.when((me + h <= n - 1) & (me > 0))
+            def _(h=h):
+                gather_copy(c, jnp.minimum(me + h, n - 1), h, False).wait_send()
+
+        for j in range(n):
+
+            @pl.when(j > me)
+            def _(j=j):
+                sum_copy(c, j, True).wait_send()
+
+            @pl.when(j < me)
+            def _(j=j):
+                sum_copy(c, j, False).wait_send()
+
+        return carry
+
+    lax.fori_loop(0, chunks, drain, 0)
+
+
+def line_scratch(n, chunks, rows, width):
+    whole = n * rows
+    refs = [
+        pltpu.VMEM((chunks, whole, width), BF16),
+        pltpu.VMEM((chunks, whole, width), F32),
+    ] + [pltpu.VMEM((chunks, whole, width), BF16)] * 4
+    sems = [pltpu.SemaphoreType.DMA((chunks, n))] * 7
+    return refs, sems
+
+
+def forward_kernel(
+    cfg,
+    tokens,
+    w_q_hbm,
+    w_o_hbm,
+    w_up_hbm,
+    w_dn_hbm,
+    w_kv,
+    vecs,
+    up_bias,
+    pair_bias,
+    normed_out,
+    query_out,
+    att_out,
+    lse_out,
+    input_out,
+    hidden_out,
+    result_out,
+    kv_out,
+    two_hbm,
+    act_hbm,
+    slope_hbm,
+    w_q,
+    w_o,
+    w_up,
+    w_dn,
+    x_ref,
+    q_ref,
+    v_t,
+    s_ref,
+    act,
+    slope,
+    inbox,
+    g,
+    terms,
+    sum_r,
+    sum_l,
+    in_l,
+    in_r,
+    gs_r,
+    gs_l,
+    g_recv,
+    rs_r,
+    rs_l,
+    rr_l,
+    rr_r,
+    w_sem,
+    kv_send,
+    kv_recv,
+    keep_sem,
+    hand_send,
+    hand_recv,
+):
+    n, nb, own, chunks, rows, tile = (cfg[k] for k in ("n", "nb", "own", "chunks", "rows", "tile"))
+    dim = x_ref.shape[1]
+    ff = w_up.shape[1]
+    width = w_q.shape[1]
+    heads = width // HD
+    block = n * own
+    per = cfg["per"]
+    me = lax.axis_index("tensor")
+    sec = lax.axis_index("section")
+    scale = 1.0 / math.sqrt(HD)
+    loads = [
+        pltpu.make_async_copy(src, dst, w_sem.at[k])
+        for k, (src, dst) in enumerate(((w_q_hbm, w_q), (w_o_hbm, w_o), (w_up_hbm, w_up), (w_dn_hbm, w_dn)))
+    ]
+    for load in loads:
+        load.start()
+    greet(n)
+
+    def pairs_copy(b, k):
+        rows_here = aligned(b * block + me * own, own)
+        return pltpu.make_async_remote_copy(
+            src_ref=kv_out.at[rows_here],
+            dst_ref=kv_out.at[rows_here],
+            send_sem=kv_send.at[k],
+            recv_sem=kv_recv.at[k],
+            device_id={"tensor": lax.rem(me + k, n)},
+            device_id_type=MESH,
+        )
+
+    def hand_copy(b):
+        return pltpu.make_async_remote_copy(
+            src_ref=result_out.at[b],
+            dst_ref=inbox.at[b],
+            send_sem=hand_send.at[b],
+            recv_sem=hand_recv.at[b],
+            device_id={"section": 1 - sec},
+            device_id_type=MESH,
+        )
+
+    def keep_copies(b, c):
+        return [
+            pltpu.make_async_copy(g.at[c], two_hbm.at[b, c], keep_sem.at[0, c]),
+            pltpu.make_async_copy(act.at[c], act_hbm.at[b, c], keep_sem.at[1, c]),
+            pltpu.make_async_copy(slope.at[c], slope_hbm.at[b, c], keep_sem.at[2, c]),
+        ]
+
+    def block_step(b, carry):
+        @pl.when(sec == 0)
+        def _():
+            input_out[b] = tokens[b]
+
+        @pl.when(sec != 0)
+        def _():
+            hand_copy(b).wait_recv()
+            input_out[b] = inbox[b]
+
+        x_ref[...] = input_out[b].astype(F32)
+        unit, _ = normalize(x_ref[...])
+        normed = (unit * vecs[0:1] + vecs[1:2]).astype(BF16)
+        normed_out[b] = normed
+        pairs = (dot(normed, w_kv[...]) + pair_bias[...]).astype(BF16)
+        kv_out[aligned(b * block + me * own, own)] = pairs
+        for k in range(1, n):
+            pairs_copy(b, k).start()
+
+        @pl.when(b == 0)
+        def _():
+            loads[0].wait()
+
+        def query_tile(t, carry):
+            cols = aligned(t * tile, tile)
+            q = (dot(normed_out[b], w_q[:, cols]) + vecs[6:7, cols]).astype(BF16)
+            for k in range(tile // HD):
+                q_ref[aligned((t * (tile // HD) + k) * own, own)] = q[:, k * HD : (k + 1) * HD]
+            return carry
+
+        lax.fori_loop(0, width // tile, query_tile, 0)
+        query_out[b] = q_ref[...]
+        for k in range(1, n):
+            pairs_copy(b, k).wait_recv()
+        here = aligned(b * block, block)
+        v_t[b] = kv_out[here, HD:].astype(F32).T.astype(BF16)
+
+        def head_tile(t, carry):
+            q = q_ref[aligned(t * per * own, per * own)]
+
+            def score(kb, top):
+                s = dot_t(kv_out[aligned(kb * block, block), :HD], q) * scale
+                s_ref[kb] = s
+                return jnp.maximum(top, jnp.max(s, axis=0, keepdims=True))
+
+            top = lax.fori_loop(0, b + 1, score, jnp.full((1, per * own), -jnp.inf, F32))
+
+            def weigh(kb, state):
+                total, acc = state
+                e = jnp.exp(s_ref[kb] - top)
+                return total + jnp.sum(e, axis=0, keepdims=True), acc + dot(v_t[kb], e.astype(BF16))
+
+            total, acc = lax.fori_loop(
+                0,
+                b + 1,
+                weigh,
+                (jnp.zeros((1, per * own), F32), jnp.zeros((HD, per * own), F32)),
+            )
+            lse_out[b, t] = top + jnp.log(total)
+            mixed = (acc / total).T.astype(BF16)
+            for k in range(per):
+                att_out[b, :, aligned((t * per + k) * HD, HD)] = mixed[k * own : (k + 1) * own]
+            return carry
+
+        lax.fori_loop(0, heads // per, head_tile, 0)
+
+        @pl.when(b == 0)
+        def _():
+            loads[1].wait()
+
+        def out_tile(t, carry):
+            cols = aligned(t * tile, tile)
+            hidden_out[b, :, cols] = (
+                x_ref[:, cols] + dot(att_out[b], w_o[:, cols]) + vecs[4:5, cols]
+            )
+            return carry
+
+        lax.fori_loop(0, dim // tile, out_tile, 0)
+        unit, _ = normalize(hidden_out[b])
+        normed_two = (unit * vecs[2:3] + vecs[3:4]).astype(BF16)
+        for c in range(chunks):
+            g[c, aligned(me * rows, rows)] = normed_two[c * rows : (c + 1) * rows]
+
+        @pl.when(b == 0)
+        def _():
+            loads[2].wait()
+            loads[3].wait()
+
+        def compute(c):
+            def up_tile(t, carry):
+                cols = aligned(t * tile, tile)
+                pre = dot(g[c], w_up[:, cols]) + up_bias[:, cols]
+                inner = GELU_A * (pre + GELU_B * pre * pre * pre)
+                th = jnp.tanh(inner)
+                half = 0.5 * (1.0 + th)
+                act[c, :, cols] = (pre * half).astype(BF16)
+                slope[c, :, cols] = (
+                    half + 0.5 * pre * (1.0 - th * th) * (GELU_A * (1.0 + 3.0 * GELU_B * pre * pre))
+                ).astype(BF16)
+                return carry
+
+            lax.fori_loop(0, ff // tile, up_tile, 0)
+
+            def down_tile(t, carry):
+                cols = aligned(t * tile, tile)
+                terms[c, :, cols] = dot(act[c], w_dn[:, cols])
+                return carry
+
+            lax.fori_loop(0, dim // tile, down_tile, 0)
+            for copy in keep_copies(b, c):
+                copy.start()
+
+        def finish(c, what):
+            for copy in keep_copies(b, c):
+                copy.wait()
+
+        line_rounds(
+            n,
+            chunks,
+            rows,
+            {
+                "refs": (g, terms, sum_r, sum_l, in_l, in_r),
+                "sems": (gs_r, gs_l, g_recv, rs_r, rs_l, rr_l, rr_r),
+            },
+            compute,
+            finish,
+        )
+        for c in range(chunks):
+            part = slice(c * rows, (c + 1) * rows)
+            result_out[b, part] = (
+                hidden_out[b, part] + terms[c, aligned(me * rows, rows)] + vecs[5:6]
+            ).astype(BF16)
+
+        @pl.when(sec == 0)
+        def _():
+            hand_copy(b).start()
+
+        for k in range(1, n):
+            pairs_copy(b, k).wait_send()
+        return carry
+
+    lax.fori_loop(0, nb, block_step, 0)
+
+    def settle(b, carry):
+        @pl.when(sec == 0)
+        def _():
+            hand_copy(b).wait_send()
+
+        return carry
+
+    lax.fori_loop(0, nb, settle, 0)
+
+
+def forward(tokens, w_q, w_o, w_up, w_dn, w_kv, vecs, up_bias, pair_bias):
+    n = lax.axis_size("tensor")
+    nb, own, dim = tokens.shape
+    rows = min(16, own)
+    chunks = own // rows
+    ff = w_up.shape[1]
+    width = w_q.shape[1]
+    heads = width // HD
+    tile = min(512, dim, ff)
+    per = min(heads, max(1, 256 // own))
+    block = n * own
+    cfg = dict(n=n, nb=nb, own=own, chunks=chunks, rows=rows, tile=tile, per=per)
+    S = jax.ShapeDtypeStruct
+    vmem = pl.BlockSpec(memory_space=pltpu.VMEM)
+    hbm = pl.BlockSpec(memory_space=pl.ANY)
+    line_refs, line_sems = line_scratch(n, chunks, rows, dim)
+    dma = pltpu.SemaphoreType.DMA
+    return pl.pallas_call(
+        functools.partial(forward_kernel, cfg),
+        name="forward",
+        out_shape=(
+            S((nb, own, dim), BF16),
+            S((nb, heads * own, HD), BF16),
+            S((nb, own, width), BF16),
+            S((nb, heads // per, 1, per * own), F32),
+            S((nb, own, dim), BF16),
+            S((nb, own, dim), F32),
+            S((nb, own, dim), BF16),
+            S((nb * block, 2 * HD), BF16),
+            S((nb, chunks, n * rows, dim), BF16),
+            S((nb, chunks, n * rows, ff), BF16),
+            S((nb, chunks, n * rows, ff), BF16),
+        ),
+        in_specs=[vmem, hbm, hbm, hbm, hbm, vmem, vmem, vmem, vmem],
+        out_specs=(vmem,) * 8 + (hbm,) * 3,
+        scratch_shapes=[
+            pltpu.VMEM((dim, width), BF16),
+            pltpu.VMEM((width, dim), BF16),
+            pltpu.VMEM((dim, ff), BF16),
+            pltpu.VMEM((ff, dim), BF16),
+            pltpu.VMEM((own, dim), F32),
+            pltpu.VMEM((heads * own, HD), BF16),
+            pltpu.VMEM((nb, HD, block), BF16),
+            pltpu.VMEM((nb, block, per * own), F32),
+            pltpu.VMEM((chunks, n * rows, ff), BF16),
+            pltpu.VMEM((chunks, n * rows, ff), BF16),
+            pltpu.VMEM((nb, own, dim), BF16),
+            *line_refs,
+            *line_sems,
+            dma((4,)),
+            dma((n,)),
+            dma((n,)),
+            dma((3, chunks)),
+            dma((nb,)),
+            dma((nb,)),
+        ],
+        compiler_params=pltpu.CompilerParams(
+            collective_id=1, has_side_effects=True, vmem_limit_bytes=67000000
+        ),
+    )(tokens, w_q, w_o, w_up, w_dn, w_kv, vecs, up_bias, pair_bias)
 
 
 def from_behind(block, axis, distance):
@@ -25,14 +532,6 @@
 
 def gelu_tanh(values):
     return jax.nn.gelu(values, approximate=True)
-
-
-def dot(a, b):
-    return jnp.dot(a, b, preferred_element_type=F32)
-
-
-def dot_t(a, b):
-    return lax.dot_general(a, b, (((1,), (1,)), ((), ())), preferred_element_type=F32)
 
 
 def t_dot(a, b):
@@ -145,59 +644,43 @@
     def zeros(shape, dtype):
         return jnp.zeros(shape, dtype)
 
-    kept_normed = zeros((blocks, own_count, model_dim), BF16)
-    kept_query = zeros((blocks, own_count, width), BF16)
-    kept_attended = zeros((blocks, own_count, width), BF16)
-    kept_logsum = zeros((blocks, own_count * heads), F32)
-    kv_cache = zeros((total_len, 2 * HD), BF16)
-    kept_input = zeros((blocks, own_count, model_dim), F32)
-    kept_hidden = zeros((blocks, own_count, model_dim), F32)
-    kept_normed_two = zeros((blocks, block_len, model_dim), BF16)
-    kept_pre = zeros((blocks, block_len, ff_local), F32)
-    kept_active = zeros((blocks, block_len, ff_local), BF16)
-    outputs = zeros((blocks, own_count, model_dim), BF16)
-    received = zeros((own_count, model_dim), F32)
-
     def put(kept, value, index):
         return lax.dynamic_update_index_in_dim(kept, value, index, 0)
 
     def take(kept, index):
         return lax.dynamic_index_in_dim(kept, index, 0, keepdims=False)
 
-    for turn in range(blocks + 1):
-        block_index = jnp.clip(turn - section, 0, blocks - 1)
-        layer_input = jnp.where(section == 0, take(tokens_in, block_index).astype(F32), received)
-        normed = layer_norm(layer_input, gain_one, bias_one).astype(BF16)
-        pairs = gather_rows((dot(normed, w_pairs) + pair_bias).astype(BF16))
-        kv_cache = lax.dynamic_update_slice_in_dim(kv_cache, pairs, block_index * block_len, 0)
-        query = (dot(normed, w_query) + b_query).astype(BF16)
-        visible = positions < (block_index + 1) * block_len
-        query_rows = query.reshape(own_count * heads, HD)
-        scores = dot_t(query_rows, kv_cache[:, :HD]) * score_scale
-        scores = jnp.where(visible, scores, -1e30)
-        row_top = jnp.max(scores, axis=-1, keepdims=True)
-        exponent = jnp.exp(scores - row_top)
-        row_total = jnp.sum(exponent, axis=-1, keepdims=True)
-        log_total = (row_top + jnp.log(row_total))[:, 0]
-        weights_low = (exponent / row_total).astype(BF16)
-        attended = dot(weights_low, kv_cache[:, HD:]).astype(BF16).reshape(own_count, width)
-        hidden = layer_input + dot(attended, w_out) + b_out
-        normed_two = gather_rows(layer_norm(hidden, gain_two, bias_two).astype(BF16))
-        pre_active = dot(normed_two, w_up) + b_up
-        active = gelu_tanh(pre_active).astype(BF16)
-        result_low = (hidden + sum_rows(dot(active, w_down)) + b_down).astype(BF16)
-        kept_normed = put(kept_normed, normed, block_index)
-        kept_query = put(kept_query, query, block_index)
-        kept_attended = put(kept_attended, attended, block_index)
-        kept_logsum = put(kept_logsum, log_total, block_index)
-        kept_input = put(kept_input, layer_input, block_index)
-        kept_hidden = put(kept_hidden, hidden, block_index)
-        kept_normed_two = put(kept_normed_two, normed_two, block_index)
-        kept_pre = put(kept_pre, pre_active, block_index)
-        kept_active = put(kept_active, active, block_index)
-        outputs = put(outputs, result_low, block_index)
-        if turn < blocks:
-            received = from_behind(result_low, "section", 1).astype(F32)
+    vecs = jnp.stack([gain_one, bias_one, gain_two, bias_two, b_out, b_down, b_query, b_query])
+    (
+        kept_normed,
+        kept_query,
+        kept_attended,
+        kept_logsum,
+        kept_input,
+        kept_hidden,
+        outputs,
+        kv_cache,
+        kept_normed_two,
+        kept_active,
+        kept_slope,
+    ) = forward(
+        tokens_in, w_query, w_out, w_up, w_down, w_pairs, vecs, b_up[None], pair_bias[None]
+    )
+    chunks, chunk_rows = kept_active.shape[1], own_count // kept_active.shape[1]
+    kept_query = kept_query.reshape(blocks, heads, own_count, HD)
+    kept_logsum = kept_logsum.reshape(blocks, heads, own_count)
+    kept_input = kept_input.astype(F32)
+    kept_normed_two = kept_normed_two.reshape(blocks, block_len, model_dim)
+    kept_active = kept_active.reshape(blocks, block_len, ff_local)
+    kept_slope = kept_slope.reshape(blocks, block_len, ff_local)
+
+    def to_chunks(rows):
+        rows = rows.reshape(tensor_count, chunks, chunk_rows, -1)
+        return rows.transpose(1, 0, 2, 3).reshape(block_len, -1)
+
+    def from_chunks(rows):
+        rows = rows.reshape(chunks, tensor_count, chunk_rows, -1)
+        return rows.transpose(1, 0, 2, 3).reshape(block_len, -1)
 
     key_rows = kv_cache[:, :HD]
     value_rows = kv_cache[:, HD:]
@@ -217,18 +700,17 @@
         slot = jnp.where(valid, block_index, blocks)
         grad_out = jnp.where(section == 1, take(cotangent, block_index).astype(F32), received_back)
         grad_out = grad_out * valid.astype(F32)
-        pre_active = take(kept_pre, block_index)
-        grad_mlp = gather_rows(grad_out.astype(BF16))
+        grad_mlp = to_chunks(gather_rows(grad_out.astype(BF16)))
         grad_active = dot_t(grad_mlp, w_down)
-        grad_pre = jax.vjp(gelu_tanh, pre_active)[1](grad_active)[0].astype(BF16)
-        grad_normed_two = sum_rows(dot_t(grad_pre, w_up))
+        grad_pre = (grad_active * take(kept_slope, block_index).astype(F32)).astype(BF16)
+        grad_normed_two = sum_rows(from_chunks(dot_t(grad_pre, w_up)))
         norm_back_two = jax.vjp(layer_norm, take(kept_hidden, block_index), gain_two, bias_two)[1]
         grad_hidden_norm, gain_two_term, bias_two_term = norm_back_two(grad_normed_two)
         grad_hidden = grad_out + grad_hidden_norm
         branch = grad_hidden.astype(BF16)
         grad_attended = dot_t(branch, w_out).astype(BF16).reshape(own_count * heads, HD)
-        query_rows = take(kept_query, block_index).reshape(own_count * heads, HD)
-        log_total = take(kept_logsum, block_index)
+        query_rows = take(kept_query, block_index).transpose(1, 0, 2).reshape(own_count * heads, HD)
+        log_total = take(kept_logsum, block_index).T.reshape(-1)
         visible = positions < (block_index + 1) * block_len
         scores = dot_t(query_rows, key_rows) * score_scale
         scores = jnp.where(visible, scores, -1e30)

time: 1820 us -> 1590 us (0.87)
  Pallas kernels: 0 us -> 200 us
  matrix products: 387 us -> 231 us
  waiting for transfers between devices: 880 us -> 769 us
  blocking collectives: 64.5 us -> 9.27 us
  local copies, waits for them, and re-layouts: 197 us -> 148 us
  other arithmetic: 224 us -> 178 us
    pallas_call x0 -> x1, Pallas kernels: none -> 200 us  [forward(): pl.pallas_call(functools.partial(forward_kernel, cfg), name='forward', ou...]
    dot_general x35 -> x5, matrix products: 141 us -> 7.35 us  [dot(): return jnp.dot(a, b, preferred_element_type=F32)]
    all_gather x10 -> x5, waiting for transfers between devices: 222 us -> 117 us  [gather_rows(): return lax.all_gather(own_rows, 'tensor', axis=0, tiled=True)]
    all_gather x5 -> x0, blocking collectives: 55.3 us -> none  [gather_rows(): return lax.all_gather(own_rows, 'tensor', axis=0, tiled=True)]
    all_gather x2, waiting for transfers between devices: 86.6 us -> 117 us  [whole_weight(): return lax.all_gather(own, 'dp', axis=split, tiled=True)]
    dynamic_update_slice x39 -> x15, local copies, waits for them, and re-layouts: 43.1 us -> 20 us  [put(): return lax.dynamic_update_index_in_dim(kept, value, index, 0)]
    ppermute x8 -> x4, waiting for transfers between devices: 41.6 us -> 19.7 us  [from_behind(): return lax.ppermute(block, axis, route)]
    dynamic_update_slice x25 -> x10, other arithmetic: 31.5 us -> 11.7 us  [put(): return lax.dynamic_update_index_in_dim(kept, value, index, 0)]
  transfers between devices with their start and end apart: 57 -> 43, of which waited for: 42 -> 30; matrix products, arithmetic and copies ran while one was open for 22% -> 19% of each run, Pallas kernels for 0% -> 0%
where the time goes in v2:
time: 1590 us; the launch traced here: 1580 us
  waiting for transfers between devices  769 us (48%)
  matrix products  231 us (15%)
  Pallas kernels  200 us (13%)
  other arithmetic  178 us (11%)
  local copies, waits for them, and re-layouts  148 us (9%)
  starting transfers between devices  29.8 us (2%)
  between operations  16.2 us (1%)
    pallas_call x1, Pallas kernels, forward(): pl.pallas_call(functools.partial(forward_kernel, cfg), name='forward', ou...  200 us
    reduce_scatter x10, waiting for transfers between devices, sum_rows(): lax.psum_scatter(partial.astype(BF16), 'tensor', scatter_dimension=0, til...  187 us
    dot_general x35, matrix products, dot_t(): lax.dot_general(a, b, (((1,), (1,)), ((), ())), preferred_element_type=F32)  171 us
    ppermute x16, waiting for transfers between devices, swap(): return lax.ppermute(value, 'dp', [(i, i ^ distance) for i in range(size)])  166 us
    all_gather x2, waiting for transfers between devices, whole_weight(): return lax.all_gather(own, 'dp', axis=split, tiled=True)  117 us
    all_gather x5, waiting for transfers between devices, gather_rows(): return lax.all_gather(own_rows, 'tensor', axis=0, tiled=True)  117 us
    all_gather x2, waiting for transfers between devices, whole_weight(): own = lax.all_gather(own, 'tensor', axis=join, tiled=True)  91.4 us
    reduce_scatter x2, waiting for transfers between devices, sum_dp(): lax.psum_scatter(value.astype(BF16), 'tensor', scatter_dimension=scatter,...  70.6 us
  transfers between devices with their start and end apart: 43, of which 30 were waited for; matrix products, arithmetic and copies ran while one was open for 19% of the time, Pallas kernels for 0%

profile of v2, /device:TPU:1, one launch (start us, length us, event | category | flops | bytes accessed | tf_op | source)
XLA Modules:
  0.0 1581.3 jit_solution(17211097756721221923)
XLA Ops:
  13.6 44.6 %all-gather.25.cloned.1.call-done = bf16[1,512,2048]{2,1,0:T(8,128)(2,1)} async-done(((bf16[1,512,512]{2,1,0:T(8,128)(2,1)}), bf16[1,512,2048]{2,1,0:T(8,128)(2,1)}) %all-gather.25.cloned.1.call-update) | async-done | bytes 2097168 | tf_op jit(solution)/shard_map/all_gather | solution.py:593
  58.3 46.8 %all-gather.29.cloned.1.call-done = bf16[1,2048,512]{2,1,0:T(8,128)(2,1)} async-done(((bf16[1,512,512]{2,1,0:T(8,128)(2,1)}), bf16[1,2048,512]{2,1,0:T(8,128)(2,1)}) %all-gather.29.cloned.1.call-update) | async-done | bytes 2097168 | tf_op jit(solution)/shard_map/all_gather | solution.py:593
  105.8 9.3 all-gather.4
  116.4 17.4 %all-gather.15.cloned.1.call-done = bf16[256,2048]{1,0:T(8,128)(2,1)} async-done(((bf16[64,2048]{1,0:T(8,128)(2,1)}), bf16[256,2048]{1,0:T(8,128)(2,1)}) %all-gather.15.cloned.1.call-update) | async-done | bytes 1048592 | tf_op jit(solution)/shard_map/all_gather | solution.py:542
  136.2 57.4 %all-gather.27.cloned.1.call-done = bf16[1,2048,2048]{2,1,0:T(8,128)(2,1)} async-done(((bf16[1,512,2048]{2,1,0:T(8,128)(2,1)}), bf16[1,2048,2048]{2,1,0:T(8,128)(2,1)}) %all-gather.27.cloned.1.call-update) | async-done | bytes 8388624 | tf_op jit(solution)/shard_map/all_gather | solution.py:594
  193.6 59.7 %all-gather.31.cloned.1.call-done = bf16[1,2048,2048]{2,1,0:T(8,128)(2,1)} async-done(((bf16[1,2048,512]{2,1,0:T(8,128)(2,1)}), bf16[1,2048,2048]{2,1,0:T(8,128)(2,1)}) %all-gather.31.cloned.1.call-update) | async-done | bytes 8388624 | tf_op jit(solution)/shard_map/all_gather | solution.py:594
  253.3 200.1 %forward.1 = (bf16[4,64,2048]{2,1,0:T(8,128)(2,1)}, bf16[4,1024,128]{2,1,0:T(8,128)(2,1)}, bf16[4,64,2048]{2,1,0:T(8,128)(2,1)}, f32[4,4,1,256]{3,2,1,0:T(1,128)...) custom-call(bf16[4,64,2048]{2,1,0:T(8,128)(2,1)} %bitcast.567, ...), custom_call_target="tpu_custom_call" | custom-call | tf_op jit(solution)/shard_map/forward/pallas_call | solution.py:475
  473.5 91.6 %reduce-scatter.13.cloned.1.call-done = bf16[64,2048]{1,0:T(8,128)(2,1)} async-done(((bf16[256,2048]{1,0:T(8,128)(2,1)}), bf16[64,2048]{1,0:T(8,128)(2,1)}) %reduce-scatter.13.cloned.1.call-update) | async-done | bytes 262160 | tf_op jit(solution)/shard_map/reduce_scatter | solution.py:546
  596.7 8.9 reduce-scatter.15.cloned.1.call-done
  619.2 28.4 %all-gather.17.cloned.1.call-done = bf16[256,2048]{1,0:T(8,128)(2,1)} async-done(((bf16[64,2048]{1,0:T(8,128)(2,1)}), bf16[256,2048]{1,0:T(8,128)(2,1)}) %all-gather.17.cloned.1.call-update) | async-done | bytes 1048592 | tf_op jit(solution)/shard_map/all_gather | solution.py:542
  649.1 7.5 bitcast_dynamic-update-slice_fusion.3
  665.1 21.7 %reduce-scatter.17.cloned.1.call-done = bf16[64,2048]{1,0:T(8,128)(2,1)} async-done(((bf16[256,2048]{1,0:T(8,128)(2,1)}), bf16[64,2048]{1,0:T(8,128)(2,1)}) %reduce-scatter.17.cloned.1.call-update) | async-done | bytes 262160 | tf_op jit(solution)/shard_map/reduce_scatter | solution.py:546
  723.8 9.0 reduce-scatter.19.cloned.1.call-done
  745.9 28.2 %all-gather.19.cloned.1.call-done = bf16[256,2048]{1,0:T(8,128)(2,1)} async-done(((bf16[64,2048]{1,0:T(8,128)(2,1)}), bf16[256,2048]{1,0:T(8,128)(2,1)}) %all-gather.19.cloned.1.call-update) | async-done | bytes 1048592 | tf_op jit(solution)/shard_map/all_gather | solution.py:542
  775.5 7.3 bitcast_dynamic-update-slice_fusion.2
  794.7 21.7 %reduce-scatter.21.cloned.1.call-done = bf16[64,2048]{1,0:T(8,128)(2,1)} async-done(((bf16[256,2048]{1,0:T(8,128)(2,1)}), bf16[64,2048]{1,0:T(8,128)(2,1)}) %reduce-scatter.21.cloned.1.call-update) | async-done | bytes 262160 | tf_op jit(solution)/shard_map/reduce_scatter | solution.py:546
  853.5 8.9 reduce-scatter.23.cloned.1.call-done
  876.4 27.8 %all-gather.21.cloned.1.call-done = bf16[256,2048]{1,0:T(8,128)(2,1)} async-done(((bf16[64,2048]{1,0:T(8,128)(2,1)}), bf16[256,2048]{1,0:T(8,128)(2,1)}) %all-gather.21.cloned.1.call-update) | async-done | bytes 1048592 | tf_op jit(solution)/shard_map/all_gather | solution.py:542
  984.6 8.7 reduce-scatter.27.cloned.1.call-done
  1021.4 15.2 all-gather.23.cloned.1.call-done
  1037.9 7.3 bitcast_dynamic-update-slice_fusion
  1060.3 12.3 fusion.208
  1168.8 8.4 add_convert_fusion.1
  1177.3 12.7 fusion.209
  1233.0 40.5 %collective-permute-done.13 = bf16[512,2048]{1,0:T(8,128)(2,1)} collective-permute-done((bf16[512,2048]{1,0:T(8,128)(2,1)}, bf16[512,2048]{1,0:T(8,128)(2,1)}, u32[]{:S(2)}, u32[]{:S(2)}) %collective-permute-start.13) | collective-permute-done | bytes 2097184 | tf_op jit(solution)/shard_map/ppermute | solution.py:553
  1279.6 8.4 add_convert_fusion
  1288.0 33.3 %collective-permute-done.17 = bf16[512,2048]{1,0:T(8,128)(2,1)} collective-permute-done((bf16[512,2048]{1,0:T(8,128)(2,1)}, bf16[512,2048]{1,0:T(8,128)(2,1)}, u32[]{:S(2)}, u32[]{:S(2)}) %collective-permute-start.17) | collective-permute-done | bytes 2097184 | tf_op jit(solution)/shard_map/ppermute | solution.py:553
  1326.0 43.1 %collective-permute-done.14 = bf16[512,2048]{1,0:T(8,128)(2,1)} collective-permute-done((bf16[512,2048]{1,0:T(8,128)(2,1)}, bf16[512,2048]{1,0:T(8,128)(2,1)}, u32[]{:S(2)}, u32[]{:S(2)}) %collective-permute-start.14) | collective-permute-done | bytes 2097184 | tf_op jit(solution)/shard_map/ppermute | solution.py:553
  1376.9 37.2 %collective-permute-done.18 = bf16[512,2048]{1,0:T(8,128)(2,1)S(1)} collective-permute-done((bf16[512,2048]{1,0:T(8,128)(2,1)S(1)}, bf16[512,2048]{1,0:T(8,128)(2,1)S(1)}, u32[]{:S(2)}, u32[]{:S(2)}) %collective-permute-start.18) | collective-permute-done | bytes 2097184 | tf_op jit(solution)/shard_map/ppermute | solution.py:553
  1440.0 70.6 %reduce-scatter.35.cloned.1.call-done = bf16[512,1024]{1,0:T(8,128)(2,1)} async-done(((bf16[2048,1024]{1,0:T(8,128)(2,1)}), bf16[512,1024]{1,0:T(8,128)(2,1)}) %reduce-scatter.35.cloned.1.call-update) | async-done | bytes 1048592 | tf_op jit(solution)/shard_map/reduce_scatter | solution.py:578
  1514.2 11.8 maximum_convert_fusion
  1554.5 11.8 maximum_convert_fusion.1
  (603 shorter events, 547.2 us)
Async XLA Ops:
  7.3 51.0 %all-gather.25.cloned.1.call-start = ((), (), s32[]{:S(2)}) async-start(), calls=%async_computation.31 | async-start | bytes 2621440 | tf_op jit(solution)/shard_map/all_gather | solution.py:593
  9.2 95.9 %all-gather.29.cloned.1.call-start = ((), (), s32[]{:S(2)}) async-start(), calls=%async_computation.33 | async-start | bytes 2621440 | tf_op jit(solution)/shard_map/all_gather | solution.py:593
  11.2 122.7 %all-gather.15.cloned.1.call-start = ((), (), s32[]{:S(2)}) async-start(), calls=%async_computation.12 | async-start | bytes 1310720 | tf_op jit(solution)/shard_map/all_gather | solution.py:542
  13.6 180.0 %all-gather.27.cloned.1.call-start = ((), (), s32[]{:S(2)}) async-start(), calls=%async_computation.32 | async-start | bytes 10485760 | tf_op jit(solution)/shard_map/all_gather | solution.py:594
  58.3 195.1 %all-gather.31.cloned.1.call-start = ((), (), s32[]{:S(2)}) async-start(), calls=%async_computation.34 | async-start | bytes 10485760 | tf_op jit(solution)/shard_map/all_gather | solution.py:594
  105.2 459.9 %reduce-scatter.13.cloned.1.call-start = ((), (), s32[]{:S(2)}) async-start(), calls=%async_computation.13 | async-start | bytes 1310720 | tf_op jit(solution)/shard_map/reduce_scatter | solution.py:546
  464.6 141.0 %reduce-scatter.15.cloned.1.call-start = ((), (), s32[]{:S(2)}) async-start(), calls=%async_computation.14 | async-start | bytes 163840 | tf_op jit(solution)/shard_map/reduce_scatter | solution.py:546
  589.7 57.9 %all-gather.17.cloned.1.call-start = ((), (), s32[]{:S(2)}) async-start(), calls=%async_computation.15 | async-start | bytes 1310720 | tf_op jit(solution)/shard_map/all_gather | solution.py:542
  619.0 67.9 %reduce-scatter.17.cloned.1.call-start = ((), (), s32[]{:S(2)}) async-start(), calls=%async_computation.16 | async-start | bytes 1310720 | tf_op jit(solution)/shard_map/reduce_scatter | solution.py:546
  660.1 72.7 %reduce-scatter.19.cloned.1.call-start = ((), (), s32[]{:S(2)}) async-start(), calls=%async_computation.17 | async-start | bytes 163840 | tf_op jit(solution)/shard_map/reduce_scatter | solution.py:546
  717.0 57.2 %all-gather.19.cloned.1.call-start = ((), (), s32[]{:S(2)}) async-start(), calls=%async_computation.18 | async-start | bytes 1310720 | tf_op jit(solution)/shard_map/all_gather | solution.py:542
  745.5 71.0 %reduce-scatter.21.cloned.1.call-start = ((), (), s32[]{:S(2)}) async-start(), calls=%async_computation.19 | async-start | bytes 1310720 | tf_op jit(solution)/shard_map/reduce_scatter | solution.py:546
  789.7 72.8 %reduce-scatter.23.cloned.1.call-start = ((), (), s32[]{:S(2)}) async-start(), calls=%async_computation.20 | async-start | bytes 163840 | tf_op jit(solution)/shard_map/reduce_scatter | solution.py:546
  846.6 57.6 %all-gather.21.cloned.1.call-start = ((), (), s32[]{:S(2)}) async-start(), calls=%async_computation.21 | async-start | bytes 1310720 | tf_op jit(solution)/shard_map/all_gather | solution.py:542
  875.6 70.9 %reduce-scatter.25.cloned.1.call-start = ((), (), s32[]{:S(2)}) async-start(), calls=%async_computation.22 | async-start | bytes 1310720 | tf_op jit(solution)/shard_map/reduce_scatter | solution.py:546
  919.8 73.5 %reduce-scatter.27.cloned.1.call-start = ((), (), s32[]{:S(2)}) async-start(), calls=%async_computation.23 | async-start | bytes 163840 | tf_op jit(solution)/shard_map/reduce_scatter | solution.py:546
  977.4 59.2 %all-gather.23.cloned.1.call-start = ((), (), s32[]{:S(2)}) async-start(), calls=%async_computation.24 | async-start | bytes 1310720 | tf_op jit(solution)/shard_map/all_gather | solution.py:542
  1007.9 78.6 %reduce-scatter.29.cloned.1.call-start = ((), (), s32[]{:S(2)}) async-start(), calls=%async_computation.25 | async-start | bytes 1310720 | tf_op jit(solution)/shard_map/reduce_scatter | solution.py:546
  1059.7 97.7 %reduce-scatter.31.cloned.1.call-start = ((), (), s32[]{:S(2)}) async-start(), calls=%async_computation.26 | async-start | bytes 163840 | tf_op jit(solution)/shard_map/reduce_scatter | solution.py:546
  1081.6 131.1 %collective-permute-start.12 = (bf16[1024,2048]{1,0:T(8,128)(2,1)}, bf16[1024,2048]{1,0:T(8,128)(2,1)}, u32[]{:S(2)}, u32[]{:S(2)}) collective-permute-start(bf16[1024,2048]{1,0:T(8,128)(2,1)} %dynamic-slice_convert_fusion.1), channel_id=1, source_target_pairs={{0,1},{1,0},{2,3},{3,2},{4,5},{5,4},{6,7},{7,6},{8,9},{9,8},{10,11... | collective-permute-start | bytes 12582920 | tf_op jit(solution)/shard_map/ppermute | solution.py:553
  1142.3 279.8 %all-reduce.4.cloned.1.call-start = ((), (), s32[]{:S(2)}) async-start(), calls=%async_computation.27 | async-start | bytes 188416 | tf_op jit(solution)/shard_map/psum | solution.py:770
  1166.0 260.1 %all-reduce.6.cloned.1.call-start = ((), (), s32[]{:S(2)}) async-start(), calls=%async_computation.29 | async-start | bytes 2097152 | tf_op jit(solution)/shard_map/psum | solution.py:766
  1168.8 266.5 %reduce-scatter.33.cloned.1.call-start = ((), (), s32[]{:S(2)}) async-start(), calls=%async_computation.28 | async-start | bytes 5242880 | tf_op jit(solution)/shard_map/reduce_scatter | solution.py:578
  1177.3 333.4 %reduce-scatter.35.cloned.1.call-start = ((), (), s32[]{:S(2)}) async-start(), calls=%async_computation.30 | async-start | bytes 5242880 | tf_op jit(solution)/shard_map/reduce_scatter | solution.py:578
  1209.7 69.9 %collective-permute-start.8 = (bf16[2048,1024]{1,0:T(8,128)(2,1)}, bf16[2048,1024]{1,0:T(8,128)(2,1)}, u32[]{:S(2)}, u32[]{:S(2)}) collective-permute-start(bf16[2048,1024]{1,0:T(8,128)(2,1)} %dynamic-slice_convert_fusion.2), channel_id=1, source_target_pairs={{0,1},{1,0},{2,3},{3,2},{4,5},{5,4},{6,7},{7,6},{8,9},{9,8},{10,11... | collective-permute-start | bytes 12582920 | tf_op jit(solution)/shard_map/ppermute | solution.py:553
  1223.7 49.8 %collective-permute-start.13 = (bf16[512,2048]{1,0:T(8,128)(2,1)}, bf16[512,2048]{1,0:T(8,128)(2,1)}, u32[]{:S(2)}, u32[]{:S(2)}) collective-permute-start(bf16[512,2048]{1,0:T(8,128)(2,1)} %dynamic-slice_convert_fusion.5), channel_id=1, source_target_pairs={{0,2},{1,3},{2,0},{3,1},{4,6},{5,7},{6,4},{7,5},{8,10},{9,11},{10,... | collective-permute-start | bytes 6291464 | tf_op jit(solution)/shard_map/ppermute | solution.py:553
  1232.7 88.6 %collective-permute-start.17 = (bf16[512,2048]{1,0:T(8,128)(2,1)}, bf16[512,2048]{1,0:T(8,128)(2,1)}, u32[]{:S(2)}, u32[]{:S(2)}) collective-permute-start(bf16[512,2048]{1,0:T(8,128)(2,1)} %dynamic-slice_convert_fusion.4), channel_id=1, source_target_pairs={{0,2},{1,3},{2,0},{3,1},{4,6},{5,7},{6,4},{7,5},{8,10},{9,11},{10,... | collective-permute-start | bytes 6291464 | tf_op jit(solution)/shard_map/ppermute | solution.py:553
  1278.4 90.7 %collective-permute-start.14 = (bf16[512,2048]{1,0:T(8,128)(2,1)}, bf16[512,2048]{1,0:T(8,128)(2,1)}, u32[]{:S(2)}, u32[]{:S(2)}) collective-permute-start(bf16[512,2048]{1,0:T(8,128)(2,1)} %add_convert_fusion.3), channel_id=1, source_target_pairs={{0,2},{1,3},{2,0},{3,1},{4,6},{5,7},{6,4},{7,5},{8,10},{9,11},{10,... | collective-permute-start | bytes 6291464 | tf_op jit(solution)/shard_map/ppermute | solution.py:553
  1324.9 89.2 %collective-permute-start.18 = (bf16[512,2048]{1,0:T(8,128)(2,1)S(1)}, bf16[512,2048]{1,0:T(8,128)(2,1)S(1)}, u32[]{:S(2)}, u32[]{:S(2)}) collective-permute-start(bf16[512,2048]{1,0:T(8,128)(2,1)S(1)} %add_convert_fusion.2), channel_id=1, source_target_pairs={{0,2},{1,3},{2,0},{3,1},{4,6},{5,7},{6,4},{7,5},{8,10},{9,11},{10,... | collective-permute-start | bytes 6291464 | tf_op jit(solution)/shard_map/ppermute | solution.py:553
  1374.9 54.1 %collective-permute-start.15 = (bf16[1024,2048]{1,0:T(8,128)(2,1)}, bf16[1024,2048]{1,0:T(8,128)(2,1)}, u32[]{:S(2)}, u32[]{:S(2)}) collective-permute-start(bf16[1024,2048]{1,0:T(8,128)(2,1)} %pad_maximum_fusion), channel_id=1, source_target_pairs={{0,1},{1,0},{2,3},{3,2},{4,5},{5,4},{6,7},{7,6},{8,9},{9,8},{10,11... | collective-permute-start | bytes 12582920 | tf_op jit(solution)/shard_map/ppermute | solution.py:553
  1417.8 111.6 %collective-permute-start.19 = (bf16[1024,2048]{1,0:T(8,128)(2,1)}, bf16[1024,2048]{1,0:T(8,128)(2,1)}, u32[]{:S(2)}, u32[]{:S(2)}) collective-permute-start(bf16[1024,2048]{1,0:T(8,128)(2,1)} %pad_maximum_fusion.1), channel_id=1, source_target_pairs={{0,1},{1,0},{2,3},{3,2},{4,5},{5,4},{6,7},{7,6},{8,9},{9,8},{10,11... | collective-permute-start | bytes 12582920 | tf_op jit(solution)/shard_map/ppermute | solution.py:553
  1439.0 87.1 %collective-permute-start.5 = (bf16[512,512]{1,0:T(8,128)(2,1)}, bf16[512,512]{1,0:T(8,128)(2,1)S(1)}, u32[]{:S(2)}, u32[]{:S(2)}) collective-permute-start(bf16[512,512]{1,0:T(8,128)(2,1)} %dynamic-slice_convert_fusion.7), channel_id=1, source_target_pairs={{0,2},{1,3},{2,0},{3,1},{4,6},{5,7},{6,4},{7,5},{8,10},{9,11},{10,... | collective-permute-start | bytes 1572872 | tf_op jit(solution)/shard_map/ppermute | solution.py:553
  (134 other events, 2679.6 us)
Sparse Core Ops, SparseCore 0:
  10.3 47.9 all-gather.24
  60.4 44.6 all-gather.28
  107.3 26.5 all-gather.14
  135.3 58.2 all-gather.26
  195.0 58.2 all-gather.30
  464.7 100.3 reduce-scatter.12
  589.8 15.6 reduce-scatter.14
  619.1 28.5 all-gather.16
  660.2 26.5 reduce-scatter.16
  717.1 15.6 reduce-scatter.18
  745.6 28.5 all-gather.18
  789.8 26.6 reduce-scatter.20
  846.7 15.6 reduce-scatter.22
  875.7 28.4 all-gather.20
  919.9 26.5 reduce-scatter.24
  977.5 15.6 reduce-scatter.26
  1008.0 28.5 all-gather.22
  1059.8 26.6 reduce-scatter.28
  1142.4 15.0 reduce-scatter.30
  1166.1 86.9 all-reduce.3
  1257.6 93.1 all-reduce.5
  1353.7 76.6 reduce-scatter.32
  1433.3 77.2 reduce-scatter.34

commit v3 on v2

--- a/solution.py
+++ b/solution.py
@@ -517,35 +517,366 @@
     )(tokens, w_q, w_o, w_up, w_dn, w_kv, vecs, up_bias, pair_bias)
 
 
-def from_behind(block, axis, distance):
-    devices = range(lax.axis_size(axis))
-    route = [(i - distance, i) for i in devices if i - distance in devices]
-    return lax.ppermute(block, axis, route)
-
-
-def layer_norm(values, gain_vec, bias_vec):
-    row_mean = jnp.mean(values, axis=-1, keepdims=True)
-    centred = values - row_mean
-    row_var = jnp.mean(centred * centred, axis=-1, keepdims=True)
-    return centred * lax.rsqrt(row_var + 1e-05) * gain_vec + bias_vec
-
-
-def gelu_tanh(values):
-    return jax.nn.gelu(values, approximate=True)
+def norm_back(v, gain, grad):
+    unit, rstd = normalize(v)
+    scaled = grad * gain
+    mean_one = jnp.mean(scaled, axis=-1, keepdims=True)
+    mean_two = jnp.mean(scaled * unit, axis=-1, keepdims=True)
+    back = rstd * (scaled - mean_one - unit * mean_two)
+    return back, jnp.sum(grad * unit, axis=0, keepdims=True), jnp.sum(grad, axis=0, keepdims=True)
+
+
+def backward_kernel(
+    cfg,
+    cot,
+    inputs,
+    hidden,
+    query,
+    lse,
+    kv,
+    vecs,
+    w_kv,
+    slope_hbm,
+    w_dn_hbm,
+    w_up_hbm,
+    w_o_hbm,
+    w_q_hbm,
+    branch_out,
+    gq_out,
+    pairs_out,
+    input_grad,
+    common,
+    up_sum,
+    mlp_hbm,
+    pre_hbm,
+    w_dn,
+    w_up,
+    w_o,
+    w_q,
+    go,
+    gn,
+    slope,
+    gpre,
+    p_ref,
+    g_ref,
+    gk,
+    gv,
+    k_t,
+    ga,
+    inbox,
+    hand,
+    pair_send,
+    pair_recv,
+    g,
+    terms,
+    sum_r,
+    sum_l,
+    in_l,
+    in_r,
+    gs_r,
+    gs_l,
+    g_recv,
+    rs_r,
+    rs_l,
+    rr_l,
+    rr_r,
+    w_sem,
+    ps_sem,
+    pr_sem,
+    keep_sem,
+    slope_sem,
+    hand_send,
+    hand_recv,
+):
+    n, nb, own, chunks, rows, tile = (cfg[k] for k in ("n", "nb", "own", "chunks", "rows", "tile"))
+    per = cfg["per"]
+    dim = go.shape[1]
+    ff = w_up.shape[1]
+    width = w_q.shape[1]
+    heads = width // HD
+    block = n * own
+    me = lax.axis_index("tensor")
+    sec = lax.axis_index("section")
+    scale = 1.0 / math.sqrt(HD)
+    loads = [
+        pltpu.make_async_copy(src, dst, w_sem.at[k])
+        for k, (src, dst) in enumerate(((w_dn_hbm, w_dn), (w_up_hbm, w_up), (w_o_hbm, w_o), (w_q_hbm, w_q)))
+    ]
+    for load in loads:
+        load.start()
+    greet(n)
+    gk[...] = jnp.zeros_like(gk)
+    gv[...] = jnp.zeros_like(gv)
+    common[...] = jnp.zeros_like(common)
+    up_sum[...] = jnp.zeros_like(up_sum)
+    for kb in range(nb):
+        k_t[kb] = kv[kb * block : (kb + 1) * block, :HD].astype(F32).T.astype(BF16)
+
+    def pair_copy(k):
+        target = lax.rem(me + k, n)
+        return pltpu.make_async_remote_copy(
+            src_ref=pair_send.at[aligned(target * own, own)],
+            dst_ref=pair_recv.at[k],
+            send_sem=ps_sem.at[k],
+            recv_sem=pr_sem.at[k],
+            device_id={"tensor": target},
+            device_id_type=MESH,
+        )
+
+    def hand_copy(b):
+        return pltpu.make_async_remote_copy(
+            src_ref=hand,
+            dst_ref=inbox.at[b],
+            send_sem=hand_send,
+            recv_sem=hand_recv.at[b],
+            device_id={"section": 1 - sec},
+            device_id_type=MESH,
+        )
+
+    def keep_copies(b, c):
+        return [
+            pltpu.make_async_copy(g.at[c], mlp_hbm.at[b, c], keep_sem.at[0, c]),
+            pltpu.make_async_copy(gpre.at[c], pre_hbm.at[b, c], keep_sem.at[1, c]),
+        ]
+
+    def block_step(i, carry):
+        b = nb - 1 - i
+        slope_load = pltpu.make_async_copy(slope_hbm.at[b], slope, slope_sem)
+        slope_load.start()
+
+        @pl.when(sec == 1)
+        def _():
+            go[...] = cot[b].astype(F32)
+
+        @pl.when(sec != 1)
+        def _():
+            hand_copy(b).wait_recv()
+            go[...] = inbox[b].astype(F32)
+
+        common[5:6, :dim] += jnp.sum(go[...], axis=0, keepdims=True)
+        for c in range(chunks):
+            g[c, aligned(me * rows, rows)] = go[c * rows : (c + 1) * rows].astype(BF16)
+        slope_load.wait()
+
+        @pl.when(i == 0)
+        def _():
+            loads[0].wait()
+            loads[1].wait()
+
+        def compute(c):
+            def act_tile(t, carry):
+                cols = aligned(t * tile, tile)
+                grad = (dot_t(g[c], w_dn[cols]) * slope[c, :, cols].astype(F32)).astype(BF16)
+                gpre[c, :, cols] = grad
+                up_sum[:, cols] += jnp.sum(grad.astype(F32), axis=0, keepdims=True)
+                return carry
+
+            lax.fori_loop(0, ff // tile, act_tile, 0)
+
+            def back_tile(t, carry):
+                cols = aligned(t * tile, tile)
+                terms[c, :, cols] = dot_t(gpre[c], w_up[cols])
+                return carry
+
+            lax.fori_loop(0, dim // tile, back_tile, 0)
+            for copy in keep_copies(b, c):
+                copy.start()
+
+        def finish(c, what):
+            for copy in keep_copies(b, c):
+                copy.wait()
+
+        line_rounds(
+            n,
+            chunks,
+            rows,
+            {
+                "refs": (g, terms, sum_r, sum_l, in_l, in_r),
+                "sems": (gs_r, gs_l, g_recv, rs_r, rs_l, rr_l, rr_r),
+            },
+            compute,
+            finish,
+        )
+        for c in range(chunks):
+            gn[c * rows : (c + 1) * rows] = terms[c, aligned(me * rows, rows)]
+        back, gain_sum, bias_sum = norm_back(hidden[b], vecs[2:3], gn[...])
+        common[3:4, :dim] += gain_sum
+        common[4:5, :dim] += bias_sum
+        go[...] += back
+        common[2:3, :dim] += jnp.sum(go[...], axis=0, keepdims=True)
+        branch_out[b] = go[...].astype(BF16)
+
+        @pl.when(i == 0)
+        def _():
+            loads[2].wait()
+
+        def att_tile(t, carry):
+            grad = dot_t(branch_out[b], w_o[aligned(t * tile, tile)]).astype(BF16)
+            for k in range(tile // HD):
+                ga[aligned((t * (tile // HD) + k) * own, own)] = grad[:, k * HD : (k + 1) * HD]
+            return carry
+
+        lax.fori_loop(0, width // tile, att_tile, 0)
+
+        def head_tile(t, carry):
+            here = aligned(t * per * own, per * own)
+            q = query[b, here]
+            grad = ga[here]
+            log_total = lse[b, t]
+
+            def first(kb, inner):
+                keys = aligned(kb * block, block)
+                prob = jnp.exp(dot_t(kv[keys, :HD], q) * scale - log_total)
+                grad_prob = dot_t(kv[keys, HD:], grad)
+                p_ref[kb] = prob
+                g_ref[kb] = grad_prob
+                return inner + jnp.sum(prob * grad_prob, axis=0, keepdims=True)
+
+            inner = lax.fori_loop(0, b + 1, first, jnp.zeros((1, per * own), F32))
+
+            def second(kb, acc):
+                keys = aligned(kb * block, block)
+                prob = p_ref[kb]
+                grad_score = (prob * (g_ref[kb] - inner)).astype(BF16)
+                gk[keys] += dot(grad_score, q)
+                gv[keys] += dot(prob.astype(BF16), grad)
+                return acc + dot(k_t[kb], grad_score)
+
+            acc = lax.fori_loop(0, b + 1, second, jnp.zeros((HD, per * own), F32))
+            back = (acc * scale).T.astype(BF16)
+            for k in range(per):
+                gq_out[b, :, aligned((t * per + k) * HD, HD)] = back[k * own : (k + 1) * own]
+            return carry
+
+        lax.fori_loop(0, heads // per, head_tile, 0)
+        here = aligned(b * block, block)
+        pair_send[:, :HD] = (gk[here] * scale).astype(BF16)
+        pair_send[:, HD:] = gv[here].astype(BF16)
+        for k in range(1, n):
+            pair_copy(k).start()
+        common[6:7, :width] += jnp.sum(gq_out[b].astype(F32), axis=0, keepdims=True)
+
+        @pl.when(i == 0)
+        def _():
+            loads[3].wait()
+
+        def normed_tile(t, carry):
+            cols = aligned(t * tile, tile)
+            gn[:, cols] = dot_t(gq_out[b], w_q[cols])
+            return carry
+
+        lax.fori_loop(0, dim // tile, normed_tile, 0)
+        mine = aligned(b * block + me * own, own)
+        total_k = gk[mine] * scale
+        total_v = gv[mine]
+        for k in range(1, n):
+            pair_copy(k).wait_recv()
+            total_k += pair_recv[k, :, :HD].astype(F32)
+            total_v += pair_recv[k, :, HD:].astype(F32)
+        pairs_out[b, :, :HD] = total_k.astype(BF16)
+        pairs_out[b, :, HD:] = total_v.astype(BF16)
+        common[7:8, : 2 * HD] += jnp.sum(pairs_out[b].astype(F32), axis=0, keepdims=True)
+
+        def pair_tile(t, carry):
+            cols = aligned(t * tile, tile)
+            gn[:, cols] += dot_t(pairs_out[b], w_kv[cols])
+            return carry
+
+        lax.fori_loop(0, dim // tile, pair_tile, 0)
+        back, gain_sum, bias_sum = norm_back(inputs[b].astype(F32), vecs[0:1], gn[...])
+        common[0:1, :dim] += gain_sum
+        common[1:2, :dim] += bias_sum
+        go[...] += back
+        input_grad[b] = go[...]
+        for k in range(1, n):
+            pair_copy(k).wait_send()
+
+        @pl.when(sec == 1)
+        def _():
+            @pl.when(i > 0)
+            def _():
+                hand_copy(b).wait_send()
+
+            hand[...] = go[...].astype(BF16)
+            hand_copy(b).start()
+
+        return carry
+
+    lax.fori_loop(0, nb, block_step, 0)
+
+    @pl.when(sec == 1)
+    def _():
+        hand_copy(0).wait_send()
+
+
+def backward(cot, inputs, hidden, query, lse, kv, vecs, w_kv, slope, w_dn, w_up, w_o, w_q):
+    n = lax.axis_size("tensor")
+    nb, own, dim = cot.shape
+    chunks, rows = slope.shape[1], own // slope.shape[1]
+    ff = w_up.shape[1]
+    width = w_q.shape[1]
+    heads = width // HD
+    tile = min(512, dim, ff)
+    per = lse.shape[3] // own
+    block = n * own
+    cfg = dict(n=n, nb=nb, own=own, chunks=chunks, rows=rows, tile=tile, per=per)
+    S = jax.ShapeDtypeStruct
+    vmem = pl.BlockSpec(memory_space=pltpu.VMEM)
+    hbm = pl.BlockSpec(memory_space=pl.ANY)
+    line_refs, line_sems = line_scratch(n, chunks, rows, dim)
+    dma = pltpu.SemaphoreType.DMA
+    return pl.pallas_call(
+        functools.partial(backward_kernel, cfg),
+        name="backward",
+        out_shape=(
+            S((nb, own, dim), BF16),
+            S((nb, own, width), BF16),
+            S((nb, own, 2 * HD), BF16),
+            S((nb, own, dim), F32),
+            S((8, max(dim, width)), F32),
+            S((1, ff), F32),
+            S((nb, chunks, n * rows, dim), BF16),
+            S((nb, chunks, n * rows, ff), BF16),
+        ),
+        in_specs=[vmem] * 8 + [hbm] * 5,
+        out_specs=(vmem,) * 6 + (hbm,) * 2,
+        scratch_shapes=[
+            pltpu.VMEM((ff, dim), BF16),
+            pltpu.VMEM((dim, ff), BF16),
+            pltpu.VMEM((width, dim), BF16),
+            pltpu.VMEM((dim, width), BF16),
+            pltpu.VMEM((own, dim), F32),
+            pltpu.VMEM((own, dim), F32),
+            pltpu.VMEM((chunks, n * rows, ff), BF16),
+            pltpu.VMEM((chunks, n * rows, ff), BF16),
+            pltpu.VMEM((nb, block, per * own), F32),
+            pltpu.VMEM((nb, block, per * own), F32),
+            pltpu.VMEM((nb * block, HD), F32),
+            pltpu.VMEM((nb * block, HD), F32),
+            pltpu.VMEM((nb, HD, block), BF16),
+            pltpu.VMEM((heads * own, HD), BF16),
+            pltpu.VMEM((nb, own, dim), BF16),
+            pltpu.VMEM((own, dim), BF16),
+            pltpu.VMEM((block, 2 * HD), BF16),
+            pltpu.VMEM((n, own, 2 * HD), BF16),
+            *line_refs,
+            *line_sems,
+            dma((4,)),
+            dma((n,)),
+            dma((n,)),
+            dma((2, chunks)),
+            dma(()),
+            dma(()),
+            dma((nb,)),
+        ],
+        compiler_params=pltpu.CompilerParams(
+            collective_id=2, has_side_effects=True, vmem_limit_bytes=67000000
+        ),
+    )(cot, inputs, hidden, query, lse, kv, vecs, w_kv, slope, w_dn, w_up, w_o, w_q)
 
 
 def t_dot(a, b):
     return lax.dot_general(a, b, (((0,), (0,)), ((), ())), preferred_element_type=F32)
-
-
-def gather_rows(own_rows):
-    return lax.all_gather(own_rows, "tensor", axis=0, tiled=True)
-
-
-def sum_rows(partial):
-    return lax.psum_scatter(
-        partial.astype(BF16), "tensor", scatter_dimension=0, tiled=True
-    ).astype(F32)
 
 
 def swap(value, distance):
@@ -612,7 +943,6 @@
     down_weight,
     down_bias,
 ):
-    section = lax.axis_index("section")
     tensor_count = lax.axis_size("tensor")
     tensor_rank = lax.axis_index("tensor")
     gain_one = ln1_gain[0].astype(F32)
@@ -630,25 +960,11 @@
     assert seq_count == 1
     tokens_in = tokens_in[:, :, 0]
     cotangent = cotangent[:, :, 0]
-    block_len = own_count * tensor_count
-    total_len = blocks * block_len
     w_query = whole_weight(q_weight[0], 0, 1)
     w_out = whole_weight(o_weight[0], 1, 0)
     b_query = lax.all_gather(q_bias[0], "tensor", axis=0, tiled=True).astype(F32)
-    heads = w_query.shape[1] // HD
-    width = heads * HD
+    width = w_query.shape[1]
     ff_local = w_up.shape[1]
-    score_scale = 1.0 / math.sqrt(HD)
-    positions = jnp.arange(total_len, dtype=jnp.int32)
-
-    def zeros(shape, dtype):
-        return jnp.zeros(shape, dtype)
-
-    def put(kept, value, index):
-        return lax.dynamic_update_index_in_dim(kept, value, index, 0)
-
-    def take(kept, index):
-        return lax.dynamic_index_in_dim(kept, index, 0, keepdims=False)
 
     vecs = jnp.stack([gain_one, bias_one, gain_two, bias_two, b_out, b_down, b_query, b_query])
     (
@@ -666,107 +982,49 @@
     ) = forward(
         tokens_in, w_query, w_out, w_up, w_down, w_pairs, vecs, b_up[None], pair_bias[None]
     )
-    chunks, chunk_rows = kept_active.shape[1], own_count // kept_active.shape[1]
-    kept_query = kept_query.reshape(blocks, heads, own_count, HD)
-    kept_logsum = kept_logsum.reshape(blocks, heads, own_count)
-    kept_input = kept_input.astype(F32)
-    kept_normed_two = kept_normed_two.reshape(blocks, block_len, model_dim)
-    kept_active = kept_active.reshape(blocks, block_len, ff_local)
-    kept_slope = kept_slope.reshape(blocks, block_len, ff_local)
-
-    def to_chunks(rows):
-        rows = rows.reshape(tensor_count, chunks, chunk_rows, -1)
-        return rows.transpose(1, 0, 2, 3).reshape(block_len, -1)
-
-    def from_chunks(rows):
-        rows = rows.reshape(chunks, tensor_count, chunk_rows, -1)
-        return rows.transpose(1, 0, 2, 3).reshape(block_len, -1)
-
-    key_rows = kv_cache[:, :HD]
-    value_rows = kv_cache[:, HD:]
-    kept_grad_mlp = zeros((blocks + 1, block_len, model_dim), BF16)
-    kept_grad_pre = zeros((blocks + 1, block_len, ff_local), BF16)
-    kept_branch = zeros((blocks + 1, own_count, model_dim), BF16)
-    kept_grad_query = zeros((blocks + 1, own_count, width), BF16)
-    kept_grad_pairs = zeros((blocks + 1, own_count, 2 * HD), BF16)
-    input_grads = zeros((blocks + 1, own_count, model_dim), F32)
-    pair_grad_acc = zeros((total_len, 2 * HD), F32)
-    received_back = zeros((own_count, model_dim), F32)
-    common = [zeros((model_dim,), F32) for _ in range(6)]
-    for turn in range(blocks + 1):
-        step_count = turn - (1 - section)
-        valid = (step_count >= 0) & (step_count < blocks)
-        block_index = blocks - 1 - jnp.clip(step_count, 0, blocks - 1)
-        slot = jnp.where(valid, block_index, blocks)
-        grad_out = jnp.where(section == 1, take(cotangent, block_index).astype(F32), received_back)
-        grad_out = grad_out * valid.astype(F32)
-        grad_mlp = to_chunks(gather_rows(grad_out.astype(BF16)))
-        grad_active = dot_t(grad_mlp, w_down)
-        grad_pre = (grad_active * take(kept_slope, block_index).astype(F32)).astype(BF16)
-        grad_normed_two = sum_rows(from_chunks(dot_t(grad_pre, w_up)))
-        norm_back_two = jax.vjp(layer_norm, take(kept_hidden, block_index), gain_two, bias_two)[1]
-        grad_hidden_norm, gain_two_term, bias_two_term = norm_back_two(grad_normed_two)
-        grad_hidden = grad_out + grad_hidden_norm
-        branch = grad_hidden.astype(BF16)
-        grad_attended = dot_t(branch, w_out).astype(BF16).reshape(own_count * heads, HD)
-        query_rows = take(kept_query, block_index).transpose(1, 0, 2).reshape(own_count * heads, HD)
-        log_total = take(kept_logsum, block_index).T.reshape(-1)
-        visible = positions < (block_index + 1) * block_len
-        scores = dot_t(query_rows, key_rows) * score_scale
-        scores = jnp.where(visible, scores, -1e30)
-        probabilities = jnp.exp(scores - log_total[:, None])
-        grad_probs = dot_t(grad_attended, value_rows)
-        row_inner = jnp.sum(probabilities * grad_probs, axis=-1, keepdims=True)
-        grad_scores = (probabilities * (grad_probs - row_inner)).astype(BF16)
-        grad_query = (dot(grad_scores, key_rows) * score_scale).astype(BF16)
-        grad_query = grad_query.reshape(own_count, width)
-        grad_keys = t_dot(grad_scores, query_rows) * score_scale
-        grad_values = t_dot(probabilities.astype(BF16), grad_attended)
-        pair_grad_acc = pair_grad_acc + jnp.concatenate([grad_keys, grad_values], axis=-1)
-        block_pairs = lax.dynamic_slice_in_dim(pair_grad_acc, block_index * block_len, block_len, 0)
-        grad_pairs = sum_rows(block_pairs).astype(BF16)
-        grad_normed = dot_t(grad_query, w_query) + dot_t(grad_pairs, w_pairs)
-        norm_back_one = jax.vjp(layer_norm, take(kept_input, block_index), gain_one, bias_one)[1]
-        grad_input_norm, gain_one_term, bias_one_term = norm_back_one(grad_normed)
-        grad_input = grad_hidden + grad_input_norm
-        if turn < blocks:
-            received_back = from_behind(grad_input.astype(BF16), "section", -1).astype(F32)
-        scale = valid.astype(F32)
-        terms = (
-            gain_one_term * scale,
-            bias_one_term * scale,
-            jnp.sum(grad_hidden, axis=0),
-            gain_two_term,
-            bias_two_term,
-            jnp.sum(grad_out, axis=0),
-        )
-        common = [total + term for total, term in zip(common, terms)]
-        input_grads = put(input_grads, grad_input, slot)
-        kept_grad_mlp = put(kept_grad_mlp, grad_mlp, slot)
-        kept_grad_pre = put(kept_grad_pre, grad_pre, slot)
-        kept_branch = put(kept_branch, branch, slot)
-        kept_grad_query = put(kept_grad_query, grad_query, slot)
-        kept_grad_pairs = put(kept_grad_pairs, grad_pairs, slot)
+    (
+        kept_branch,
+        kept_grad_query,
+        kept_grad_pairs,
+        input_grads,
+        common,
+        up_b,
+        kept_grad_mlp,
+        kept_grad_pre,
+    ) = backward(
+        cotangent,
+        kept_input,
+        kept_hidden,
+        kept_query,
+        kept_logsum,
+        kv_cache,
+        vecs,
+        w_pairs,
+        kept_slope,
+        w_down,
+        w_up,
+        w_out,
+        w_query,
+    )
 
     def flat(kept):
-        return kept[:blocks].reshape(-1, kept.shape[-1])
+        return kept.reshape(-1, kept.shape[-1])
 
     down_w = t_dot(flat(kept_active), flat(kept_grad_mlp))
     up_w = t_dot(flat(kept_normed_two), flat(kept_grad_pre))
-    up_b = jnp.sum(flat(kept_grad_pre).astype(F32), axis=0)
     out_w = t_dot(flat(kept_attended), flat(kept_branch))
     query_w = t_dot(flat(kept_normed), flat(kept_grad_query))
-    query_b = jnp.sum(flat(kept_grad_query).astype(F32), axis=0)
     pair_w = t_dot(flat(kept_normed), flat(kept_grad_pairs))
-    value_b = jnp.sum(flat(kept_grad_pairs)[:, HD:].astype(F32), axis=0)
     down_w = sum_dp(down_w, 0)
     up_w = sum_dp(up_w, 0)
     out_w = sum_dp(out_w, 1, 0)
     query_w = sum_dp(query_w, 0, 1)
     pair_w = lax.psum(pair_w.astype(BF16), ("tensor", "dp")).astype(F32)
     wide = jnp.zeros((tensor_count, ff_local), F32)
-    wide = lax.dynamic_update_index_in_dim(wide, up_b, tensor_rank, 0)
-    packed = jnp.concatenate([*common, query_b, value_b, wide.reshape(-1)])
+    wide = lax.dynamic_update_index_in_dim(wide, up_b[0], tensor_rank, 0)
+    packed = jnp.concatenate(
+        [common[:6, :model_dim].reshape(-1), common[6, :width], common[7, HD : 2 * HD], wide.reshape(-1)]
+    )
     packed = lax.psum(packed, ("tensor", "dp"))
     vecs = packed[: 6 * model_dim].reshape(6, model_dim)
     own_query = lax.dynamic_slice_in_dim(
@@ -778,7 +1036,7 @@
     )
     return (
         outputs[None, :, :, None],
-        input_grads[None, :blocks, :, None],
+        input_grads[None, :, :, None],
         vecs[0][None],
         vecs[1][None],
         query_w[None],

time: 1590 us -> 1260 us (0.79)
  Pallas kernels: 200 us -> 561 us
  waiting for transfers between devices: 769 us -> 411 us
  matrix products: 231 us -> 34.9 us
  local copies, waits for them, and re-layouts: 148 us -> 48.5 us
  other arithmetic: 178 us -> 105 us
  starting transfers between devices: 29.8 us -> 71.1 us
    pallas_call x0 -> x1, Pallas kernels: none -> 360 us  [backward(): pl.pallas_call(functools.partial(backward_kernel, cfg), name='backward',...]
    reduce_scatter x10 -> x0, waiting for transfers between devices: 187 us -> none  [sum_rows(): lax.psum_scatter(partial.astype(BF16), 'tensor', scatter_dimension=0, til...]
    dot_general x40 -> x0, matrix products: 178 us -> none  [the longest x35 171 us: dot_t(): lax.dot_general(a, b, (((1,), (1,)), ((), ())), preferred_element_type=F32)]
    all_gather x5 -> x0, waiting for transfers between devices: 117 us -> none  [gather_rows(): return lax.all_gather(own_rows, 'tensor', axis=0, tiled=True)]
    ppermute x16, starting transfers between devices: 22.3 us -> 70.6 us  [swap(): return lax.ppermute(value, 'dp', [(i, i ^ distance) for i in range(size)])]
    reduce_sum x28 -> x0, other arithmetic: 41.5 us -> none  [the longest x5 10.7 us: layer_norm(): return centred * lax.rsqrt(row_var + 1e-05) * gain_vec + bias_vec]
    reshape x16 -> x1, local copies, waits for them, and re-layouts: 21.8 us -> 0.86 us  [on_device(): common[:6, :model_dim].reshape(-1)]
    dynamic_update_slice x16 -> x1, local copies, waits for them, and re-layouts: 20.6 us -> 0.82 us  [on_device(): wide = lax.dynamic_update_index_in_dim(wide, up_b[0], tensor_rank, 0)]
  transfers between devices with their start and end apart: 43 -> 24, of which waited for: 30 -> 10; matrix products, arithmetic and copies ran while one was open for 19% -> 13% of each run, Pallas kernels for 0% -> 0%
where the time goes in v3:
time: 1260 us
  Pallas kernels  561 us (45%)
  waiting for transfers between devices  411 us (33%)
  other arithmetic  105 us (8%)
  starting transfers between devices  71.1 us (6%)
  local copies, waits for them, and re-layouts  48.5 us (4%)
  matrix products  34.9 us (3%)
  between operations  14.8 us (1%)
    pallas_call x1, Pallas kernels, backward(): pl.pallas_call(functools.partial(backward_kernel, cfg), name='backward',...  360 us
    pallas_call x1, Pallas kernels, forward(): pl.pallas_call(functools.partial(forward_kernel, cfg), name='forward', ou...  200 us
    ppermute x16, waiting for transfers between devices, swap(): return lax.ppermute(value, 'dp', [(i, i ^ distance) for i in range(size)])  153 us
    all_gather x2, waiting for transfers between devices, whole_weight(): return lax.all_gather(own, 'dp', axis=split, tiled=True)  107 us
    all_gather x2, waiting for transfers between devices, whole_weight(): own = lax.all_gather(own, 'tensor', axis=join, tiled=True)  93.8 us
    ppermute x16, starting transfers between devices, swap(): return lax.ppermute(value, 'dp', [(i, i ^ distance) for i in range(size)])  70.6 us
    reduce_scatter x2, waiting for transfers between devices, sum_dp(): lax.psum_scatter(value.astype(BF16), 'tensor', scatter_dimension=scatter,...  57.3 us
    dot_general x5, matrix products, t_dot(): lax.dot_general(a, b, (((0,), (0,)), ((), ())), preferred_element_type=F32)  34.9 us
  transfers between devices with their start and end apart: 24, of which 10 were waited for; matrix products, arithmetic and copies ran while one was open for 13% of the time, Pallas kernels for 0%

profile of v3, /device:TPU:1, one launch (start us, length us, event | category | flops | bytes accessed | tf_op | source)
XLA Modules:
  0.0 1256.0 jit_solution(9586560198409294054)
XLA Ops:
  11.2 47.0 %all-gather.10.cloned.1.call-done = bf16[1,512,2048]{2,1,0:T(8,128)(2,1)} async-done(((bf16[1,512,512]{2,1,0:T(8,128)(2,1)}), bf16[1,512,2048]{2,1,0:T(8,128)(2,1)}) %all-gather.10.cloned.1.call-update) | async-done | bytes 2097168 | tf_op jit(solution)/shard_map/all_gather | solution.py:924
  58.3 46.8 %all-gather.14.cloned.1.call-done = bf16[1,2048,512]{2,1,0:T(8,128)(2,1)} async-done(((bf16[1,512,512]{2,1,0:T(8,128)(2,1)}), bf16[1,2048,512]{2,1,0:T(8,128)(2,1)}) %all-gather.14.cloned.1.call-update) | async-done | bytes 2097168 | tf_op jit(solution)/shard_map/all_gather | solution.py:924
  105.2 9.3 all-gather.4
  116.5 47.7 %all-gather.12.cloned.1.call-done = bf16[1,2048,2048]{2,1,0:T(8,128)(2,1)} async-done(((bf16[1,512,2048]{2,1,0:T(8,128)(2,1)}), bf16[1,2048,2048]{2,1,0:T(8,128)(2,1)}) %all-gather.12.cloned.1.call-update) | async-done | bytes 8388624 | tf_op jit(solution)/shard_map/all_gather | solution.py:925
  164.2 59.7 %all-gather.16.cloned.1.call-done = bf16[1,2048,2048]{2,1,0:T(8,128)(2,1)} async-done(((bf16[1,2048,512]{2,1,0:T(8,128)(2,1)}), bf16[1,2048,2048]{2,1,0:T(8,128)(2,1)}) %all-gather.16.cloned.1.call-update) | async-done | bytes 8388624 | tf_op jit(solution)/shard_map/all_gather | solution.py:925
  223.9 200.3 %forward.1 = (bf16[4,64,2048]{2,1,0:T(8,128)(2,1)}, bf16[4,1024,128]{2,1,0:T(8,128)(2,1)}, bf16[4,64,2048]{2,1,0:T(8,128)(2,1)}, f32[4,4,1,256]{3,2,1,0:T(1,128)...) custom-call(bf16[4,64,2048]{2,1,0:T(8,128)(2,1)} %bitcast.86, ...), custom_call_target="tpu_custom_call" | custom-call | tf_op jit(solution)/shard_map/forward/pallas_call | solution.py:475
  424.2 360.4 %backward.1 = (bf16[4,64,2048]{2,1,0:T(8,128)(2,1)}, bf16[4,64,2048]{2,1,0:T(8,128)(2,1)}, bf16[4,64,256]{2,1,0:T(8,128)(2,1)}, f32[4,64,2048]{2,1,0:T(8,128)}, ...) custom-call(bf16[4,64,2048]{2,1,0:T(8,128)(2,1)} %bitcast.87, ...), custom_call_target="tpu_custom_call" | custom-call | tf_op jit(solution)/shard_map/backward/pallas_call | solution.py:828
  788.8 3.9 convolution_bitcast_fusion.1
  795.4 48.5 %collective-permute-start = (bf16[1024,2048]{1,0:T(8,128)(2,1)}, bf16[1024,2048]{1,0:T(8,128)(2,1)}, u32[]{:S(2)}, u32[]{:S(2)}) collective-permute-start(bf16[1024,2048]{1,0:T(8,128)(2,1)} %dynamic-slice_convert_fusion.3), channel_id=1, source_target_pairs={{0,1},{1,0},{2,3},{3,2},{4,5},{5,4},{6,7},{7,6},{8,9},{9,8},{10,11... | collective-permute-start | bytes 12582920 | tf_op jit(solution)/shard_map/ppermute | solution.py:884
  844.0 14.3 %convolution_bitcast_fusion.2 = f32[2048,2048]{1,0:T(8,128)} fusion(bf16[4,4,64,2048]{3,2,1,0:T(8,128)(2,1)S(1)} %copy-done.22, bf16[4,4,64,2048]{3,2,1,0:T(8,128)(2,1)} %get-tuple-element.53), kind=kOutput, calls=%fused_computation.2 | convolution fusion | flops 8589934592 | bytes 25165824 | tf_op jit(solution)/shard_map/dot_general | solution.py:879
  858.3 6.2 dynamic-slice_convert_fusion
  866.0 4.1 collective-permute-start.12
  870.2 8.4 add_convert_fusion.1
  878.6 12.7 %convolution_bitcast_fusion.3 = f32[2048,2048]{1,0:T(8,128)S(1)} fusion(bf16[4,4,64,2048]{3,2,1,0:T(8,128)(2,1)} %get-tuple-element.50, bf16[4,4,64,2048]{3,2,1,0:T(8,128)(2,1)} %get-tuple-element.51), kind=kOutput, calls=%fused_computation.3 | convolution fusion | flops 8589934592 | bytes 25165824 | tf_op jit(solution)/shard_map/dot_general | solution.py:879
  894.1 4.9 copy-done.9
  901.3 6.2 copy-done.7
  910.2 5.9 convert_add_fusion
  918.2 10.8 convert_add_fusion.1
  929.0 3.8 dynamic-slice_convert_fusion.5
  934.7 8.4 add_convert_fusion
  943.2 23.5 %collective-permute-done.13 = bf16[512,2048]{1,0:T(8,128)(2,1)} collective-permute-done((bf16[512,2048]{1,0:T(8,128)(2,1)S(1)}, bf16[512,2048]{1,0:T(8,128)(2,1)}, u32[]{:S(2)}, u32[]{:S(2)}) %collective-permute-start.13) | collective-permute-done | bytes 2097184 | tf_op jit(solution)/shard_map/ppermute | solution.py:884
  966.7 3.5 add_convert_fusion.2
  972.3 44.1 %collective-permute-done.9 = bf16[512,2048]{1,0:T(8,128)(2,1)} collective-permute-done((bf16[512,2048]{1,0:T(8,128)(2,1)}, bf16[512,2048]{1,0:T(8,128)(2,1)}, u32[]{:S(2)}, u32[]{:S(2)}) %collective-permute-start.9) | collective-permute-done | bytes 2097184 | tf_op jit(solution)/shard_map/ppermute | solution.py:884
  1016.4 3.7 add_convert_fusion.3
  1021.2 40.2 %collective-permute-done.14 = bf16[512,2048]{1,0:T(8,128)(2,1)} collective-permute-done((bf16[512,2048]{1,0:T(8,128)(2,1)S(1)}, bf16[512,2048]{1,0:T(8,128)(2,1)}, u32[]{:S(2)}, u32[]{:S(2)}) %collective-permute-start.14) | collective-permute-done | bytes 2097184 | tf_op jit(solution)/shard_map/ppermute | solution.py:884
  1068.4 38.0 %collective-permute-done.10 = bf16[512,2048]{1,0:T(8,128)(2,1)} collective-permute-done((bf16[512,2048]{1,0:T(8,128)(2,1)}, bf16[512,2048]{1,0:T(8,128)(2,1)}, u32[]{:S(2)}, u32[]{:S(2)}) %collective-permute-start.10) | collective-permute-done | bytes 2097184 | tf_op jit(solution)/shard_map/ppermute | solution.py:884
  1113.3 5.2 copy.33
  1129.5 57.3 %reduce-scatter.5.cloned.1.call-done = bf16[512,1024]{1,0:T(8,128)(2,1)} async-done(((bf16[2048,1024]{1,0:T(8,128)(2,1)}), bf16[512,1024]{1,0:T(8,128)(2,1)}) %reduce-scatter.5.cloned.1.call-update) | async-done | bytes 1048592 | tf_op jit(solution)/shard_map/reduce_scatter | solution.py:909
  1189.8 12.0 select_bitcast_fusion.1
  1203.8 11.8 maximum_convert_fusion
  1219.0 6.9 collective-permute-done.6
  1228.9 11.8 maximum_convert_fusion.1
  (140 shorter events, 73.6 us)
Async XLA Ops:
  7.2 107.3 %copy-start.14 = (bf16[1,2048]{1,0:T(2,128)(2,1)S(1)}, bf16[1,2048]{1,0:T(2,128)(2,1)}, u32[]{:S(2)}) copy-start(bf16[1,2048]{1,0:T(2,128)(2,1)} %param.18) | copy-start | bytes 12292
  7.2 107.3 %copy-start.15 = (bf16[1,2048]{1,0:T(2,128)(2,1)S(1)}, bf16[1,2048]{1,0:T(2,128)(2,1)}, u32[]{:S(2)}) copy-start(bf16[1,2048]{1,0:T(2,128)(2,1)} %param.19) | copy-start | bytes 12292
  7.2 107.3 %copy-start.16 = (bf16[1,2048]{1,0:T(2,128)(2,1)S(1)}, bf16[1,2048]{1,0:T(2,128)(2,1)}, u32[]{:S(2)}) copy-start(bf16[1,2048]{1,0:T(2,128)(2,1)} %param.26) | copy-start | bytes 12292
  7.2 107.3 %copy-start.17 = (bf16[1,2048]{1,0:T(2,128)(2,1)S(1)}, bf16[1,2048]{1,0:T(2,128)(2,1)}, u32[]{:S(2)}) copy-start(bf16[1,2048]{1,0:T(2,128)(2,1)} %param.27) | copy-start | bytes 12292
  7.2 107.3 %copy-start.18 = (bf16[1,2048]{1,0:T(2,128)(2,1)S(1)}, bf16[1,2048]{1,0:T(2,128)(2,1)}, u32[]{:S(2)}) copy-start(bf16[1,2048]{1,0:T(2,128)(2,1)} %param.25) | copy-start | bytes 12292
  7.2 107.3 %copy-start.19 = (bf16[1,2048]{1,0:T(2,128)(2,1)S(1)}, bf16[1,2048]{1,0:T(2,128)(2,1)}, u32[]{:S(2)}) copy-start(bf16[1,2048]{1,0:T(2,128)(2,1)} %param.31) | copy-start | bytes 12292
  7.3 108.0 %copy-start.20 = (bf16[1,2048]{1,0:T(2,128)(2,1)S(1)}, bf16[1,2048]{1,0:T(2,128)(2,1)}, u32[]{:S(2)}) copy-start(bf16[1,2048]{1,0:T(2,128)(2,1)} %param.29) | copy-start | bytes 12292
  7.3 108.7 %copy-start.27 = (bf16[1,128]{1,0:T(2,128)(2,1)S(1)}, bf16[1,128]{1,0:T(2,128)(2,1)}, u32[]{:S(2)}) copy-start(bf16[1,128]{1,0:T(2,128)(2,1)} %param.23) | copy-start | bytes 772
  7.3 51.0 %all-gather.10.cloned.1.call-start = ((), (), s32[]{:S(2)}) async-start(), calls=%async_computation.6 | async-start | bytes 2621440 | tf_op jit(solution)/shard_map/all_gather | solution.py:924
  9.2 95.9 %all-gather.14.cloned.1.call-start = ((), (), s32[]{:S(2)}) async-start(), calls=%async_computation.8 | async-start | bytes 2621440 | tf_op jit(solution)/shard_map/all_gather | solution.py:924
  11.2 153.0 %all-gather.12.cloned.1.call-start = ((), (), s32[]{:S(2)}) async-start(), calls=%async_computation.7 | async-start | bytes 10485760 | tf_op jit(solution)/shard_map/all_gather | solution.py:925
  58.3 165.6 %all-gather.16.cloned.1.call-start = ((), (), s32[]{:S(2)}) async-start(), calls=%async_computation.9 | async-start | bytes 10485760 | tf_op jit(solution)/shard_map/all_gather | solution.py:925
  105.2 1013.3 %all-reduce.4.cloned.1.call-start = ((), (), s32[]{:S(2)}) async-start(), calls=%async_computation.2 | async-start | bytes 188416 | tf_op jit(solution)/shard_map/psum | solution.py:1028
  788.6 333.9 %all-reduce.6.cloned.1.call-start = ((), (), s32[]{:S(2)}) async-start(), calls=%async_computation.4 | async-start | bytes 2097152 | tf_op jit(solution)/shard_map/psum | solution.py:1022
  795.4 74.7 %collective-permute-start = (bf16[1024,2048]{1,0:T(8,128)(2,1)}, bf16[1024,2048]{1,0:T(8,128)(2,1)}, u32[]{:S(2)}, u32[]{:S(2)}) collective-permute-start(bf16[1024,2048]{1,0:T(8,128)(2,1)} %dynamic-slice_convert_fusion.3), channel_id=1, source_target_pairs={{0,1},{1,0},{2,3},{3,2},{4,5},{5,4},{6,7},{7,6},{8,9},{9,8},{10,11... | collective-permute-start | bytes 12582920 | tf_op jit(solution)/shard_map/ppermute | solution.py:884
  866.0 44.2 %collective-permute-start.12 = (bf16[1024,2048]{1,0:T(8,128)(2,1)}, bf16[1024,2048]{1,0:T(8,128)(2,1)}, u32[]{:S(2)}, u32[]{:S(2)}) collective-permute-start(bf16[1024,2048]{1,0:T(8,128)(2,1)} %dynamic-slice_convert_fusion), channel_id=1, source_target_pairs={{0,1},{1,0},{2,3},{3,2},{4,5},{5,4},{6,7},{7,6},{8,9},{9,8},{10,11... | collective-permute-start | bytes 12582920 | tf_op jit(solution)/shard_map/ppermute | solution.py:884
  870.1 255.1 %reduce-scatter.3.cloned.1.call-start = ((), (), s32[]{:S(2)}) async-start(), calls=%async_computation.3 | async-start | bytes 5242880 | tf_op jit(solution)/shard_map/reduce_scatter | solution.py:909
  878.6 308.3 %reduce-scatter.5.cloned.1.call-start = ((), (), s32[]{:S(2)}) async-start(), calls=%async_computation.5 | async-start | bytes 5242880 | tf_op jit(solution)/shard_map/reduce_scatter | solution.py:909
  894.1 24.2 %collective-permute-start.8 = (bf16[1024,2048]{1,0:T(8,128)(2,1)}, bf16[1024,2048]{1,0:T(8,128)(2,1)}, u32[]{:S(2)}, u32[]{:S(2)}) collective-permute-start(bf16[1024,2048]{1,0:T(8,128)(2,1)} %dynamic-slice_convert_fusion.1), channel_id=1, source_target_pairs={{0,1},{1,0},{2,3},{3,2},{4,5},{5,4},{6,7},{7,6},{8,9},{9,8},{10,11... | collective-permute-start | bytes 12582920 | tf_op jit(solution)/shard_map/ppermute | solution.py:884
  910.2 24.5 %collective-permute-start.4 = (bf16[2048,1024]{1,0:T(8,128)(2,1)}, bf16[2048,1024]{1,0:T(8,128)(2,1)}, u32[]{:S(2)}, u32[]{:S(2)}) collective-permute-start(bf16[2048,1024]{1,0:T(8,128)(2,1)} %dynamic-slice_convert_fusion.2), channel_id=1, source_target_pairs={{0,1},{1,0},{2,3},{3,2},{4,5},{5,4},{6,7},{7,6},{8,9},{9,8},{10,11... | collective-permute-start | bytes 12582920 | tf_op jit(solution)/shard_map/ppermute | solution.py:884
  916.5 50.3 %collective-permute-start.13 = (bf16[512,2048]{1,0:T(8,128)(2,1)S(1)}, bf16[512,2048]{1,0:T(8,128)(2,1)}, u32[]{:S(2)}, u32[]{:S(2)}) collective-permute-start(bf16[512,2048]{1,0:T(8,128)(2,1)S(1)} %dynamic-slice_convert_fusion.4), channel_id=1, source_target_pairs={{0,2},{1,3},{2,0},{3,1},{4,6},{5,7},{6,4},{7,5},{8,10},{9,11},{10,... | collective-permute-start | bytes 6291464 | tf_op jit(solution)/shard_map/ppermute | solution.py:884
  932.9 83.6 %collective-permute-start.9 = (bf16[512,2048]{1,0:T(8,128)(2,1)}, bf16[512,2048]{1,0:T(8,128)(2,1)}, u32[]{:S(2)}, u32[]{:S(2)}) collective-permute-start(bf16[512,2048]{1,0:T(8,128)(2,1)} %dynamic-slice_convert_fusion.5), channel_id=1, source_target_pairs={{0,2},{1,3},{2,0},{3,1},{4,6},{5,7},{6,4},{7,5},{8,10},{9,11},{10,... | collective-permute-start | bytes 6291464 | tf_op jit(solution)/shard_map/ppermute | solution.py:884
  970.2 91.1 %collective-permute-start.14 = (bf16[512,2048]{1,0:T(8,128)(2,1)S(1)}, bf16[512,2048]{1,0:T(8,128)(2,1)}, u32[]{:S(2)}, u32[]{:S(2)}) collective-permute-start(bf16[512,2048]{1,0:T(8,128)(2,1)S(1)} %add_convert_fusion.2), channel_id=1, source_target_pairs={{0,2},{1,3},{2,0},{3,1},{4,6},{5,7},{6,4},{7,5},{8,10},{9,11},{10,... | collective-permute-start | bytes 6291464 | tf_op jit(solution)/shard_map/ppermute | solution.py:884
  1020.1 86.2 %collective-permute-start.10 = (bf16[512,2048]{1,0:T(8,128)(2,1)}, bf16[512,2048]{1,0:T(8,128)(2,1)}, u32[]{:S(2)}, u32[]{:S(2)}) collective-permute-start(bf16[512,2048]{1,0:T(8,128)(2,1)} %add_convert_fusion.3), channel_id=1, source_target_pairs={{0,2},{1,3},{2,0},{3,1},{4,6},{5,7},{6,4},{7,5},{8,10},{9,11},{10,... | collective-permute-start | bytes 6291464 | tf_op jit(solution)/shard_map/ppermute | solution.py:884
  1066.6 123.2 %collective-permute-start.15 = (bf16[1024,2048]{1,0:T(8,128)(2,1)}, bf16[1024,2048]{1,0:T(8,128)(2,1)}, u32[]{:S(2)}, u32[]{:S(2)}) collective-permute-start(bf16[1024,2048]{1,0:T(8,128)(2,1)} %pad_maximum_fusion.1), channel_id=1, source_target_pairs={{0,1},{1,0},{2,3},{3,2},{4,5},{5,4},{6,7},{7,6},{8,9},{9,8},{10,11... | collective-permute-start | bytes 12582920 | tf_op jit(solution)/shard_map/ppermute | solution.py:884
  1112.2 77.6 %collective-permute-start.11 = (bf16[1024,2048]{1,0:T(8,128)(2,1)}, bf16[1024,2048]{1,0:T(8,128)(2,1)}, u32[]{:S(2)}, u32[]{:S(2)}) collective-permute-start(bf16[1024,2048]{1,0:T(8,128)(2,1)} %pad_maximum_fusion), channel_id=1, source_target_pairs={{0,1},{1,0},{2,3},{3,2},{4,5},{5,4},{6,7},{7,6},{8,9},{9,8},{10,11... | collective-permute-start | bytes 12582920 | tf_op jit(solution)/shard_map/ppermute | solution.py:884
  1128.1 73.7 %collective-permute-start.1 = (bf16[512,512]{1,0:T(8,128)(2,1)S(1)}, bf16[512,512]{1,0:T(8,128)(2,1)S(1)}, u32[]{:S(2)}, u32[]{:S(2)}) collective-permute-start(bf16[512,512]{1,0:T(8,128)(2,1)S(1)} %dynamic-slice_convert_fusion.7), channel_id=1, source_target_pairs={{0,2},{1,3},{2,0},{3,1},{4,6},{5,7},{6,4},{7,5},{8,10},{9,11},{10,... | collective-permute-start | bytes 1572872 | tf_op jit(solution)/shard_map/ppermute | solution.py:884
  1188.6 14.2 %collective-permute-start.5 = (bf16[512,512]{1,0:T(8,128)(2,1)S(1)}, bf16[512,512]{1,0:T(8,128)(2,1)S(1)}, u32[]{:S(2)}, u32[]{:S(2)}) collective-permute-start(bf16[512,512]{1,0:T(8,128)(2,1)S(1)} %dynamic-slice_convert_fusion.6), channel_id=1, source_target_pairs={{0,2},{1,3},{2,0},{3,1},{4,6},{5,7},{6,4},{7,5},{8,10},{9,11},{10,... | collective-permute-start | bytes 1572872 | tf_op jit(solution)/shard_map/ppermute | solution.py:884
  1202.0 13.6 %collective-permute-start.2 = (bf16[512,512]{1,0:T(8,128)(2,1)S(1)}, bf16[512,512]{1,0:T(8,128)(2,1)S(1)}, u32[]{:S(2)}, u32[]{:S(2)}) collective-permute-start(bf16[512,512]{1,0:T(8,128)(2,1)S(1)} %add_convert_fusion.5), channel_id=1, source_target_pairs={{0,2},{1,3},{2,0},{3,1},{4,6},{5,7},{6,4},{7,5},{8,10},{9,11},{10,... | collective-permute-start | bytes 1572872 | tf_op jit(solution)/shard_map/ppermute | solution.py:884
  1203.0 22.8 %collective-permute-start.6 = (bf16[512,512]{1,0:T(8,128)(2,1)S(1)}, bf16[512,512]{1,0:T(8,128)(2,1)S(1)}, u32[]{:S(2)}, u32[]{:S(2)}) collective-permute-start(bf16[512,512]{1,0:T(8,128)(2,1)S(1)} %add_convert_fusion.4), channel_id=1, source_target_pairs={{0,2},{1,3},{2,0},{3,1},{4,6},{5,7},{6,4},{7,5},{8,10},{9,11},{10,... | collective-permute-start | bytes 1572872 | tf_op jit(solution)/shard_map/ppermute | solution.py:884
  1216.7 24.0 %collective-permute-start.3 = (bf16[1024,512]{1,0:T(8,128)(2,1)}, bf16[1024,512]{1,0:T(8,128)(2,1)}, u32[]{:S(2)}, u32[]{:S(2)}) collective-permute-start(bf16[1024,512]{1,0:T(8,128)(2,1)} %pad_maximum_fusion.2), channel_id=1, source_target_pairs={{0,1},{1,0},{2,3},{3,2},{4,5},{5,4},{6,7},{7,6},{8,9},{9,8},{10,11... | collective-permute-start | bytes 3145736 | tf_op jit(solution)/shard_map/ppermute | solution.py:884
  1227.0 17.9 %collective-permute-start.7 = (bf16[512,1024]{1,0:T(8,128)(2,1)}, bf16[512,1024]{1,0:T(8,128)(2,1)S(1)}, u32[]{:S(2)}, u32[]{:S(2)}) collective-permute-start(bf16[512,1024]{1,0:T(8,128)(2,1)} %pad_maximum_fusion.3), channel_id=1, source_target_pairs={{0,1},{1,0},{2,3},{3,2},{4,5},{5,4},{6,7},{7,6},{8,9},{9,8},{10,11... | collective-permute-start | bytes 3145736 | tf_op jit(solution)/shard_map/ppermute | solution.py:884
  (20 other events, 424.3 us)
Sparse Core Ops, SparseCore 0:
  10.3 47.9 all-gather.9
  60.4 44.6 all-gather.13
  106.7 57.4 all-gather.11
  165.6 58.2 all-gather.15
  788.7 138.9 all-reduce.3
  932.0 92.3 all-reduce.5
  1027.3 79.3 reduce-scatter.2
  1109.6 77.2 reduce-scatter.4

commit v4 on v3

--- a/solution.py
+++ b/solution.py
@@ -29,16 +29,114 @@
 
 
 def greet(n):
-    me = lax.axis_index("tensor")
+    me, d = lax.axis_index("tensor"), lax.axis_index("dp")
+    dp = lax.axis_size("dp")
     barrier = pltpu.get_barrier_semaphore()
     for k in range(1, n):
         pl.semaphore_signal(
             barrier, inc=1, device_id={"tensor": lax.rem(me + k, n)}, device_id_type=MESH
         )
+    for k in range(1, dp):
+        pl.semaphore_signal(
+            barrier, inc=1, device_id={"dp": lax.rem(d + k, dp)}, device_id_type=MESH
+        )
     pl.semaphore_signal(
         barrier, inc=1, device_id={"section": 1 - lax.axis_index("section")}, device_id_type=MESH
     )
-    pl.semaphore_wait(barrier, n)
+    pl.semaphore_wait(barrier, n + dp - 1)
+
+
+def gather_weight(n, whole, piece, recv, sends):
+    z_recv, x_recv, c_recv = recv
+    s_r, s_l, s_x, s_c, s_cx = sends
+    me, d = lax.axis_index("tensor"), lax.axis_index("dp")
+    dp = lax.axis_size("dp")
+    peers = dp // 2
+    partner = d + 1 - 2 * lax.rem(d, 2)
+
+    def copy(rank, j, send, recv, device):
+        ref = piece(whole, rank, j)
+        return pltpu.make_async_remote_copy(
+            src_ref=ref, dst_ref=ref, send_sem=send, recv_sem=recv, device_id=device, device_id_type=MESH
+        )
+
+    def along(j, h, to_right):
+        target = jnp.minimum(me + 1, n - 1) if to_right else jnp.maximum(me - 1, 0)
+        return copy(d, j, (s_r if to_right else s_l).at[h], z_recv.at[j], {"tensor": target})
+
+    def across(rank, k, j):
+        return copy(rank, j, s_x.at[k, j], x_recv.at[k, j], {"dp": lax.rem(d + 2 * k, dp)})
+
+    def on_chip(rank, k, j):
+        return copy(rank, j, (s_c if k == 0 else s_cx).at[k, j], c_recv.at[k, j], {"dp": partner})
+
+    def arrivals(h):
+        return ((me - h >= 0, jnp.maximum(me - h, 0), True), (me + h <= n - 1, jnp.minimum(me + h, n - 1), False))
+
+    for h in range(n):
+        for there, j, to_right in arrivals(h):
+            onward = (me < n - 1) if to_right else (me > 0)
+            if h > 0:
+
+                @pl.when(there)
+                def _(j=j, h=h, to_right=to_right):
+                    along(j, 0, to_right).wait_recv()
+
+            if h < n - 1:
+
+                @pl.when(there & onward)
+                def _(j=j, h=h, to_right=to_right):
+                    along(j, h, to_right).start()
+
+            if h > 0:
+
+                @pl.when(there)
+                def _(j=j):
+                    for k in range(1, peers):
+                        across(d, k, j).start()
+                    on_chip(d, 0, j).start()
+
+    def relay():
+        for h in range(1, n):
+            for there, j, _ in arrivals(h):
+
+                @pl.when(there)
+                def _(j=j):
+                    for k in range(1, peers):
+                        rank = lax.rem(d + dp - 2 * k, dp)
+                        across(rank, k, j).wait_recv()
+                        on_chip(rank, k, j).start()
+
+    def complete():
+        for h in range(1, n):
+            for there, j, _ in arrivals(h):
+
+                @pl.when(there)
+                def _(j=j):
+                    for k in range(peers):
+                        rank = lax.rem(partner + dp - 2 * k, dp)
+                        on_chip(rank, k, j).wait_recv()
+
+    def drain():
+        for h in range(n):
+            for there, j, to_right in arrivals(h):
+                onward = (me < n - 1) if to_right else (me > 0)
+                if h < n - 1:
+
+                    @pl.when(there & onward)
+                    def _(j=j, h=h, to_right=to_right):
+                        along(j, h, to_right).wait_send()
+
+                if h > 0:
+
+                    @pl.when(there)
+                    def _(j=j):
+                        for k in range(1, peers):
+                            across(d, k, j).wait_send()
+                        for k in range(peers):
+                            on_chip(d, k, j).wait_send()
+
+    return relay, complete, drain
 
 
 def normalize(v):
@@ -206,17 +304,16 @@
 def forward_kernel(
     cfg,
     tokens,
-    w_q_hbm,
-    w_o_hbm,
+    q_hbm,
+    o_hbm,
     w_up_hbm,
     w_dn_hbm,
     w_kv,
     vecs,
+    q_bias,
     up_bias,
     pair_bias,
-    normed_out,
     query_out,
-    att_out,
     lse_out,
     input_out,
     hidden_out,
@@ -225,6 +322,13 @@
     two_hbm,
     act_hbm,
     slope_hbm,
+    normed_all,
+    att_all,
+    q_whole,
+    o_whole,
+    normed_out,
+    att_out,
+    bias_q,
     w_q,
     w_o,
     w_up,
@@ -255,9 +359,29 @@
     keep_sem,
     hand_send,
     hand_recv,
+    wz_recv,
+    wx_recv,
+    wc_recv,
+    wz_right,
+    wz_left,
+    wx_send,
+    wc_send,
+    wcx_send,
+    bias_send,
+    bias_recv,
+    rows_send,
+    rows_recv,
+    own_sem,
+    swap_send,
+    swap_recv,
 ):
     n, nb, own, chunks, rows, tile = (cfg[k] for k in ("n", "nb", "own", "chunks", "rows", "tile"))
+    dp = lax.axis_size("dp")
+    d = lax.axis_index("dp")
+    peers, mine = dp // 2, d // 2
     dim = x_ref.shape[1]
+    share = bias_q.shape[2]
+    q_tile = min(tile, share)
     ff = w_up.shape[1]
     width = w_q.shape[1]
     heads = width // HD
@@ -268,11 +392,103 @@
     scale = 1.0 / math.sqrt(HD)
     loads = [
         pltpu.make_async_copy(src, dst, w_sem.at[k])
-        for k, (src, dst) in enumerate(((w_q_hbm, w_q), (w_o_hbm, w_o), (w_up_hbm, w_up), (w_dn_hbm, w_dn)))
+        for k, (src, dst) in enumerate(
+            (
+                (q_hbm, w_q.at[:, aligned(me * share, share)]),
+                (o_hbm, w_o.at[aligned(me * share, share)]),
+                (w_up_hbm, w_up),
+                (w_dn_hbm, w_dn),
+            )
+        )
     ]
     for load in loads:
         load.start()
     greet(n)
+
+    def q_piece(ref, rank, j):
+        return ref.at[aligned(rank * (dim // dp), dim // dp), aligned(j * share, share)]
+
+    def o_piece(ref, rank, j):
+        return ref.at[aligned(j * share + rank * (share // dp), share // dp)]
+
+    def bias_copy(k):
+        return pltpu.make_async_remote_copy(
+            src_ref=q_bias,
+            dst_ref=bias_q.at[me],
+            send_sem=bias_send.at[k],
+            recv_sem=bias_recv.at[k],
+            device_id={"tensor": lax.rem(me + k, n)},
+            device_id_type=MESH,
+        )
+
+    bias_q[me] = q_bias[...]
+    for k in range(1, n):
+        bias_copy(k).start()
+    loads[0].wait()
+    loads[1].wait()
+    gathers = []
+    for m, (whole, piece) in enumerate(((w_q, q_piece), (w_o, o_piece))):
+        gathers.append(
+            gather_weight(
+                n,
+                whole,
+                piece,
+                (wz_recv.at[m], wx_recv.at[m], wc_recv.at[m]),
+                (wz_right.at[m], wz_left.at[m], wx_send.at[m], wc_send.at[m], wcx_send.at[m]),
+            )
+        )
+    for relay, complete, drain in gathers:
+        relay()
+    for relay, complete, drain in gathers:
+        complete()
+    stores = [
+        pltpu.make_async_copy(w_q, q_whole, w_sem.at[0]),
+        pltpu.make_async_copy(w_o, o_whole, w_sem.at[1]),
+    ]
+    for store in stores:
+        store.start()
+    for k in range(1, n):
+        bias_copy(k).wait_recv()
+
+    def rows_copies(b, k):
+        target = lax.rem(me + k, n)
+        return [
+            pltpu.make_async_remote_copy(
+                src_ref=src,
+                dst_ref=dst,
+                send_sem=rows_send.at[a, b, k],
+                recv_sem=rows_recv.at[a, b, k],
+                device_id={"tensor": target},
+                device_id_type=MESH,
+            )
+            for a, (src, dst) in enumerate(
+                (
+                    (normed_out.at[b], normed_all.at[me, b]),
+                    (att_out.at[b, :, aligned(target * share, share)], att_all.at[me, b]),
+                )
+            )
+        ]
+
+    def own_copies(b):
+        return [
+            pltpu.make_async_copy(normed_out.at[b], normed_all.at[me, b], own_sem.at[0]),
+            pltpu.make_async_copy(
+                att_out.at[b, :, aligned(me * share, share)], att_all.at[me, b], own_sem.at[1]
+            ),
+        ]
+
+    def swap_copies(b, k):
+        return [
+            pltpu.make_async_remote_copy(
+                src_ref=ref.at[mine, b],
+                dst_ref=ref.at[mine, b],
+                send_sem=swap_send.at[a, b, k],
+                recv_sem=swap_recv.at[a, b, k],
+                device_id={"dp": lax.rem(d + 2 * k, dp)},
+                device_id_type=MESH,
+            )
+            for a, ref in enumerate((two_hbm, act_hbm))
+        ]
 
     def pairs_copy(b, k):
         rows_here = aligned(b * block + me * own, own)
@@ -297,8 +513,8 @@
 
     def keep_copies(b, c):
         return [
-            pltpu.make_async_copy(g.at[c], two_hbm.at[b, c], keep_sem.at[0, c]),
-            pltpu.make_async_copy(act.at[c], act_hbm.at[b, c], keep_sem.at[1, c]),
+            pltpu.make_async_copy(g.at[c], two_hbm.at[mine, b, c], keep_sem.at[0, c]),
+            pltpu.make_async_copy(act.at[c], act_hbm.at[mine, b, c], keep_sem.at[1, c]),
             pltpu.make_async_copy(slope.at[c], slope_hbm.at[b, c], keep_sem.at[2, c]),
         ]
 
@@ -320,19 +536,19 @@
         kv_out[aligned(b * block + me * own, own)] = pairs
         for k in range(1, n):
             pairs_copy(b, k).start()
-
-        @pl.when(b == 0)
-        def _():
-            loads[0].wait()
+        for k in range(1, n):
+            rows_copies(b, k)[0].start()
+        own_copies(b)[0].start()
 
         def query_tile(t, carry):
-            cols = aligned(t * tile, tile)
-            q = (dot(normed_out[b], w_q[:, cols]) + vecs[6:7, cols]).astype(BF16)
-            for k in range(tile // HD):
-                q_ref[aligned((t * (tile // HD) + k) * own, own)] = q[:, k * HD : (k + 1) * HD]
+            cols = aligned(t * q_tile, q_tile)
+            bias = bias_q[t // (share // q_tile), 0:1, aligned(lax.rem(t, share // q_tile) * q_tile, q_tile)]
+            q = (dot(normed_out[b], w_q[:, cols]) + bias).astype(BF16)
+            for k in range(q_tile // HD):
+                q_ref[aligned((t * (q_tile // HD) + k) * own, own)] = q[:, k * HD : (k + 1) * HD]
             return carry
 
-        lax.fori_loop(0, width // tile, query_tile, 0)
+        lax.fori_loop(0, width // q_tile, query_tile, 0)
         query_out[b] = q_ref[...]
         for k in range(1, n):
             pairs_copy(b, k).wait_recv()
@@ -367,10 +583,9 @@
             return carry
 
         lax.fori_loop(0, heads // per, head_tile, 0)
-
-        @pl.when(b == 0)
-        def _():
-            loads[1].wait()
+        for k in range(1, n):
+            rows_copies(b, k)[1].start()
+        own_copies(b)[1].start()
 
         def out_tile(t, carry):
             cols = aligned(t * tile, tile)
@@ -439,8 +654,16 @@
         def _():
             hand_copy(b).start()
 
+        @pl.when(b < nb - 1)
+        def _():
+            for k in range(1, peers):
+                for copy in swap_copies(b, k):
+                    copy.start()
+
         for k in range(1, n):
             pairs_copy(b, k).wait_send()
+        for copy in own_copies(b):
+            copy.wait()
         return carry
 
     lax.fori_loop(0, nb, block_step, 0)
@@ -450,18 +673,37 @@
         def _():
             hand_copy(b).wait_send()
 
+        for k in range(1, n):
+            for copy in rows_copies(b, k):
+                copy.wait()
+
+        @pl.when(b < nb - 1)
+        def _():
+            for k in range(1, peers):
+                for copy in swap_copies(b, k):
+                    copy.wait()
+
         return carry
 
     lax.fori_loop(0, nb, settle, 0)
-
-
-def forward(tokens, w_q, w_o, w_up, w_dn, w_kv, vecs, up_bias, pair_bias):
+    for relay, complete, drain in gathers:
+        drain()
+    for k in range(1, n):
+        bias_copy(k).wait_send()
+    for store in stores:
+        store.wait()
+
+
+def forward(tokens, q_shard, o_shard, w_up, w_dn, w_kv, vecs, q_bias, up_bias, pair_bias):
     n = lax.axis_size("tensor")
+    dp = lax.axis_size("dp")
+    peers = dp // 2
     nb, own, dim = tokens.shape
     rows = min(16, own)
     chunks = own // rows
     ff = w_up.shape[1]
-    width = w_q.shape[1]
+    share = q_shard.shape[1]
+    width = share * n
     heads = width // HD
     tile = min(512, dim, ff)
     per = min(heads, max(1, 256 // own))
@@ -476,21 +718,26 @@
         functools.partial(forward_kernel, cfg),
         name="forward",
         out_shape=(
-            S((nb, own, dim), BF16),
             S((nb, heads * own, HD), BF16),
-            S((nb, own, width), BF16),
             S((nb, heads // per, 1, per * own), F32),
             S((nb, own, dim), BF16),
             S((nb, own, dim), F32),
             S((nb, own, dim), BF16),
             S((nb * block, 2 * HD), BF16),
-            S((nb, chunks, n * rows, dim), BF16),
+            S((peers, nb, chunks, n * rows, dim), BF16),
+            S((peers, nb, chunks, n * rows, ff), BF16),
             S((nb, chunks, n * rows, ff), BF16),
-            S((nb, chunks, n * rows, ff), BF16),
+            S((n, nb, own, dim), BF16),
+            S((n, nb, own, share), BF16),
+            S((dim, width), BF16),
+            S((width, dim), BF16),
         ),
-        in_specs=[vmem, hbm, hbm, hbm, hbm, vmem, vmem, vmem, vmem],
-        out_specs=(vmem,) * 8 + (hbm,) * 3,
+        in_specs=[vmem, hbm, hbm, hbm, hbm, vmem, vmem, vmem, vmem, vmem],
+        out_specs=(vmem,) * 6 + (hbm,) * 7,
         scratch_shapes=[
+            pltpu.VMEM((nb, own, dim), BF16),
+            pltpu.VMEM((nb, own, width), BF16),
+            pltpu.VMEM((n, 8, share), F32),
             pltpu.VMEM((dim, width), BF16),
             pltpu.VMEM((width, dim), BF16),
             pltpu.VMEM((dim, ff), BF16),
@@ -510,11 +757,26 @@
             dma((3, chunks)),
             dma((nb,)),
             dma((nb,)),
+            dma((2, n)),
+            dma((2, peers, n)),
+            dma((2, peers, n)),
+            dma((2, n)),
+            dma((2, n)),
+            dma((2, peers, n)),
+            dma((2, peers, n)),
+            dma((2, peers, n)),
+            dma((n,)),
+            dma((n,)),
+            dma((2, nb, n)),
+            dma((2, nb, n)),
+            dma((2,)),
+            dma((2, nb, peers)),
+            dma((2, nb, peers)),
         ],
         compiler_params=pltpu.CompilerParams(
             collective_id=1, has_side_effects=True, vmem_limit_bytes=67000000
         ),
-    )(tokens, w_q, w_o, w_up, w_dn, w_kv, vecs, up_bias, pair_bias)
+    )(tokens, q_shard, o_shard, w_up, w_dn, w_kv, vecs, q_bias, up_bias, pair_bias)
 
 
 def norm_back(v, gain, grad):
@@ -541,14 +803,23 @@
     w_up_hbm,
     w_o_hbm,
     w_q_hbm,
-    branch_out,
-    gq_out,
-    pairs_out,
+    two_in,
+    act_in,
     input_grad,
     common,
     up_sum,
     mlp_hbm,
     pre_hbm,
+    branch_all,
+    gq_all,
+    pairs_all,
+    two_hbm,
+    act_hbm,
+    branch_out,
+    gq_out,
+    pairs_out,
+    z_sum,
+    dp_sum,
     w_dn,
     w_up,
     w_o,
@@ -587,9 +858,22 @@
     slope_sem,
     hand_send,
     hand_recv,
+    rows_send,
+    rows_recv,
+    own_sem,
+    swap_send,
+    swap_recv,
+    z_send,
+    z_recv,
+    dp_send,
+    dp_recv,
 ):
     n, nb, own, chunks, rows, tile = (cfg[k] for k in ("n", "nb", "own", "chunks", "rows", "tile"))
     per = cfg["per"]
+    dp = lax.axis_size("dp")
+    d = lax.axis_index("dp")
+    peers, rank = dp // 2, d // 2
+    share = w_q.shape[1] // n
     dim = go.shape[1]
     ff = w_up.shape[1]
     width = w_q.shape[1]
@@ -605,6 +889,65 @@
     for load in loads:
         load.start()
     greet(n)
+
+    def rows_copies(b, k):
+        target = lax.rem(me + k, n)
+        return [
+            pltpu.make_async_remote_copy(
+                src_ref=src,
+                dst_ref=dst,
+                send_sem=rows_send.at[a, b, k],
+                recv_sem=rows_recv.at[a, b, k],
+                device_id={"tensor": target},
+                device_id_type=MESH,
+            )
+            for a, (src, dst) in enumerate(
+                (
+                    (branch_out.at[b], branch_all.at[me, b]),
+                    (gq_out.at[b, :, aligned(target * share, share)], gq_all.at[me, b]),
+                    (pairs_out.at[b], pairs_all.at[me, b]),
+                )
+            )
+        ]
+
+    def own_copies(b):
+        return [
+            pltpu.make_async_copy(branch_out.at[b], branch_all.at[me, b], own_sem.at[0]),
+            pltpu.make_async_copy(
+                gq_out.at[b, :, aligned(me * share, share)], gq_all.at[me, b], own_sem.at[1]
+            ),
+            pltpu.make_async_copy(pairs_out.at[b], pairs_all.at[me, b], own_sem.at[2]),
+        ]
+
+    def swap_copies(b, k):
+        return [
+            pltpu.make_async_remote_copy(
+                src_ref=ref.at[rank, b],
+                dst_ref=ref.at[rank, b],
+                send_sem=swap_send.at[a, b, k],
+                recv_sem=swap_recv.at[a, b, k],
+                device_id={"dp": lax.rem(d + 2 * k, dp)},
+                device_id_type=MESH,
+            )
+            for a, ref in enumerate((mlp_hbm, pre_hbm))
+        ]
+
+    def late_copies(k):
+        return [
+            pltpu.make_async_remote_copy(
+                src_ref=ref.at[rank, nb - 1],
+                dst_ref=ref.at[rank, nb - 1],
+                send_sem=swap_send.at[2 + a, 0, k],
+                recv_sem=swap_recv.at[2 + a, 0, k],
+                device_id={"dp": lax.rem(d + 2 * k, dp)},
+                device_id_type=MESH,
+            )
+            for a, ref in enumerate((two_hbm, act_hbm))
+        ]
+
+    for k in range(1, peers):
+        for copy in late_copies(k):
+            copy.start()
     gk[...] = jnp.zeros_like(gk)
     gv[...] = jnp.zeros_like(gv)
     common[...] = jnp.zeros_like(common)
@@ -635,8 +978,8 @@
 
     def keep_copies(b, c):
         return [
-            pltpu.make_async_copy(g.at[c], mlp_hbm.at[b, c], keep_sem.at[0, c]),
-            pltpu.make_async_copy(gpre.at[c], pre_hbm.at[b, c], keep_sem.at[1, c]),
+            pltpu.make_async_copy(g.at[c], mlp_hbm.at[rank, b, c], keep_sem.at[0, c]),
+            pltpu.make_async_copy(gpre.at[c], pre_hbm.at[rank, b, c], keep_sem.at[1, c]),
         ]
 
     def block_step(i, carry):
@@ -697,6 +1040,9 @@
             compute,
             finish,
         )
+        for k in range(1, peers):
+            for copy in swap_copies(b, k):
+                copy.start()
         for c in range(chunks):
             gn[c * rows : (c + 1) * rows] = terms[c, aligned(me * rows, rows)]
         back, gain_sum, bias_sum = norm_back(hidden[b], vecs[2:3], gn[...])
@@ -705,6 +1051,9 @@
         go[...] += back
         common[2:3, :dim] += jnp.sum(go[...], axis=0, keepdims=True)
         branch_out[b] = go[...].astype(BF16)
+        for k in range(1, n):
+            rows_copies(b, k)[0].start()
+        own_copies(b)[0].start()
 
         @pl.when(i == 0)
         def _():
@@ -754,6 +1103,9 @@
         pair_send[:, HD:] = gv[here].astype(BF16)
         for k in range(1, n):
             pair_copy(k).start()
+        for k in range(1, n):
+            rows_copies(b, k)[1].start()
+        own_copies(b)[1].start()
         common[6:7, :width] += jnp.sum(gq_out[b].astype(F32), axis=0, keepdims=True)
 
         @pl.when(i == 0)
@@ -775,6 +1127,9 @@
             total_v += pair_recv[k, :, HD:].astype(F32)
         pairs_out[b, :, :HD] = total_k.astype(BF16)
         pairs_out[b, :, HD:] = total_v.astype(BF16)
+        for k in range(1, n):
+            rows_copies(b, k)[2].start()
+        own_copies(b)[2].start()
         common[7:8, : 2 * HD] += jnp.sum(pairs_out[b].astype(F32), axis=0, keepdims=True)
 
         def pair_tile(t, carry):
@@ -800,17 +1155,76 @@
             hand[...] = go[...].astype(BF16)
             hand_copy(b).start()
 
+        for copy in own_copies(b):
+            copy.wait()
         return carry
 
     lax.fori_loop(0, nb, block_step, 0)
+
+    def z_copy(k):
+        return pltpu.make_async_remote_copy(
+            src_ref=common,
+            dst_ref=z_sum.at[me],
+            send_sem=z_send.at[k],
+            recv_sem=z_recv.at[k],
+            device_id={"tensor": lax.rem(me + k, n)},
+            device_id_type=MESH,
+        )
+
+    def dp_copy(k):
+        return pltpu.make_async_remote_copy(
+            src_ref=dp_sum.at[d],
+            dst_ref=dp_sum.at[d],
+            send_sem=dp_send.at[k],
+            recv_sem=dp_recv.at[k],
+            device_id={"dp": lax.rem(d + k, dp)},
+            device_id_type=MESH,
+        )
+
+    z_sum[me] = common[...]
+    for k in range(1, n):
+        z_copy(k).start()
+    for k in range(1, n):
+        z_copy(k).wait()
+    total = z_sum[0]
+    for j in range(1, n):
+        total += z_sum[j]
+    dp_sum[d, :8] = total
+    dp_sum[d, 8:] = jnp.zeros((8, total.shape[1]), F32)
+    dp_sum[d, 8:9, :ff] = up_sum[...]
+    for k in range(1, dp):
+        dp_copy(k).start()
+    for k in range(1, dp):
+        dp_copy(k).wait()
+    total = dp_sum[0]
+    for j in range(1, dp):
+        total += dp_sum[j]
+    common[...] = total[:8]
+    up_sum[...] = total[8:9, :ff]
+
+    def settle(b, carry):
+        for k in range(1, n):
+            for copy in rows_copies(b, k):
+                copy.wait()
+        for k in range(1, peers):
+            for copy in swap_copies(b, k):
+                copy.wait()
+        return carry
+
+    lax.fori_loop(0, nb, settle, 0)
+    for k in range(1, peers):
+        for copy in late_copies(k):
+            copy.wait()
 
     @pl.when(sec == 1)
     def _():
         hand_copy(0).wait_send()
 
 
-def backward(cot, inputs, hidden, query, lse, kv, vecs, w_kv, slope, w_dn, w_up, w_o, w_q):
+def backward(cot, inputs, hidden, query, lse, kv, vecs, w_kv, slope, w_dn, w_up, w_o, w_q, two, act):
     n = lax.axis_size("tensor")
+    dp = lax.axis_size("dp")
+    peers = dp // 2
     nb, own, dim = cot.shape
     chunks, rows = slope.shape[1], own // slope.shape[1]
     ff = w_up.shape[1]
@@ -819,6 +1233,8 @@
     tile = min(512, dim, ff)
     per = lse.shape[3] // own
     block = n * own
+    span = max(dim, width)
+    assert ff <= span
     cfg = dict(n=n, nb=nb, own=own, chunks=chunks, rows=rows, tile=tile, per=per)
     S = jax.ShapeDtypeStruct
     vmem = pl.BlockSpec(memory_space=pltpu.VMEM)
@@ -829,18 +1245,26 @@
         functools.partial(backward_kernel, cfg),
         name="backward",
         out_shape=(
-            S((nb, own, dim), BF16),
-            S((nb, own, width), BF16),
-            S((nb, own, 2 * HD), BF16),
             S((nb, own, dim), F32),
-            S((8, max(dim, width)), F32),
+            S((8, span), F32),
             S((1, ff), F32),
-            S((nb, chunks, n * rows, dim), BF16),
-            S((nb, chunks, n * rows, ff), BF16),
+            S((peers, nb, chunks, n * rows, dim), BF16),
+            S((peers, nb, chunks, n * rows, ff), BF16),
+            S((n, nb, own, dim), BF16),
+            S((n, nb, own, width // n), BF16),
+            S((n, nb, own, 2 * HD), BF16),
+            S(two.shape, BF16),
+            S(act.shape, BF16),
         ),
-        in_specs=[vmem] * 8 + [hbm] * 5,
-        out_specs=(vmem,) * 6 + (hbm,) * 2,
+        in_specs=[vmem] * 8 + [hbm] * 7,
+        out_specs=(vmem,) * 3 + (hbm,) * 7,
+        input_output_aliases={13: 8, 14: 9},
         scratch_shapes=[
+            pltpu.VMEM((nb, own, dim), BF16),
+            pltpu.VMEM((nb, own, width), BF16),
+            pltpu.VMEM((nb, own, 2 * HD), BF16),
+            pltpu.VMEM((n, 8, span), F32),
+            pltpu.VMEM((dp, 16, span), F32),
             pltpu.VMEM((ff, dim), BF16),
             pltpu.VMEM((dim, ff), BF16),
             pltpu.VMEM((width, dim), BF16),
@@ -868,11 +1292,20 @@
             dma(()),
             dma(()),
             dma((nb,)),
+            dma((3, nb, n)),
+            dma((3, nb, n)),
+            dma((3,)),
+            dma((4, nb, peers)),
+            dma((4, nb, peers)),
+            dma((n,)),
+            dma((n,)),
+            dma((dp,)),
+            dma((dp,)),
         ],
         compiler_params=pltpu.CompilerParams(
             collective_id=2, has_side_effects=True, vmem_limit_bytes=67000000
         ),
-    )(cot, inputs, hidden, query, lse, kv, vecs, w_kv, slope, w_dn, w_up, w_o, w_q)
+    )(cot, inputs, hidden, query, lse, kv, vecs, w_kv, slope, w_dn, w_up, w_o, w_q, two, act)
 
 
 def t_dot(a, b):
@@ -900,15 +1333,11 @@
     return jnp.concatenate([low, high], axis=axis)
 
 
-def sum_dp(value, axis, scatter=None):
+def sum_dp(value, axis):
     size = lax.axis_size("dp")
     distance = 1
     while distance < size:
         value = fold(value, distance, axis)
-        if distance == 1 and scatter is not None:
-            value = lax.psum_scatter(
-                value.astype(BF16), "tensor", scatter_dimension=scatter, tiled=True
-            ).astype(F32)
         distance *= 2
     value = value.astype(BF16)
     while distance > 1:
@@ -917,12 +1346,9 @@
     return value.astype(F32)
 
 
-def whole_weight(shard, split, join):
-    size = lax.axis_size("dp")
-    part = shard.shape[split] // size
-    own = lax.dynamic_slice_in_dim(shard, lax.axis_index("dp") * part, part, split)
-    own = lax.all_gather(own, "tensor", axis=join, tiled=True)
-    return lax.all_gather(own, "dp", axis=split, tiled=True)
+def sum_pair(value):
+    value = value.astype(BF16)
+    return value.astype(F32) + swap(value, 1).astype(F32)
 
 
 def on_device(
@@ -960,37 +1386,48 @@
     assert seq_count == 1
     tokens_in = tokens_in[:, :, 0]
     cotangent = cotangent[:, :, 0]
-    w_query = whole_weight(q_weight[0], 0, 1)
-    w_out = whole_weight(o_weight[0], 1, 0)
-    b_query = lax.all_gather(q_bias[0], "tensor", axis=0, tiled=True).astype(F32)
-    width = w_query.shape[1]
-    ff_local = w_up.shape[1]
-
-    vecs = jnp.stack([gain_one, bias_one, gain_two, bias_two, b_out, b_down, b_query, b_query])
+    share = q_weight.shape[2]
+    width = share * tensor_count
+    query_bias = jnp.broadcast_to(q_bias.astype(F32), (8, share))
+
+    vecs = jnp.stack([gain_one, bias_one, gain_two, bias_two, b_out, b_down, b_down, b_down])
     (
-        kept_normed,
         kept_query,
-        kept_attended,
         kept_logsum,
         kept_input,
         kept_hidden,
         outputs,
         kv_cache,
-        kept_normed_two,
-        kept_active,
-        kept_slope,
+        normed_two,
+        active,
+        slope,
+        normed_all,
+        att_all,
+        w_query,
+        w_out,
     ) = forward(
-        tokens_in, w_query, w_out, w_up, w_down, w_pairs, vecs, b_up[None], pair_bias[None]
+        tokens_in,
+        q_weight[0],
+        o_weight[0],
+        w_up,
+        w_down,
+        w_pairs,
+        vecs,
+        query_bias,
+        b_up[None],
+        pair_bias[None],
     )
     (
-        kept_branch,
-        kept_grad_query,
-        kept_grad_pairs,
         input_grads,
         common,
         up_b,
-        kept_grad_mlp,
-        kept_grad_pre,
+        grad_mlp,
+        grad_pre,
+        branch_all,
+        gq_all,
+        pairs_all,
+        normed_two,
+        active,
     ) = backward(
         cotangent,
         kept_input,
@@ -1000,40 +1437,26 @@
         kv_cache,
         vecs,
         w_pairs,
-        kept_slope,
+        slope,
         w_down,
         w_up,
         w_out,
         w_query,
+        normed_two,
+        active,
     )
 
     def flat(kept):
         return kept.reshape(-1, kept.shape[-1])
 
-    down_w = t_dot(flat(kept_active), flat(kept_grad_mlp))
-    up_w = t_dot(flat(kept_normed_two), flat(kept_grad_pre))
-    out_w = t_dot(flat(kept_attended), flat(kept_branch))
-    query_w = t_dot(flat(kept_normed), flat(kept_grad_query))
-    pair_w = t_dot(flat(kept_normed), flat(kept_grad_pairs))
-    down_w = sum_dp(down_w, 0)
-    up_w = sum_dp(up_w, 0)
-    out_w = sum_dp(out_w, 1, 0)
-    query_w = sum_dp(query_w, 0, 1)
-    pair_w = lax.psum(pair_w.astype(BF16), ("tensor", "dp")).astype(F32)
-    wide = jnp.zeros((tensor_count, ff_local), F32)
-    wide = lax.dynamic_update_index_in_dim(wide, up_b[0], tensor_rank, 0)
-    packed = jnp.concatenate(
-        [common[:6, :model_dim].reshape(-1), common[6, :width], common[7, HD : 2 * HD], wide.reshape(-1)]
-    )
-    packed = lax.psum(packed, ("tensor", "dp"))
-    vecs = packed[: 6 * model_dim].reshape(6, model_dim)
-    own_query = lax.dynamic_slice_in_dim(
-        packed, 6 * model_dim + tensor_rank * (width // tensor_count), width // tensor_count, 0
-    )
-    value_b = lax.slice_in_dim(packed, 6 * model_dim + width, 6 * model_dim + width + HD)
-    own_up = lax.dynamic_slice_in_dim(
-        packed, 6 * model_dim + width + HD + tensor_rank * ff_local, ff_local, 0
-    )
+    query_w = sum_dp(t_dot(flat(normed_all), flat(gq_all)), 0)
+    out_w = sum_dp(t_dot(flat(att_all), flat(branch_all)), 1)
+    pair_w = sum_dp(t_dot(flat(normed_all), flat(pairs_all)), 0)
+    down_w = sum_pair(t_dot(flat(active), flat(grad_mlp)))
+    up_w = sum_pair(t_dot(flat(normed_two), flat(grad_pre)))
+    own_query = lax.dynamic_slice_in_dim(common[6, :width], tensor_rank * share, share, 0)
+    value_b = common[7, HD : 2 * HD]
+    vecs = common[:6, :model_dim]
     return (
         outputs[None, :, :, None],
         input_grads[None, :, :, None],
@@ -1048,7 +1471,7 @@
         vecs[3][None],
         vecs[4][None],
         up_w[None],
-        own_up[None],
+        up_b,
         down_w[None],
         vecs[5][None],
     )

time: 1260 us -> 1060 us (0.84)
  waiting for transfers between devices: 411 us -> 40.2 us
  Pallas kernels: 561 us -> 885 us
  starting transfers between devices: 71.1 us -> 10.9 us
  other arithmetic: 105 us -> 50 us
  local copies, waits for them, and re-layouts: 48.5 us -> 16.3 us
  matrix products: 34.9 us -> 53.2 us
  between operations: 14.8 us -> 0.88 us
    all_gather x4 -> x0, waiting for transfers between devices: 201 us -> none  [the longest x2 107 us: whole_weight(): return lax.all_gather(own, 'dp', axis=split, tiled=True)]
    pallas_call x1, Pallas kernels: 200 us -> 380 us  [forward(): pl.pallas_call(functools.partial(forward_kernel, cfg), name='forward', ou...]
    pallas_call x1, Pallas kernels: 360 us -> 504 us  [backward(): pl.pallas_call(functools.partial(backward_kernel, cfg), name='backward',...]
    ppermute x16 -> x14, waiting for transfers between devices: 153 us -> 40.2 us  [swap(): return lax.ppermute(value, 'dp', [(i, i ^ distance) for i in range(size)])]
    ppermute x16 -> x14, starting transfers between devices: 70.6 us -> 10.9 us  [swap(): return lax.ppermute(value, 'dp', [(i, i ^ distance) for i in range(size)])]
    reduce_scatter x2 -> x0, waiting for transfers between devices: 57.3 us -> none  [sum_dp(): lax.psum_scatter(value.astype(BF16), 'tensor', scatter_dimension=scatter,...]
    broadcast_in_dim x1 -> x3, other arithmetic: 2.7 us -> 25.8 us  [the longest x1 12.6 us: on_device(): up_w[None]]
    convert_element_type x4 -> x3, other arithmetic: 28.8 us -> 6.63 us  [sum_dp(): return value.astype(F32)]
  transfers between devices with their start and end apart: 24 -> 14, of which waited for: 10 -> 5; matrix products, arithmetic and copies ran while one was open for 13% -> 7% of each run, Pallas kernels for 0% -> 0%
where the time goes in v4:
time: 1060 us
  Pallas kernels  885 us (83%)
  matrix products  53.2 us (5%)
  other arithmetic  50 us (5%)
  waiting for transfers between devices  40.2 us (4%)
  local copies, waits for them, and re-layouts  16.3 us (2%)
  starting transfers between devices  10.9 us (1%)
    pallas_call x1, Pallas kernels, backward(): pl.pallas_call(functools.partial(backward_kernel, cfg), name='backward',...  504 us
    pallas_call x1, Pallas kernels, forward(): pl.pallas_call(functools.partial(forward_kernel, cfg), name='forward', ou...  380 us
    dot_general x5, matrix products, t_dot(): lax.dot_general(a, b, (((0,), (0,)), ((), ())), preferred_element_type=F32)  53.2 us
    ppermute x14, waiting for transfers between devices, swap(): return lax.ppermute(value, 'dp', [(i, i ^ distance) for i in range(size)])  40.2 us
  transfers between devices with their start and end apart: 14, of which 5 were waited for; matrix products, arithmetic and copies ran while one was open for 7% of the time, Pallas kernels for 0%

profile of v4, /device:TPU:1, one launch (start us, length us, event | category | flops | bytes accessed | tf_op | source)
XLA Modules:
  0.0 1056.1 jit_solution(8482132139813998979)
XLA Ops:
  2.9 1.3 convert_element_type.114.up_bias
  4.2 1.2 pad_convert_fusion
  6.1 380.3 %forward.1 = (bf16[4,1024,128]{2,1,0:T(8,128)(2,1)}, f32[4,4,1,256]{3,2,1,0:T(1,128)}, bf16[4,64,2048]{2,1,0:T(8,128)(2,1)}, f32[4,64,2048]{2,1,0:T(8,128)}, bf1...) custom-call(bf16[4,64,2048]{2,1,0:T(8,128)(2,1)} %bitcast.70, ...), custom_call_target="tpu_custom_call" | custom-call | tf_op jit(solution)/shard_map/forward/pallas_call | solution.py:717
  386.4 504.3 %backward.1 = (f32[4,64,2048]{2,1,0:T(8,128)}, f32[8,2048]{1,0:T(8,128)}, f32[1,2048]{1,0:T(1,128)}, bf16[2,4,4,64,2048]{4,3,2,1,0:T(8,128)(2,1)}, bf16[2,4,4,64...) custom-call(bf16[4,64,2048]{2,1,0:T(8,128)(2,1)} %bitcast.69, ...), custom_call_target="tpu_custom_call", output_to_operand_aliasing={{8}: (13, {}), {9}: (14, {})} | custom-call | tf_op jit(solution)/shard_map/backward/pallas_call | solution.py:1244
  890.7 24.0 %bitcast_convert_fusion = bf16[2048,2048]{1,0:T(8,128)(2,1)} fusion(bf16[2,4,4,64,2048]{4,3,2,1,0:T(8,128)(2,1)} %get-tuple-element.60, bf16[2,4,4,64,2048]{4,3,2,1,0:T(8,128)(2,1)} %get-tuple-element.61), kind=kOutput, calls=%fused_computation | convolution fusion | flops 17184063488 | bytes 25165824 | tf_op jit(solution)/shard_map/dot_general | solution.py:1312
  914.7 20.6 %bitcast_convert_fusion.1 = bf16[2048,2048]{1,0:T(8,128)(2,1)} fusion(bf16[2,4,4,64,2048]{4,3,2,1,0:T(8,128)(2,1)S(1)} %copy-done.1, bf16[2,4,4,64,2048]{4,3,2,1,0:T(8,128)(2,1)S(1)} %copy-done.9), kind=kOutput, calls=%fused_computation.1 | convolution fusion | flops 17184063488 | bytes 25165824 | tf_op jit(solution)/shard_map/dot_general | solution.py:1312
  935.9 4.8 convolution_bitcast_fusion
  941.0 1.4 convolution_bitcast_fusion.2
  943.7 2.4 convolution_bitcast_fusion.1
  946.1 2.0 copy-done.3
  950.5 1.4 convert_add_fusion.2
  952.0 1.1 collective-permute-start.5
  953.1 2.2 convert_add_fusion
  956.7 1.5 convert_add_fusion.1
  961.0 10.0 collective-permute-done.9
  971.1 1.4 add_convert_fusion
  972.5 1.1 collective-permute-start.10
  973.6 14.5 %collective-permute-done.6 = bf16[512,256]{1,0:T(8,128)(2,1)} collective-permute-done((bf16[512,256]{1,0:T(8,128)(2,1)S(1)}, bf16[512,256]{1,0:T(8,128)(2,1)}, u32[]{:S(2)}, u32[]{:S(2)}) %collective-permute-start.6) | collective-permute-done | bytes 262176 | tf_op jit(solution)/shard_map/ppermute | solution.py:1317
  989.2 1.1 collective-permute-start.2
  991.1 1.8 collective-permute-start.7
  992.9 6.2 collective-permute-done.10
  999.2 1.1 pad_maximum_fusion.1
  1000.4 1.5 collective-permute-start.11
  1001.9 8.5 collective-permute-done.2
  1013.6 5.1 copy.35
  1019.5 1.5 maximum_convert_fusion.2
  1020.9 1.7 select_bitcast_fusion.1
  1022.7 1.6 select_bitcast_fusion.3
  1024.3 2.6 maximum_convert_fusion.1
  1026.8 2.6 maximum_convert_fusion
  1029.4 12.5 %add_bitcast_fusion = f32[1,2048,2048]{2,1,0:T(8,128)} fusion(bf16[2048,2048]{1,0:T(8,128)(2,1)} %collective-permute-done.13, bf16[2048,2048]{1,0:T(8,128)(2,1)} %bitcast_convert_fusion), kind=kLoop, calls=%fused_computation.2 | loop fusion | flops 12582912 | bytes 33554432 | tf_op jit(solution)/shard_map/broadcast_in_dim | solution.py:1475
  1041.9 12.6 %add_bitcast_fusion.1 = f32[1,2048,2048]{2,1,0:T(8,128)} fusion(bf16[2048,2048]{1,0:T(8,128)(2,1)} %collective-permute-done.12, bf16[2048,2048]{1,0:T(8,128)(2,1)} %bitcast_convert_fusion.1), kind=kLoop, calls=%fused_computation.3 | loop fusion | flops 12582912 | bytes 33554432 | tf_op jit(solution)/shard_map/broadcast_in_dim | solution.py:1473
  (67 shorter events, 19.2 us)
Async XLA Ops:
  890.7 24.0 %copy-start.1 = (bf16[2,4,4,64,2048]{4,3,2,1,0:T(8,128)(2,1)S(1)}, bf16[2,4,4,64,2048]{4,3,2,1,0:T(8,128)(2,1)}, u32[]{:S(2)}) copy-start(bf16[2,4,4,64,2048]{4,3,2,1,0:T(8,128)(2,1)} %get-tuple-element.57) | copy-start | bytes 25165828
  890.7 24.0 %copy-start.9 = (bf16[2,4,4,64,2048]{4,3,2,1,0:T(8,128)(2,1)S(1)}, bf16[2,4,4,64,2048]{4,3,2,1,0:T(8,128)(2,1)}, u32[]{:S(2)}) copy-start(bf16[2,4,4,64,2048]{4,3,2,1,0:T(8,128)(2,1)} %get-tuple-element.58) | copy-start | bytes 25165828
  914.7 114.7 %collective-permute-start.13 = (bf16[2048,2048]{1,0:T(8,128)(2,1)}, bf16[2048,2048]{1,0:T(8,128)(2,1)}, u32[]{:S(2)}, u32[]{:S(2)}) collective-permute-start(bf16[2048,2048]{1,0:T(8,128)(2,1)} %bitcast_convert_fusion), channel_id=1, source_target_pairs={{0,1},{1,0},{2,3},{3,2},{4,5},{5,4},{6,7},{7,6},{8,9},{9,8},{10,11... | collective-permute-start | bytes 25165832 | tf_op jit(solution)/shard_map/ppermute | solution.py:1317
  914.7 21.1 %copy-start.5 = (bf16[4,4,64,512]{3,2,1,0:T(8,128)(2,1)S(1)}, bf16[4,4,64,512]{3,2,1,0:T(8,128)(2,1)}, u32[]{:S(2)}) copy-start(bf16[4,4,64,512]{3,2,1,0:T(8,128)(2,1)} %get-tuple-element.55) | copy-start | bytes 3145732
  935.4 106.6 %collective-permute-start.12 = (bf16[2048,2048]{1,0:T(8,128)(2,1)}, bf16[2048,2048]{1,0:T(8,128)(2,1)}, u32[]{:S(2)}, u32[]{:S(2)}) collective-permute-start(bf16[2048,2048]{1,0:T(8,128)(2,1)} %bitcast_convert_fusion.1), channel_id=1, source_target_pairs={{0,1},{1,0},{2,3},{3,2},{4,5},{5,4},{6,7},{7,6},{8,9},{9,8},{10,11... | collective-permute-start | bytes 25165832 | tf_op jit(solution)/shard_map/ppermute | solution.py:1317
  935.9 5.1 copy-start.10
  935.9 5.1 copy-start.12
  940.7 2.0 copy-start
  940.8 12.3 %collective-permute-start.8 = (bf16[512,1024]{1,0:T(8,128)(2,1)S(1)}, bf16[512,1024]{1,0:T(8,128)(2,1)}, u32[]{:S(2)}, u32[]{:S(2)}) collective-permute-start(bf16[512,1024]{1,0:T(8,128)(2,1)S(1)} %dynamic-slice_convert_fusion), channel_id=1, source_target_pairs={{0,1},{1,0},{2,3},{3,2},{4,5},{5,4},{6,7},{7,6},{8,9},{9,8},{10,11... | collective-permute-start | bytes 3145736 | tf_op jit(solution)/shard_map/ppermute | solution.py:1317
  940.9 2.7 copy-start.11
  943.5 7.0 collective-permute-start.4
  946.0 2.0 copy-start.3
  949.2 7.6 collective-permute-start
  949.5 7.2 copy-start.4
  952.0 8.2 collective-permute-start.5
  955.3 4.9 copy-start.2
  956.3 14.8 %collective-permute-start.9 = (bf16[512,512]{1,0:T(8,128)(2,1)}, bf16[512,512]{1,0:T(8,128)(2,1)S(1)}, u32[]{:S(2)}, u32[]{:S(2)}) collective-permute-start(bf16[512,512]{1,0:T(8,128)(2,1)} %dynamic-slice_convert_fusion.2), channel_id=1, source_target_pairs={{0,2},{1,3},{2,0},{3,1},{4,6},{5,7},{6,4},{7,5},{8,10},{9,11},{10,... | collective-permute-start | bytes 1572872 | tf_op jit(solution)/shard_map/ppermute | solution.py:1317
  959.1 29.9 %collective-permute-start.1 = (bf16[512,512]{1,0:T(8,128)(2,1)}, bf16[512,512]{1,0:T(8,128)(2,1)S(1)}, u32[]{:S(2)}, u32[]{:S(2)}) collective-permute-start(bf16[512,512]{1,0:T(8,128)(2,1)} %dynamic-slice_convert_fusion.4), channel_id=1, source_target_pairs={{0,2},{1,3},{2,0},{3,1},{4,6},{5,7},{6,4},{7,5},{8,10},{9,11},{10,... | collective-permute-start | bytes 1572872 | tf_op jit(solution)/shard_map/ppermute | solution.py:1317
  960.3 27.7 %collective-permute-start.6 = (bf16[512,256]{1,0:T(8,128)(2,1)S(1)}, bf16[512,256]{1,0:T(8,128)(2,1)}, u32[]{:S(2)}, u32[]{:S(2)}) collective-permute-start(bf16[512,256]{1,0:T(8,128)(2,1)S(1)} %add_convert_fusion.2), channel_id=1, source_target_pairs={{0,2},{1,3},{2,0},{3,1},{4,6},{5,7},{6,4},{7,5},{8,10},{9,11},{10,... | collective-permute-start | bytes 786440 | tf_op jit(solution)/shard_map/ppermute | solution.py:1317
  972.5 26.7 %collective-permute-start.10 = (bf16[512,512]{1,0:T(8,128)(2,1)S(1)}, bf16[512,512]{1,0:T(8,128)(2,1)S(1)}, u32[]{:S(2)}, u32[]{:S(2)}) collective-permute-start(bf16[512,512]{1,0:T(8,128)(2,1)S(1)} %add_convert_fusion), channel_id=1, source_target_pairs={{0,2},{1,3},{2,0},{3,1},{4,6},{5,7},{6,4},{7,5},{8,10},{9,11},{10,... | collective-permute-start | bytes 1572872 | tf_op jit(solution)/shard_map/ppermute | solution.py:1317
  989.2 21.2 %collective-permute-start.2 = (bf16[512,512]{1,0:T(8,128)(2,1)S(1)}, bf16[512,512]{1,0:T(8,128)(2,1)S(1)}, u32[]{:S(2)}, u32[]{:S(2)}) collective-permute-start(bf16[512,512]{1,0:T(8,128)(2,1)S(1)} %add_convert_fusion.1), channel_id=1, source_target_pairs={{0,2},{1,3},{2,0},{3,1},{4,6},{5,7},{6,4},{7,5},{8,10},{9,11},{10,... | collective-permute-start | bytes 1572872 | tf_op jit(solution)/shard_map/ppermute | solution.py:1317
  991.1 21.3 %copy-start.7 = (f32[8,2048]{1,0:T(8,128)S(1)}, f32[8,2048]{1,0:T(8,128)}, u32[]{:S(2)}) copy-start(f32[8,2048]{1,0:T(8,128)} %get-tuple-element.51) | copy-start | bytes 196612
  991.1 28.1 %collective-permute-start.7 = (bf16[1024,256]{1,0:T(8,128)(2,1)}, bf16[1024,256]{1,0:T(8,128)(2,1)S(1)}, u32[]{:S(2)}, u32[]{:S(2)}) collective-permute-start(bf16[1024,256]{1,0:T(8,128)(2,1)} %pad_maximum_fusion.2), channel_id=1, source_target_pairs={{0,1},{1,0},{2,3},{3,2},{4,5},{5,4},{6,7},{7,6},{8,9},{9,8},{10,11... | collective-permute-start | bytes 1572872 | tf_op jit(solution)/shard_map/ppermute | solution.py:1317
  1000.4 20.6 %collective-permute-start.11 = (bf16[512,1024]{1,0:T(8,128)(2,1)}, bf16[512,1024]{1,0:T(8,128)(2,1)}, u32[]{:S(2)}, u32[]{:S(2)}) collective-permute-start(bf16[512,1024]{1,0:T(8,128)(2,1)} %pad_maximum_fusion.1), channel_id=1, source_target_pairs={{0,1},{1,0},{2,3},{3,2},{4,5},{5,4},{6,7},{7,6},{8,9},{9,8},{10,11... | collective-permute-start | bytes 3145736 | tf_op jit(solution)/shard_map/ppermute | solution.py:1317
  1011.5 11.2 %collective-permute-start.3 = (bf16[1024,512]{1,0:T(8,128)(2,1)}, bf16[1024,512]{1,0:T(8,128)(2,1)}, u32[]{:S(2)}, u32[]{:S(2)}) collective-permute-start(bf16[1024,512]{1,0:T(8,128)(2,1)} %pad_maximum_fusion), channel_id=1, source_target_pairs={{0,1},{1,0},{2,3},{3,2},{4,5},{5,4},{6,7},{7,6},{8,9},{9,8},{10,11... | collective-permute-start | bytes 3145736 | tf_op jit(solution)/shard_map/ppermute | solution.py:1317
  1041.9 12.6 %copy-start.6 = (bf16[4,64,2048]{2,1,0:T(8,128)(2,1)S(1)}, bf16[4,64,2048]{2,1,0:T(8,128)(2,1)}, u32[]{:S(2)}) copy-start(bf16[4,64,2048]{2,1,0:T(8,128)(2,1)} %get-tuple-element.39) | copy-start | bytes 3145732
  1041.9 13.6 %copy-start.8 = (f32[1,2048]{1,0:T(1,128)S(1)}, f32[1,2048]{1,0:T(1,128)}, u32[]{:S(2)}) copy-start(f32[1,2048]{1,0:T(1,128)} %get-tuple-element.126) | copy-start | bytes 24580
